TPU v7x, 32 devices: a whole 2x2x4 slice. The times are simulated.
32 devices in a mesh: band: 4 (over x, core), grid: 8 (over z, y).
Axes of the slice: x: 2, y: 2, z: 4, core: 2. Of those that a mesh axis runs over, the one named last changes fastest.
Arguments:
- orbitals: float32 [8, 8, 8, 4, 16, 256], P('band', None, 'grid'), may hold values from -6 to 6
- potential: float32 [8, 4, 16, 256], P('grid'), may hold values from -1 to 0.5
- kinetic: float32 [3, 8, 4, 16, 256], P(None, 'grid'), may hold values from 0.5 to 1.5
- occupations: float32 [8, 8], P('band'), may hold values from 0.01 to 0.08
Outputs:
- filtered: float32 [8, 8, 8, 4, 16, 256], P('band', None, 'grid')
- gram: float32 [8, 8, 8], P('band')
- density: float32 [8, 4, 16, 256], P('grid', None, 'band')
All inputs are finite; a program needn't handle non-finite values.
Results may differ from a plain program's by a relative error of at most 0.000052.
Values sent between devices are 32-bit elements; how exact they have to be, the bound alone decides.
No kernel may reach another device: no remote copies, remote signals or barrier semaphores. Data moves between devices by JAX's collectives and lax.ppermute only.
A program may use at most 64 MiB of HBM per device.

v0:
```python
import jax
import jax.numpy as jnp
from jax import lax
from jax.sharding import PartitionSpec as P

DEGREE = 4


CENTRE = 6.0
HALF_WIDTH = 4.0
EPSILON = 1e-06


def shifted(value, axis, steps):
    count = lax.axis_size(axis)
    pairs = [(source, (source + steps) % count) for source in range(count)]
    return lax.ppermute(value, axis, pairs)


def neighbour(piece, offset):
    return shifted(piece, "grid", offset)


def extend(field, width, across):
    lower = neighbour(field[..., -width:, :, :], across)
    upper = neighbour(field[..., :width, :, :], -across)
    widened = jnp.concatenate([lower, field, upper], -3)
    column = lax.axis_index("grid") % across
    left_plain = neighbour(widened[..., :, -width:, :], 1)
    left_wrap = neighbour(widened[..., :, -width:, :], -(across - 1))
    left = jnp.where(column == 0, left_wrap, left_plain)
    right_plain = neighbour(widened[..., :, :width, :], -1)
    right_wrap = neighbour(widened[..., :, :width, :], across - 1)
    right = jnp.where(column == across - 1, right_wrap, right_plain)
    return jnp.concatenate([left, widened, right], -2)


def hamilton(field, coeffs):
    inner = field[..., 1:-1, 1:-1, :]
    kin_x = coeffs[1]
    total = kin_x[1:-1, 1:-1] * (inner - field[..., 2:, 1:-1, :])
    total = total + kin_x[:-2, 1:-1] * (inner - field[..., :-2, 1:-1, :])
    kin_y = coeffs[2]
    total = total + kin_y[1:-1, 1:-1] * (inner - field[..., 1:-1, 2:, :])
    total = total + kin_y[1:-1, :-2] * (inner - field[..., 1:-1, :-2, :])
    kin_z = coeffs[3, 1:-1, 1:-1]
    total = total + kin_z * (inner - jnp.roll(inner, -1, -1))
    total = total + jnp.roll(kin_z, 1, -1) * (inner - jnp.roll(inner, 1, -1))
    return 0.5 * total + coeffs[0, 1:-1, 1:-1] * inner


def body(orbitals, potential, kinetic, occupations):
    margin = 1
    across = min(lax.axis_size("grid"), 8)
    blocks = orbitals.shape[0]
    members = orbitals.shape[1]
    rows_x = orbitals.shape[3]
    rows_y = orbitals.shape[4]
    coeffs = jnp.concatenate([potential, kinetic[:, 0]], 0)
    current = orbitals[:, :, 0]

    def advance(field, coeff_ext, previous, first):
        image = hamilton(field, coeff_ext)
        inner = field[..., 1:-1, 1:-1, :]
        if first:
            return (image - CENTRE * inner) / HALF_WIDTH
        return 2.0 / HALF_WIDTH * (image - CENTRE * inner) - previous

    previous = current
    coeff_ext = None
    for degree_step in range(DEGREE):
        if degree_step == 0:
            stacked = jnp.concatenate(
                [coeffs, current.reshape((blocks * members,) + current.shape[2:])], 0
            )
            wide = extend(stacked, margin, across)
            coeff_ext = wide[:4]
            extended = wide[4:].reshape((blocks, members) + wide.shape[1:])
        else:
            extended = extend(current, 1, across)
        fresh = advance(extended, coeff_ext, previous, degree_step == 0)
        previous = current
        current = fresh
    cells = rows_x * rows_y * orbitals.shape[5] * lax.axis_size("grid")
    flat = current.reshape(blocks, members, -1)
    local_gram = jnp.einsum("kbx,kcx->kbc", flat, flat, precision=lax.Precision.HIGHEST) / cells
    gram = lax.psum(local_gram, "grid")
    diagonal = jnp.diagonal(gram, axis1=1, axis2=2)
    weight = occupations / (diagonal + EPSILON)
    partial_value = jnp.einsum(
        "kb,kbxyz->xyz", weight, current * current, precision=lax.Precision.HIGHEST
    )
    density = lax.psum_scatter(partial_value[None], "band", scatter_dimension=2, tiled=True)
    return (current[:, :, None], gram, density)


def solution(mesh):
    placed = (
        P("band", None, "grid", None, None, None),
        P("grid", None, None, None),
        P(None, "grid", None, None, None),
        P("band", None),
    )
    return jax.shard_map(
        body,
        mesh=mesh,
        in_specs=placed,
        out_specs=(
            P("band", None, "grid", None, None, None),
            P("band", None, None),
            P("grid", None, "band", None),
        ),
        check_vma=False,
    )
```

profile of v0, /device:TPU:0, one launch (start us, length us, event | category | flops | bytes accessed | tf_op | source)
XLA Modules:
  0.0 119.2 jit_solution(18390265595370374221)
XLA Ops:
  7.2 0.0 copy-start.3
  7.2 0.0 copy-start.1
  7.2 0.0 all-reduce.3.cloned.1.call-start
  7.3 1.2 pad_maximum_fusion.27
  8.4 0.0 collective-permute-start
  8.5 0.0 collective-permute-start.1
  8.5 0.8 slice_bitcast_fusion
  9.3 1.5 %broadcast_multiply_fusion.1 = f32[4,16,256]{2,1,0:T(8,128)} fusion(f32[1,4,16,256]{3,2,1,0:T(8,128)} %param.5), kind=kLoop, calls=%fused_computation.138 | loop fusion | flops 16384 | bytes 131072 | tf_op jit(solution)/shard_map/mul | solution.py:49
  10.8 1.1 pad_maximum_fusion.32
  12.0 3.0 %collective-permute-start.2 = (f32[20,6,1,256]{3,2,1,0:T(1,128)S(1)}, f32[20,6,1,256]{3,2,1,0:T(1,128)S(1)}, u32[]{:S(2)}, u32[]{:S(2)}) collective-permute-start(f32[20,6,1,256]{3,2,1,0:T(1,128)S(1)} %get-tuple-element.13), channel_id=1, source_target_pairs={{0,1},{1,2},{2,3},{3,4},{4,5},{5,6},{6,7},{7,0},{8,9},{9,10},{10,1... | collective-permute-start | bytes 368648 | tf_op jit(solution)/shard_map/ppermute | solution.py:17
  15.0 3.1 %collective-permute-start.3 = (f32[20,6,1,256]{3,2,1,0:T(1,128)S(1)}, f32[20,6,1,256]{3,2,1,0:T(1,128)S(1)}, u32[]{:S(2)}, u32[]{:S(2)}) collective-permute-start(f32[20,6,1,256]{3,2,1,0:T(1,128)S(1)} %get-tuple-element.14), channel_id=1, source_target_pairs={{0,7},{1,0},{2,1},{3,2},{4,3},{5,4},{6,5},{7,6},{8,15},{9,8},{10,9... | collective-permute-start | bytes 368648 | tf_op jit(solution)/shard_map/ppermute | solution.py:17
  18.1 0.1 slice.323
  18.2 0.1 copy.10
  18.3 0.1 pad_maximum_fusion.42
  18.4 3.1 %collective-permute-done.2 = f32[20,6,1,256]{3,2,1,0:T(1,128)S(1)} collective-permute-done((f32[20,6,1,256]{3,2,1,0:T(1,128)S(1)}, f32[20,6,1,256]{3,2,1,0:T(1,128)S(1)}, u32[]{:S(2)}, u32[]{:S(2)}) %collective-permute-start.2) | collective-permute-done | bytes 122912 | tf_op jit(solution)/shard_map/ppermute | solution.py:17
  21.5 1.1 collective-permute-done.3
  22.5 0.5 pad_maximum_fusion
  23.0 0.2 slice.312
  23.2 0.4 fusion.80
  23.6 0.2 fusion.81
  24.0 1.3 %broadcast_multiply_fusion = (f32[2,8,4,16,256]{4,3,2,1,0:T(8,128)S(1)}, f32[2,8,4,16,256]{4,3,2,1,0:T(8,128)S(1)}) fusion(f32[4,16,256]{2,1,0:T(8,128)S(1)} %bitcast.43, f32[2,8,4,16,255]{4,3,2,1,0:T(8,128)S(1)} %get-tuple-element.8, f32[2,8,4,16,1]{4,3,2,1,0:T(8,128)S(1)} %get-tuple-element.10, f32[4,16,256]{2,1,0:T(8,128)S(1)} %pad_maximum_fusion.42, ...), kind=kLoop, calls=%fused_computation.115 | loop fusion | flops 6553600 | bytes 9895936 | tf_op jit(solution)/shard_map/div | solution.py:66
  25.3 0.0 collective-permute-start.4
  25.3 0.0 collective-permute-start.5
  25.3 0.4 fusion.89
  25.8 0.1 pad_maximum_fusion.41
  25.9 3.4 %collective-permute-start.6 = (f32[2,8,6,1,256]{4,3,2,1,0:T(1,128)S(1)}, f32[2,8,6,1,256]{4,3,2,1,0:T(1,128)S(1)}, u32[]{:S(2)}, u32[]{:S(2)}) collective-permute-start(f32[2,8,6,1,256]{4,3,2,1,0:T(1,128)S(1)} %get-tuple-element.19), channel_id=1, source_target_pairs={{0,7},{1,0},{2,1},{3,2},{4,3},{5,4},{6,5},{7,6},{8,15},{9,8},{10,9... | collective-permute-start | bytes 294920 | tf_op jit(solution)/shard_map/ppermute | solution.py:17
  29.3 0.2 fusion.88
  29.5 2.0 %collective-permute-done.6 = f32[2,8,6,1,256]{4,3,2,1,0:T(1,128)S(1)} collective-permute-done((f32[2,8,6,1,256]{4,3,2,1,0:T(1,128)S(1)}, f32[2,8,6,1,256]{4,3,2,1,0:T(1,128)S(1)}, u32[]{:S(2)}, u32[]{:S(2)}) %collective-permute-start.6) | collective-permute-done | bytes 98336 | tf_op jit(solution)/shard_map/ppermute | solution.py:17
  31.5 5.1 %collective-permute-done.7 = f32[2,8,6,1,256]{4,3,2,1,0:T(1,128)S(1)} collective-permute-done((f32[2,8,6,1,256]{4,3,2,1,0:T(1,128)S(1)}, f32[2,8,6,1,256]{4,3,2,1,0:T(1,128)S(1)}, u32[]{:S(2)}, u32[]{:S(2)}) %collective-permute-start.7) | collective-permute-done | bytes 98336 | tf_op jit(solution)/shard_map/ppermute | solution.py:17
  36.6 1.6 %fusion.45 = f32[2,8,4,16,256]{4,3,2,1,0:T(8,128)S(1)} fusion(f32[2,8,4,16,256]{4,3,2,1,0:T(8,128)S(1)} %get-tuple-element.5, f32[2,8,6,1,256]{4,3,2,1,0:T(1,128)S(1)} %collective-permute-done.7, f32[2,8,1,16,256]{4,3,2,1,0:T(8,128)S(1)} %collective-permute-done.4, f32[2,8,1,16,256]{4,3,2,1,0:T(8,128)S(1)} %collective-permute-done.5, ...), kind=kLoop, calls=%fused_computation.65 | loop fusion | flops 8912896 | bytes 7471104 | tf_op jit(solution)/shard_map/sub | solution.py:67
  38.3 0.0 collective-permute-start.8
  38.3 0.0 collective-permute-start.9
  38.3 0.4 fusion.86
  38.7 0.1 pad_maximum_fusion.38
  38.9 0.6 collective-permute-start.10
  39.4 1.5 %collective-permute-start.11 = (f32[2,8,6,1,256]{4,3,2,1,0:T(1,128)S(1)}, f32[2,8,6,1,256]{4,3,2,1,0:T(1,128)S(1)}, u32[]{:S(2)}, u32[]{:S(2)}) collective-permute-start(f32[2,8,6,1,256]{4,3,2,1,0:T(1,128)S(1)} %get-tuple-element.18), channel_id=1, source_target_pairs={{0,1},{1,2},{2,3},{3,4},{4,5},{5,6},{6,7},{7,0},{8,9},{9,10},{10,1... | collective-permute-start | bytes 294920 | tf_op jit(solution)/shard_map/ppermute | solution.py:17
  41.0 0.2 fusion.85
  41.2 3.4 %collective-permute-done.10 = f32[2,8,6,1,256]{4,3,2,1,0:T(1,128)S(1)} collective-permute-done((f32[2,8,6,1,256]{4,3,2,1,0:T(1,128)S(1)}, f32[2,8,6,1,256]{4,3,2,1,0:T(1,128)S(1)}, u32[]{:S(2)}, u32[]{:S(2)}) %collective-permute-start.10) | collective-permute-done | bytes 98336 | tf_op jit(solution)/shard_map/ppermute | solution.py:17
  44.6 2.1 %collective-permute-done.11 = f32[2,8,6,1,256]{4,3,2,1,0:T(1,128)S(1)} collective-permute-done((f32[2,8,6,1,256]{4,3,2,1,0:T(1,128)S(1)}, f32[2,8,6,1,256]{4,3,2,1,0:T(1,128)S(1)}, u32[]{:S(2)}, u32[]{:S(2)}) %collective-permute-start.11) | collective-permute-done | bytes 98336 | tf_op jit(solution)/shard_map/ppermute | solution.py:17
  46.8 1.6 %fusion.27 = f32[2,8,4,16,256]{4,3,2,1,0:T(8,128)S(1)} fusion(f32[2,8,4,16,256]{4,3,2,1,0:T(8,128)S(1)} %fusion.45, f32[2,8,6,1,256]{4,3,2,1,0:T(1,128)S(1)} %collective-permute-done.11, f32[2,8,1,16,256]{4,3,2,1,0:T(8,128)S(1)} %collective-permute-done.8, f32[2,8,1,16,256]{4,3,2,1,0:T(8,128)S(1)} %collective-permute-done.9, ...), kind=kLoop, calls=%fused_computation.39 | loop fusion | flops 9175040 | bytes 6422528 | tf_op jit(solution)/shard_map/sub | solution.py:67
  48.4 0.0 collective-permute-start.12
  48.5 0.0 collective-permute-start.13
  48.5 0.4 fusion.83
  48.9 0.1 pad_maximum_fusion.35
  49.0 0.1 collective-permute-start.14
  49.1 2.0 %collective-permute-start.15 = (f32[2,8,6,1,256]{4,3,2,1,0:T(1,128)S(1)}, f32[2,8,6,1,256]{4,3,2,1,0:T(1,128)S(1)}, u32[]{:S(2)}, u32[]{:S(2)}) collective-permute-start(f32[2,8,6,1,256]{4,3,2,1,0:T(1,128)S(1)} %get-tuple-element.16), channel_id=1, source_target_pairs={{0,1},{1,2},{2,3},{3,4},{4,5},{5,6},{6,7},{7,0},{8,9},{9,10},{10,1... | collective-permute-start | bytes 294920 | tf_op jit(solution)/shard_map/ppermute | solution.py:17
  51.1 0.2 fusion.84
  51.3 2.4 %collective-permute-done.14 = f32[2,8,6,1,256]{4,3,2,1,0:T(1,128)S(1)} collective-permute-done((f32[2,8,6,1,256]{4,3,2,1,0:T(1,128)S(1)}, f32[2,8,6,1,256]{4,3,2,1,0:T(1,128)S(1)}, u32[]{:S(2)}, u32[]{:S(2)}) %collective-permute-start.14) | collective-permute-done | bytes 98336 | tf_op jit(solution)/shard_map/ppermute | solution.py:17
  53.7 2.8 %collective-permute-done.15 = f32[2,8,6,1,256]{4,3,2,1,0:T(1,128)S(1)} collective-permute-done((f32[2,8,6,1,256]{4,3,2,1,0:T(1,128)S(1)}, f32[2,8,6,1,256]{4,3,2,1,0:T(1,128)S(1)}, u32[]{:S(2)}, u32[]{:S(2)}) %collective-permute-start.15) | collective-permute-done | bytes 98336 | tf_op jit(solution)/shard_map/ppermute | solution.py:17
  56.5 1.6 %fusion.77 = (f32[2,8,4,16,256]{4,3,2,1,0:T(8,128)S(1)}, f32[2,8,4,16,256]{4,3,2,1,0:T(8,128)S(1)}) fusion(f32[2,8,4,16,256]{4,3,2,1,0:T(8,128)S(1)} %fusion.45, f32[2,8,4,16,256]{4,3,2,1,0:T(8,128)S(1)} %fusion.27, f32[4,16,256]{2,1,0:T(8,128)S(1)} %bitcast.45, f32[2,8,4,16,255]{4,3,2,1,0:T(8,128)S(1)} %get-tuple-element.26, ...), kind=kLoop, calls=%fused_computation.143 | loop fusion | flops 9175040 | bytes 7471104 | tf_op jit(solution)/shard_map/mul | solution.py:91
  58.1 0.0 copy-start.7
  58.1 0.2 reshape.23
  58.3 2.2 %convolution_multiply_fusion = f32[2,8,8]{2,1,0:T(8,128)S(1)} fusion(f32[2,8,16384]{2,1,0:T(8,128)S(1)} %reshape.23), kind=kOutput, calls=%fused_computation.2 | convolution fusion | flops 25165952 | bytes 1049088 | tf_op jit(solution)/shard_map/kbx,kcx->kbc/dot_general | solution.py:86
  60.5 17.4 %psum.7 = f32[2,8,8]{2,1,0:T(8,128)S(1)} all-reduce(f32[2,8,8]{2,1,0:T(8,128)S(1)} %convolution_multiply_fusion), channel_id=1, replica_groups=mesh['band'=4,'grid'=8] {'grid'}, use_global_device_ids=true, to_apply=%region_0.1 | all-reduce | flops 128 | bytes 1024 | tf_op jit(solution)/shard_map/psum | solution.py:87
  77.9 0.0 copy-start.5
  77.9 0.1 copy.9
  78.1 0.6 gather_fusion
  78.6 0.1 copy.11
  78.7 1.3 %fusion.74 = f32[1,4,16,256,1]{3,0,4,2,1:T(1,128)S(1)} fusion(f32[2,8,1,1,1]{1,2,0,4,3:T(1,128)S(1)} %copy.11, f32[2,8,4,16,256]{4,3,2,1,0:T(8,128)S(1)} %get-tuple-element.3), kind=kOutput, calls=%fused_computation.113 | convolution fusion | flops 3145728 | bytes 1114176 | tf_op jit(solution)/shard_map/kb,kbxyz->xyz/dot_general | solution.py:90
  80.0 0.6 copy.19
  80.6 0.0 all-reduce.3.cloned.1.call-update
  80.6 0.6 dynamic-slice
  81.9 29.1 %all-reduce.3.cloned.1.call-done = f32[1,4,16,256]{3,2,1,0:T(8,128)} async-done(((f32[1,4,16,256]{3,2,1,0:T(8,128)}), f32[1,4,16,256]{3,2,1,0:T(8,128)}) %all-reduce.3.cloned.1.call-update) | async-done | bytes 65552
  111.0 1.4 %constant_dynamic-slice_fusion = f32[1,4,4,256]{3,2,1,0:T(4,128)} fusion(f32[1,4,16,256]{3,2,1,0:T(8,128)} %all-reduce.3.cloned.1.call-done, u32[]{:T(128)S(6)} %multiply.7), kind=kLoop, calls=%fused_computation.141 | loop fusion | bytes 32772
  (28 shorter events, 0.2 us)
Async XLA Ops:
  7.2 15.4 %copy-start.3 = (f32[3,1,4,16,256]{4,3,2,1,0:T(8,128)S(1)}, f32[3,1,4,16,256]{4,3,2,1,0:T(8,128)}, u32[]{:S(2)}) copy-start(f32[3,1,4,16,256]{4,3,2,1,0:T(8,128)} %param.6) | copy-start | bytes 589828
  7.2 3.7 %copy-start = (f32[2,8,1,4,16,256]{5,4,3,2,1,0:T(8,128)S(1)}, f32[2,8,1,4,16,256]{5,4,3,2,1,0:T(8,128)}, u32[]{:S(2)}) copy-start(f32[2,8,1,4,16,256]{5,4,3,2,1,0:T(8,128)} %param.4) | copy-start | bytes 3145732
  7.2 15.3 %copy-start.1 = (f32[1,4,16,256]{3,2,1,0:T(8,128)S(1)}, f32[1,4,16,256]{3,2,1,0:T(8,128)}, u32[]{:S(2)}) copy-start(f32[1,4,16,256]{3,2,1,0:T(8,128)} %param.5) | copy-start | bytes 196612
  7.2 11.0 %copy-start.6 = (f32[2,8]{1,0:T(2,128)S(1)}, f32[2,8]{1,0:T(2,128)}, u32[]{:S(2)}) copy-start(f32[2,8]{1,0:T(2,128)} %param.7) | copy-start | bytes 196
  7.2 103.8 %all-reduce.3.cloned.1.call-start = ((), (), s32[]{:S(2)}) async-start(), calls=%async_computation | async-start | bytes 131072
  8.4 2.4 %collective-permute-start = (f32[20,1,16,256]{3,2,1,0:T(8,128)S(1)}, f32[20,1,16,256]{3,2,1,0:T(8,128)S(1)}, u32[]{:S(2)}, u32[]{:S(2)}) collective-permute-start(f32[20,1,16,256]{3,2,1,0:T(8,128)S(1)} %get-tuple-element.21), channel_id=1, source_target_pairs={{0,0},{1,1},{2,2},{3,3},{4,4},{5,5},{6,6},{7,7},{8,8},{9,9},{10,10... | collective-permute-start | bytes 983048 | tf_op jit(solution)/shard_map/ppermute | solution.py:17
  8.5 2.4 %collective-permute-start.1 = (f32[20,1,16,256]{3,2,1,0:T(8,128)S(1)}, f32[20,1,16,256]{3,2,1,0:T(8,128)S(1)}, u32[]{:S(2)}, u32[]{:S(2)}) collective-permute-start(f32[20,1,16,256]{3,2,1,0:T(8,128)S(1)} %get-tuple-element.22), channel_id=1, source_target_pairs={{0,0},{1,1},{2,2},{3,3},{4,4},{5,5},{6,6},{7,7},{8,8},{9,9},{10,10... | collective-permute-start | bytes 983048 | tf_op jit(solution)/shard_map/ppermute | solution.py:17
  12.0 9.5 %collective-permute-start.2 = (f32[20,6,1,256]{3,2,1,0:T(1,128)S(1)}, f32[20,6,1,256]{3,2,1,0:T(1,128)S(1)}, u32[]{:S(2)}, u32[]{:S(2)}) collective-permute-start(f32[20,6,1,256]{3,2,1,0:T(1,128)S(1)} %get-tuple-element.13), channel_id=1, source_target_pairs={{0,1},{1,2},{2,3},{3,4},{4,5},{5,6},{6,7},{7,0},{8,9},{9,10},{10,1... | collective-permute-start | bytes 368648 | tf_op jit(solution)/shard_map/ppermute | solution.py:17
  15.0 7.5 %collective-permute-start.3 = (f32[20,6,1,256]{3,2,1,0:T(1,128)S(1)}, f32[20,6,1,256]{3,2,1,0:T(1,128)S(1)}, u32[]{:S(2)}, u32[]{:S(2)}) collective-permute-start(f32[20,6,1,256]{3,2,1,0:T(1,128)S(1)} %get-tuple-element.14), channel_id=1, source_target_pairs={{0,7},{1,0},{2,1},{3,2},{4,3},{5,4},{6,5},{7,6},{8,15},{9,8},{10,9... | collective-permute-start | bytes 368648 | tf_op jit(solution)/shard_map/ppermute | solution.py:17
  25.3 0.5 collective-permute-start.4
  25.3 0.4 collective-permute-start.5
  25.7 10.9 %copy-start.4 = (f32[4,16,256]{2,1,0:T(8,128)S(1)}, f32[4,16,256]{2,1,0:T(8,128)}, u32[]{:S(2)}) copy-start(f32[4,16,256]{2,1,0:T(8,128)} %broadcast_multiply_fusion.1) | copy-start | bytes 196612
  25.9 5.6 %collective-permute-start.6 = (f32[2,8,6,1,256]{4,3,2,1,0:T(1,128)S(1)}, f32[2,8,6,1,256]{4,3,2,1,0:T(1,128)S(1)}, u32[]{:S(2)}, u32[]{:S(2)}) collective-permute-start(f32[2,8,6,1,256]{4,3,2,1,0:T(1,128)S(1)} %get-tuple-element.19), channel_id=1, source_target_pairs={{0,7},{1,0},{2,1},{3,2},{4,3},{5,4},{6,5},{7,6},{8,15},{9,8},{10,9... | collective-permute-start | bytes 294920 | tf_op jit(solution)/shard_map/ppermute | solution.py:17
  29.3 7.3 %collective-permute-start.7 = (f32[2,8,6,1,256]{4,3,2,1,0:T(1,128)S(1)}, f32[2,8,6,1,256]{4,3,2,1,0:T(1,128)S(1)}, u32[]{:S(2)}, u32[]{:S(2)}) collective-permute-start(f32[2,8,6,1,256]{4,3,2,1,0:T(1,128)S(1)} %get-tuple-element.20), channel_id=1, source_target_pairs={{0,1},{1,2},{2,3},{3,4},{4,5},{5,6},{6,7},{7,0},{8,9},{9,10},{10,1... | collective-permute-start | bytes 294920 | tf_op jit(solution)/shard_map/ppermute | solution.py:17
  38.3 0.4 collective-permute-start.8
  38.3 0.4 collective-permute-start.9
  38.9 5.7 %collective-permute-start.10 = (f32[2,8,6,1,256]{4,3,2,1,0:T(1,128)S(1)}, f32[2,8,6,1,256]{4,3,2,1,0:T(1,128)S(1)}, u32[]{:S(2)}, u32[]{:S(2)}) collective-permute-start(f32[2,8,6,1,256]{4,3,2,1,0:T(1,128)S(1)} %get-tuple-element.17), channel_id=1, source_target_pairs={{0,7},{1,0},{2,1},{3,2},{4,3},{5,4},{6,5},{7,6},{8,15},{9,8},{10,9... | collective-permute-start | bytes 294920 | tf_op jit(solution)/shard_map/ppermute | solution.py:17
  39.4 7.3 %collective-permute-start.11 = (f32[2,8,6,1,256]{4,3,2,1,0:T(1,128)S(1)}, f32[2,8,6,1,256]{4,3,2,1,0:T(1,128)S(1)}, u32[]{:S(2)}, u32[]{:S(2)}) collective-permute-start(f32[2,8,6,1,256]{4,3,2,1,0:T(1,128)S(1)} %get-tuple-element.18), channel_id=1, source_target_pairs={{0,1},{1,2},{2,3},{3,4},{4,5},{5,6},{6,7},{7,0},{8,9},{9,10},{10,1... | collective-permute-start | bytes 294920 | tf_op jit(solution)/shard_map/ppermute | solution.py:17
  48.4 0.4 collective-permute-start.12
  48.5 0.4 collective-permute-start.13
  49.0 4.7 %collective-permute-start.14 = (f32[2,8,6,1,256]{4,3,2,1,0:T(1,128)S(1)}, f32[2,8,6,1,256]{4,3,2,1,0:T(1,128)S(1)}, u32[]{:S(2)}, u32[]{:S(2)}) collective-permute-start(f32[2,8,6,1,256]{4,3,2,1,0:T(1,128)S(1)} %get-tuple-element.15), channel_id=1, source_target_pairs={{0,7},{1,0},{2,1},{3,2},{4,3},{5,4},{6,5},{7,6},{8,15},{9,8},{10,9... | collective-permute-start | bytes 294920 | tf_op jit(solution)/shard_map/ppermute | solution.py:17
  49.1 7.4 %collective-permute-start.15 = (f32[2,8,6,1,256]{4,3,2,1,0:T(1,128)S(1)}, f32[2,8,6,1,256]{4,3,2,1,0:T(1,128)S(1)}, u32[]{:S(2)}, u32[]{:S(2)}) collective-permute-start(f32[2,8,6,1,256]{4,3,2,1,0:T(1,128)S(1)} %get-tuple-element.16), channel_id=1, source_target_pairs={{0,1},{1,2},{2,3},{3,4},{4,5},{5,6},{6,7},{7,0},{8,9},{9,10},{10,1... | collective-permute-start | bytes 294920 | tf_op jit(solution)/shard_map/ppermute | solution.py:17
  58.1 54.3 %copy-start.2 = (f32[2,8,4,16,256]{4,3,2,1,0:T(8,128)}, f32[2,8,4,16,256]{4,3,2,1,0:T(8,128)S(1)}, u32[]{:S(2)}) copy-start(f32[2,8,4,16,256]{4,3,2,1,0:T(8,128)S(1)} %get-tuple-element.4) | copy-start | bytes 3145732
  58.1 22.5 %copy-start.7 = (u32[32]{0:T(128)S(1)}, u32[32]{0:T(128)}, u32[]{:S(2)}) copy-start(u32[32]{0:T(128)} %constant.55) | copy-start | bytes 388
  77.9 34.5 %copy-start.5 = (f32[2,8,8]{2,1,0:T(8,128)}, f32[2,8,8]{2,1,0:T(8,128)S(1)}, u32[]{:S(2)}) copy-start(f32[2,8,8]{2,1,0:T(8,128)S(1)} %psum.7) | copy-start | bytes 1540
Sparse Core Ops, SparseCore 0:
  80.8 30.2 all-reduce.2
where the time goes:
time: 120 us; the launch traced here: 119 us
  waiting for transfers between devices  51.1 us (43%)
  blocking collectives  17.4 us (14%)
  between operations  15.1 us (13%)
  starting transfers between devices  13.9 us (12%)
  other arithmetic  11 us (9%)
  local copies, waits for them, and re-layouts  7.27 us (6%)
  matrix products  3.48 us (3%)
    unnamed x2, waiting for transfers between devices  29.1 us
    ppermute x16, waiting for transfers between devices, shifted(): return lax.ppermute(value, axis, pairs)  22 us
    psum x1, blocking collectives, body(): gram = lax.psum(local_gram, 'grid')  17.4 us
    ppermute x16, starting transfers between devices, shifted(): return lax.ppermute(value, axis, pairs)  13.9 us
    sub x2, other arithmetic, advance(): return 2.0 / HALF_WIDTH * (image - CENTRE * inner) - previous  3.24 us
  transfers between devices with their start and end apart: 17, of which 9 were waited for; matrix products, arithmetic and copies ran while one was open for 4% of the time, Pallas kernels for 0%

commit v1 on v0

v1 whole, which is shorter than its diff:
```python
import functools

import jax
import jax.numpy as jnp
from jax import lax
from jax.experimental import pallas as pl
from jax.experimental.pallas import tpu as pltpu
from jax.sharding import PartitionSpec as P

DEGREE = 4

CENTRE = 6.0
HALF_WIDTH = 4.0
EPSILON = 1e-06
SUB = 8
LANES = 128


def shifted(value, axis, steps):
    count = lax.axis_size(axis)
    pairs = [(source, (source + steps) % count) for source in range(count)]
    return lax.ppermute(value, axis, pairs)


def swapped(value, axis, bit):
    count = lax.axis_size(axis)
    return lax.ppermute(value, axis, [(i, i ^ bit) for i in range(count)])


def cut(h):
    return slice(LANES * h, LANES * (h + 1))


def iotas():
    return tuple(lax.broadcasted_iota(jnp.int32, (SUB, LANES), axis) for axis in range(2))


def ahead(line, lane):
    turned = [pltpu.roll(block, LANES - 1, 1) for block in line]
    return [jnp.where(lane == LANES - 1, turned[(h + 1) % len(line)], turned[h]) for h in range(len(line))]


def behind(line, lane):
    turned = [pltpu.roll(block, 1, 1) for block in line]
    return [jnp.where(lane == 0, turned[h - 1], turned[h]) for h in range(len(line))]


def pack_kernel(steps, odd_ref, pot_any, kin_any, orb_any, *refs):
    arrivals = refs[-1]
    pot_ref, kin_ref, orb_ref = refs[-4:-1]
    out_refs = refs[:-4]
    count, rows_x, rows_y, depth = orb_ref.shape
    odd = odd_ref[0] == 1
    row, _ = iotas()
    upper = row < DEGREE
    loads = [
        pltpu.make_async_copy(pot_any, pot_ref, arrivals.at[0]),
        pltpu.make_async_copy(kin_any, kin_ref, arrivals.at[1]),
    ]
    size = count // steps
    for k in range(steps):
        part = pl.ds(k * size, size)
        loads.append(pltpu.make_async_copy(orb_any.at[part], orb_ref.at[part], arrivals.at[2 + k]))
    for load in loads:
        load.start()
    fields = [pot_ref] + [kin_ref.at[c] for c in range(3)] + [orb_ref.at[m] for m in range(count)]
    place = 0
    for index in range(0, len(out_refs), 2):
        a_ref, b_ref = out_refs[index : index + 2]
        if index == 0:
            loads[0].wait()
            loads[1].wait()
        loads[2 + index // 2].wait()
        for p in range(a_ref.shape[0]):
            one, two = fields[place], fields[place + 1]
            place += 2
            for x in range(rows_x):
                for h in range(depth // LANES):
                    first = jnp.where(upper, one[x, 0:SUB, cut(h)], pltpu.roll(two[x, 0:SUB, cut(h)], DEGREE, 0))
                    tail = slice(rows_y - SUB, rows_y)
                    last = jnp.where(upper, pltpu.roll(one[x, tail, cut(h)], DEGREE, 0), two[x, tail, cut(h)])
                    a_ref[p, x, :, cut(h)] = jnp.where(odd, first, last)
                    b_ref[p, x, :, cut(h)] = jnp.where(odd, last, first)


def ring_tiles(ref, index, parts):
    return [
        [ref[index + (h, pl.ds(t, SUB, stride=parts), slice(None))] for h in range(ref.shape[-3])]
        for t in range(parts)
    ]


def own_coefficients(pot_ref, kin_ref, coef_ref, ring, lane):
    rows_x, rows_y, depth = pot_ref.shape
    parts = rows_y // SUB
    unit = 1.0 / HALF_WIDTH
    for x in range(rows_x):
        for c in range(4):
            own_ref = pot_ref if c == 0 else kin_ref.at[c - 1]
            for h in range(depth // LANES):
                ring[c, x, h] = own_ref[x, :, cut(h)]
    for x in range(rows_x):
        before = (x - 1) % rows_x
        pot = ring_tiles(ring, (0, x), parts)
        kx = ring_tiles(ring, (1, x), parts)
        kxm = ring_tiles(ring, (1, before), parts)
        ky = ring_tiles(ring, (2, x), parts)
        kz = ring_tiles(ring, (3, x), parts)
        for t in range(parts):
            kzm = behind(kz[t], lane)
            for h in range(depth // LANES):
                kym = ky[t - 1][h] if t > 0 else pltpu.roll(ky[parts - 1][h], 1, 0)
                total = kx[t][h] + kxm[t][h] + ky[t][h] + kym + kz[t][h] + kzm[h]
                coef_ref[0, x, t, h] = unit * total + (2.0 * unit) * (pot[t][h] - CENTRE)
                coef_ref[1, x, t, h] = unit * kx[t][h]
                coef_ref[2, x, t, h] = unit * ky[t][h]
                coef_ref[3, x, t, h] = unit * kz[t][h]
                coef_ref[4, x, t, h] = unit * kzm[h]
                if t == 0:
                    coef_ref[5, x, 0, h] = unit * kym


def apply_own(coef_ref, v, x, t, lane):
    rows_x, parts = len(v), len(v[0])
    up_x, down_x = (x + 1) % rows_x, (x - 1) % rows_x
    own = v[x][t]
    front, back = ahead(own, lane), behind(own, lane)
    result = []
    for h in range(len(own)):
        total = coef_ref[0, x, t, h] * own[h]
        total = total - coef_ref[1, x, t, h] * v[up_x][t][h]
        total = total - coef_ref[1, down_x, t, h] * v[down_x][t][h]
        above = v[x][t + 1][h] if t < parts - 1 else pltpu.roll(v[x][0][h], SUB - 1, 0)
        total = total - coef_ref[2, x, t, h] * above
        if t > 0:
            total = total - coef_ref[2, x, t - 1, h] * v[x][t - 1][h]
        else:
            total = total - coef_ref[5, x, 0, h] * pltpu.roll(v[x][parts - 1][h], 1, 0)
        total = total - coef_ref[3, x, t, h] * front[h]
        result.append(total - coef_ref[4, x, t, h] * back[h])
    return result


def pairs_of(members):
    return [(a, b) for a in range(members) for b in range(a, members)]


def interior_kernel(members, pot_ref, kin_ref, orb_ref, body_ref, seam_ref, sums_ref, coef_ref, coef_ring, ring):
    count, rows_x, rows_y, depth = orb_ref.shape
    parts = rows_y // SUB
    blocks_z = depth // LANES
    row, lane = iotas()
    upper = row < DEGREE
    own_coefficients(pot_ref, kin_ref, coef_ref, coef_ring, lane)

    def one(pair, half):
        m = 2 * pair + half
        for x in range(rows_x):
            for h in range(blocks_z):
                ring[half, x, h] = orb_ref[m, x, :, cut(h)]
        v = [ring_tiles(ring.at[half], (x,), parts) for x in range(rows_x)]
        previous = None
        for step in range(DEGREE):
            for x in range(rows_x):
                for h in range(blocks_z):
                    for side in range(2):
                        for depth_in in range(2):
                            y = step + depth_in if side == 0 else rows_y - 1 - step - depth_in
                            place = DEGREE * half + (DEGREE - 1 if side == 0 else 0)
                            value = v[x][y % parts][h][y // parts : y // parts + 1]
                            seam_ref[pair, side, step, depth_in, x, h, place : place + 1, :] = value
            fresh = []
            for x in range(rows_x):
                rows = []
                for t in range(parts):
                    image = apply_own(coef_ref, v, x, t, lane)
                    if step == 0:
                        rows.append([0.5 * i for i in image])
                    else:
                        rows.append([i - p for i, p in zip(image, previous[x][t])])
                fresh.append(rows)
            previous, v = v, fresh
        for x in range(rows_x):
            for t in range(parts):
                for h in range(blocks_z):
                    ring[half, x, h, pl.ds(t, SUB, stride=parts), :] = v[x][t][h]
        for x in range(rows_x):
            for h in range(blocks_z):
                body_ref[m, x, h] = jnp.where(upper, ring[half, x, h, rows_y - SUB :], ring[half, x, h, 0:SUB])

    def both(pair, carry):
        one(pair, 0)
        one(pair, 1)
        return carry

    lax.fori_loop(0, count // 2, both, 0)

    pairs = pairs_of(members)
    for k in range(count // members):

        def gather(x, sums, k=k):
            sums = list(sums)
            for h in range(blocks_z):
                f = [body_ref[k * members + a, x, h] for a in range(members)]
                for i, (a, b) in enumerate(pairs):
                    sums[i] = sums[i] + f[a] * f[b]
            return tuple(sums)

        sums = lax.fori_loop(0, rows_x, gather, tuple(jnp.zeros((SUB, LANES), jnp.float32) for _ in pairs))
        for i, value in enumerate(sums):
            sums_ref[k, i] = value


def windows_kernel(odd_ref, pot_ref, kin_ref, ha_ref, hb_ref, coef_ref):
    rows_x, rows_y, depth = pot_ref.shape
    odd = odd_ref[0] == 1
    row, lane = iotas()
    upper = row < DEGREE
    blocks_z = depth // LANES
    unit = 1.0 / HALF_WIDTH

    def window(tile, start):
        low = pltpu.roll(tile, (SUB - start) % SUB, 0) if start % SUB else tile
        high = pltpu.roll(tile, (SUB + DEGREE - start) % SUB, 0) if (DEGREE - start) % SUB else tile
        return jnp.where(upper, low, high)

    def field(c, x, h):
        own_ref = pot_ref if c == 0 else kin_ref.at[c - 1]
        a, b = ha_ref[c // 2, x, :, cut(h)], hb_ref[c // 2, x, :, cut(h)]
        before, after = jnp.where(odd, a, b), jnp.where(odd, b, a)
        head, tail = own_ref[x, 0:SUB, cut(h)], own_ref[x, rows_y - SUB :, cut(h)]
        if c % 2:
            before = pltpu.roll(before, DEGREE, 0)
        top = jnp.where(upper, before, pltpu.roll(head, DEGREE, 0))
        if c % 2:
            after = pltpu.roll(after, DEGREE, 0)
        kept = pltpu.roll(tail, SUB - (DEGREE - 1), 0)
        bottom = jnp.where(row < DEGREE + 1, kept, pltpu.roll(after, DEGREE + 1, 0))
        return top, bottom

    for x in range(rows_x):
        before_x = (x - 1) % rows_x
        tiles = [[field(c, x, h) for h in range(blocks_z)] for c in range(4)]
        kxm = [field(1, before_x, h) for h in range(blocks_z)]
        for side in range(2):
            for step in range(DEGREE):
                start = step + 1 if side == 0 else DEGREE - step
                kz = [window(tiles[3][h][side], start) for h in range(blocks_z)]
                kzm = behind(kz, lane)
                for h in range(blocks_z):
                    pot = window(tiles[0][h][side], start)
                    kx = window(tiles[1][h][side], start)
                    ky = window(tiles[2][h][side], start)
                    kym = window(tiles[2][h][side], start - 1)
                    total = kx + window(kxm[h][side], start) + ky + kym + kz[h] + kzm[h]
                    inner, outer = (ky, kym) if side == 0 else (kym, ky)
                    coef_ref[side, step, 0, x, h] = unit * total + (2.0 * unit) * (pot - CENTRE)
                    coef_ref[side, step, 1, x, h] = unit * kx
                    coef_ref[side, step, 2, x, h] = unit * inner
                    coef_ref[side, step, 3, x, h] = unit * outer
                    coef_ref[side, step, 4, x, h] = unit * kz[h]
                    coef_ref[side, step, 5, x, h] = unit * kzm[h]


def edge_kernel(first_pair, k, odd_ref, ha_ref, hb_ref, coef_ref, seam_ref, sums_ref, edge_ref, gram_ref):
    members, rows_x, blocks_z = edge_ref.shape[:3]
    odd = odd_ref[0] == 1
    row, lane = iotas()
    upper = row < DEGREE

    def run(pair, side, w):
        turn, mark = (SUB - 1, row % DEGREE == DEGREE - 1) if side == 0 else (1, row % DEGREE == 0)
        last = None
        for step in range(DEGREE):
            seam = seam_ref.at[k * (members // 2) + pair, side, step]
            coef = coef_ref.at[side, step]
            centre, inner = [], []
            for x in range(rows_x):
                centre.append(
                    [jnp.where(mark, seam[0, x, h], pltpu.roll(w[x][h], turn, 0)) for h in range(blocks_z)]
                )
                inner.append(
                    [jnp.where(mark, seam[1, x, h], pltpu.roll(centre[x][h], turn, 0)) for h in range(blocks_z)]
                )
            fresh = []
            for x in range(rows_x):
                up_x, down_x = (x + 1) % rows_x, (x - 1) % rows_x
                front, back = ahead(centre[x], lane), behind(centre[x], lane)
                line = []
                for h in range(blocks_z):
                    total = coef[0, x, h] * centre[x][h]
                    total = total - coef[1, x, h] * centre[up_x][h]
                    total = total - coef[1, down_x, h] * centre[down_x][h]
                    total = total - coef[2, x, h] * inner[x][h]
                    total = total - coef[3, x, h] * w[x][h]
                    total = total - coef[4, x, h] * front[h]
                    total = total - coef[5, x, h] * back[h]
                    line.append(0.5 * total if step == 0 else total - last[x][h])
                fresh.append(line)
            last, w = inner, fresh
        return w

    def both(pair, carry):
        a = [[ha_ref[first_pair + pair, x, :, cut(h)] for h in range(blocks_z)] for x in range(rows_x)]
        b = [[hb_ref[first_pair + pair, x, :, cut(h)] for h in range(blocks_z)] for x in range(rows_x)]
        before = [[jnp.where(odd, a[x][h], b[x][h]) for h in range(blocks_z)] for x in range(rows_x)]
        top = run(pair, 0, before)
        after = [[jnp.where(odd, b[x][h], a[x][h]) for h in range(blocks_z)] for x in range(rows_x)]
        bottom = run(pair, 1, after)
        for x in range(rows_x):
            for h in range(blocks_z):
                edge_ref[2 * pair, x, h] = jnp.where(upper, top[x][h], pltpu.roll(bottom[x][h], DEGREE, 0))
                edge_ref[2 * pair + 1, x, h] = jnp.where(upper, pltpu.roll(top[x][h], DEGREE, 0), bottom[x][h])
        return carry

    lax.fori_loop(0, members // 2, both, 0)

    pairs = pairs_of(members)

    def gather(x, sums):
        sums = list(sums)
        for h in range(blocks_z):
            f = [edge_ref[a, x, h] for a in range(members)]
            for i, (a, b) in enumerate(pairs):
                sums[i] = sums[i] + f[a] * f[b]
        return tuple(sums)

    sums = lax.fori_loop(0, rows_x, gather, tuple(sums_ref[k, i] for i in range(len(pairs))))
    at = {pair: jnp.sum(s, axis=0, keepdims=True) for pair, s in zip(pairs, sums)}
    column_of = lax.broadcasted_iota(jnp.int32, (members, members), 1)
    gram = jnp.zeros((members, members), jnp.float32)
    for a in range(members):
        column = jnp.concatenate([at[min(a, b), max(a, b)] for b in range(members)], 0)
        gram = jnp.where(column_of == a, jnp.sum(column, axis=1, keepdims=True), gram)
    gram_ref[...] = gram


def assemble_kernel(body_ref, *refs):
    out_ref = refs[-1]
    count, rows_x, rows_y, depth = out_ref.shape
    row, _ = iotas()
    upper = row < DEGREE
    members = refs[0].shape[0]

    for k, edge_ref in enumerate(refs[:-1]):
        for a in range(members):
            for x in range(rows_x):
                for h in range(depth // LANES):
                    body, edge = body_ref[k * members + a, x, h], edge_ref[a, x, h]
                    out_ref[k * members + a, x, 0:SUB, cut(h)] = jnp.where(upper, edge, body)
                    out_ref[k * members + a, x, rows_y - SUB :, cut(h)] = jnp.where(upper, body, edge)


def density_kernel(body_ref, gram_ref, occ_ref, *refs):
    edge_refs, out_ref = refs[:-1], refs[-1]
    rows_x, rows_y, depth = out_ref.shape
    blocks, members, _ = gram_ref.shape
    row, _ = iotas()
    upper = row < DEGREE
    down = lax.broadcasted_iota(jnp.int32, (members, members), 0)
    along = lax.broadcasted_iota(jnp.int32, (members, members), 1)
    w = []
    for k in range(blocks):
        ratio = jnp.broadcast_to(occ_ref[k : k + 1, :], (members, members)) / (gram_ref[k] + EPSILON)
        column = jnp.sum(jnp.where(down == along, ratio, 0.0), axis=1, keepdims=True)
        w += [jnp.broadcast_to(column[a : a + 1, :], (SUB, LANES)) for a in range(members)]
    for x in range(rows_x):
        for h in range(depth // LANES):
            body = edge = None
            for k, edge_ref in enumerate(edge_refs):
                for a in range(members):
                    i = k * members + a
                    f, g = body_ref[i, x, h], edge_ref[a, x, h]
                    f, g = w[i] * (f * f), w[i] * (g * g)
                    body, edge = (f, g) if body is None else (body + f, edge + g)
            out_ref[x, 0:SUB, cut(h)] = jnp.where(upper, edge, body)
            out_ref[x, rows_y - SUB :, cut(h)] = jnp.where(upper, body, edge)


def vmem():
    return pl.BlockSpec(memory_space=pltpu.VMEM)


def smem():
    return pl.BlockSpec(memory_space=pltpu.SMEM)


def anywhere():
    return pl.BlockSpec(memory_space=pltpu.HBM)


def call(kernel, name, operands, outs, scratch=(), specs=None, place=jax.ShapeDtypeStruct, limit=8):
    shapes = tuple(place(shape, jnp.float32) for shape in outs)
    return pl.pallas_call(
        kernel,
        out_shape=shapes,
        in_specs=[vmem() for _ in operands] if specs is None else specs,
        out_specs=tuple(vmem() for _ in outs),
        scratch_shapes=[pltpu.VMEM(shape, jnp.float32) if isinstance(shape, tuple) else shape for shape in scratch],
        compiler_params=pltpu.CompilerParams(vmem_limit_bytes=limit * 1024 * 1024),
        name=name,
    )(*operands)


def fast_body(orbitals, potential, kinetic, occupations):
    blocks, members, _, rows_x, rows_y, depth = orbitals.shape
    count = blocks * members
    domains = lax.axis_size("grid")
    position = lax.axis_index("grid")
    parts = rows_y // SUB
    blocks_z = depth // LANES
    tile = (SUB, LANES)
    odd = (position % 2).astype(jnp.int32).reshape(1)

    pairs_a = [(i, i ^ 1) for i in range(domains)]
    pairs_b = [(i, (i + 1) % domains if i % 2 else (i - 1) % domains) for i in range(domains)]
    half = members // 2
    sizes = [half + (2 if k == 0 else 0) for k in range(blocks)]
    *packed, pot, kin, fields = call(
        functools.partial(pack_kernel, blocks),
        "pack",
        (
            odd,
            pltpu.with_memory_space_constraint(potential[0], pltpu.HBM),
            pltpu.with_memory_space_constraint(kinetic[:, 0], pltpu.HBM),
            pltpu.with_memory_space_constraint(orbitals.reshape(count, rows_x, rows_y, depth), pltpu.HBM),
        ),
        [(size, rows_x, SUB, depth) for size in sizes for _ in range(2)]
        + [(rows_x, rows_y, depth), (3, rows_x, rows_y, depth), (count, rows_x, rows_y, depth)],
        [pltpu.SemaphoreType.DMA((2 + blocks,))],
        specs=[smem()] + [anywhere()] * 3,
        place=pltpu.VMEM,
    )
    halos = [
        lax.ppermute(value, "grid", pairs_b if i % 2 else pairs_a) for i, value in enumerate(packed)
    ]

    body, seam, sums = call(
        functools.partial(interior_kernel, members),
        "interior",
        (pot, kin, fields),
        [
            (count, rows_x, blocks_z) + tile,
            (count // 2, 2, DEGREE, 2, rows_x, blocks_z) + tile,
            (blocks, len(pairs_of(members))) + tile,
        ],
        [
            (6, rows_x, parts, blocks_z) + tile,
            (4, rows_x, blocks_z, rows_y, LANES),
            (2, rows_x, blocks_z, rows_y, LANES),
        ],
    )
    (coef,) = call(
        windows_kernel,
        "windows",
        (odd, pot, kin, halos[0], halos[1]),
        [(2, DEGREE, 6, rows_x, blocks_z) + tile],
        specs=[smem()] + [vmem()] * 4,
    )
    edges, grams = [], []
    for k in range(blocks):
        edge, gram = call(
            functools.partial(edge_kernel, sizes[k] - half, k),
            "edge",
            (odd, halos[2 * k], halos[2 * k + 1], coef, seam, sums),
            [(members, rows_x, blocks_z) + tile, (members, members)],
            specs=[smem()] + [vmem()] * 5,
        )
        edges.append(edge)
        grams.append(gram)

    cells = rows_x * rows_y * depth * domains
    gram = jnp.stack(grams) * (1.0 / cells)
    bit = 1
    while bit < domains:
        gram = gram + swapped(gram, "grid", bit)
        bit *= 2

    (filtered,) = call(assemble_kernel, "assemble", (body, *edges), [fields.shape])
    (partial_value,) = call(density_kernel, "density", (body, gram, occupations, *edges), [pot.shape])

    bands = lax.axis_size("band")
    band = lax.axis_index("band")
    share = rows_y // bands
    value = partial_value.reshape(rows_x, bands, share, depth)
    bit = 1
    width = bands
    while bit < bands:
        value = value.reshape(rows_x, width // 2, 2, share, depth)
        mine = (band // bit) % 2
        keep = lax.dynamic_index_in_dim(value, mine, 2, False)
        send = lax.dynamic_index_in_dim(value, 1 - mine, 2, False)
        value = keep + swapped(send, "band", bit)
        bit *= 2
        width //= 2
    density = value.reshape(1, rows_x, share, depth)
    return filtered.reshape(orbitals.shape), gram, density


def extend(field, width, across):
    lower = shifted(field[..., -width:, :, :], "grid", across)
    upper = shifted(field[..., :width, :, :], "grid", -across)
    widened = jnp.concatenate([lower, field, upper], -3)
    column = lax.axis_index("grid") % across
    left_plain = shifted(widened[..., :, -width:, :], "grid", 1)
    left_wrap = shifted(widened[..., :, -width:, :], "grid", -(across - 1))
    left = jnp.where(column == 0, left_wrap, left_plain)
    right_plain = shifted(widened[..., :, :width, :], "grid", -1)
    right_wrap = shifted(widened[..., :, :width, :], "grid", across - 1)
    right = jnp.where(column == across - 1, right_wrap, right_plain)
    return jnp.concatenate([left, widened, right], -2)


def hamilton(field, coeffs):
    inner = field[..., 1:-1, 1:-1, :]
    kin_x = coeffs[1]
    total = kin_x[1:-1, 1:-1] * (inner - field[..., 2:, 1:-1, :])
    total = total + kin_x[:-2, 1:-1] * (inner - field[..., :-2, 1:-1, :])
    kin_y = coeffs[2]
    total = total + kin_y[1:-1, 1:-1] * (inner - field[..., 1:-1, 2:, :])
    total = total + kin_y[1:-1, :-2] * (inner - field[..., 1:-1, :-2, :])
    kin_z = coeffs[3, 1:-1, 1:-1]
    total = total + kin_z * (inner - jnp.roll(inner, -1, -1))
    total = total + jnp.roll(kin_z, 1, -1) * (inner - jnp.roll(inner, 1, -1))
    return 0.5 * total + coeffs[0, 1:-1, 1:-1] * inner


def general_body(across, orbitals, potential, kinetic, occupations):
    blocks = orbitals.shape[0]
    members = orbitals.shape[1]
    rows_x = orbitals.shape[3]
    rows_y = orbitals.shape[4]
    coeffs = jnp.concatenate([potential, kinetic[:, 0]], 0)
    current = orbitals[:, :, 0]
    previous = current
    coeff_ext = None
    for degree_step in range(DEGREE):
        if degree_step == 0:
            stacked = jnp.concatenate(
                [coeffs, current.reshape((blocks * members,) + current.shape[2:])], 0
            )
            wide = extend(stacked, 1, across)
            coeff_ext = wide[:4]
            extended = wide[4:].reshape((blocks, members) + wide.shape[1:])
        else:
            extended = extend(current, 1, across)
        image = hamilton(extended, coeff_ext)
        inner = extended[..., 1:-1, 1:-1, :]
        if degree_step == 0:
            fresh = (image - CENTRE * inner) / HALF_WIDTH
        else:
            fresh = 2.0 / HALF_WIDTH * (image - CENTRE * inner) - previous
        previous = current
        current = fresh
    cells = rows_x * rows_y * orbitals.shape[5] * lax.axis_size("grid")
    flat = current.reshape(blocks, members, -1)
    local_gram = jnp.einsum("kbx,kcx->kbc", flat, flat, precision=lax.Precision.HIGHEST) / cells
    gram = lax.psum(local_gram, "grid")
    diagonal = jnp.diagonal(gram, axis1=1, axis2=2)
    weight = occupations / (diagonal + EPSILON)
    partial_value = jnp.einsum(
        "kb,kbxyz->xyz", weight, current * current, precision=lax.Precision.HIGHEST
    )
    density = lax.psum_scatter(partial_value[None], "band", scatter_dimension=2, tiled=True)
    return (current[:, :, None], gram, density)


def solution(mesh):
    domains = mesh.shape["grid"]
    across = min(domains, 8)
    if domains == across and domains & (domains - 1) == 0 and domains > 1:
        body = fast_body
    else:
        body = functools.partial(general_body, across)
    placed = (
        P("band", None, "grid", None, None, None),
        P("grid", None, None, None),
        P(None, "grid", None, None, None),
        P("band", None),
    )
    return jax.shard_map(
        body,
        mesh=mesh,
        in_specs=placed,
        out_specs=(
            P("band", None, "grid", None, None, None),
            P("band", None, None),
            P("grid", None, "band", None),
        ),
        check_vma=False,
    )
```

time: 120 us -> 40.1 us (0.33)
  waiting for transfers between devices: 51.1 us -> 9.59 us
  blocking collectives: 17.4 us -> 0 us
  between operations: 15.1 us -> 0.76 us
  Pallas kernels: 0 us -> 11.4 us
  other arithmetic: 11 us -> 0.65 us
  local copies, waits for them, and re-layouts: 7.27 us -> 0.06 us
  starting transfers between devices: 13.9 us -> 17.5 us
  matrix products: 3.48 us -> 0 us
    unnamed x2 -> x0, waiting for transfers between devices: 29.1 us -> none
    psum x1 -> x0, blocking collectives: 17.4 us -> none  [body(): gram = lax.psum(local_gram, 'grid')]
    ppermute x16 -> x9, waiting for transfers between devices: 22 us -> 9.59 us  [the longest x5 7.25 us: swapped(): return lax.ppermute(value, axis, [(i, i ^ bit) for i in range(count)])]
    pallas_call x0 -> x7, Pallas kernels: none -> 11.4 us  [call(): pl.pallas_call(kernel, out_shape=shapes, in_specs=[vmem() for _ in operan...]
    ppermute x16 -> x9, starting transfers between devices: 13.9 us -> 17.5 us  [the longest x5 9 us: swapped(): return lax.ppermute(value, axis, [(i, i ^ bit) for i in range(count)])]
    dot_general x2 -> x0, matrix products: 3.48 us -> none  [the longest x1 2.22 us: body(): jnp.einsum('kbx,kcx->kbc', flat, flat, precision=lax.Precision.HIGHEST)]
    sub x2 -> x0, other arithmetic: 3.24 us -> none  [advance(): return 2.0 / HALF_WIDTH * (image - CENTRE * inner) - previous]
    mul x2 -> x1, other arithmetic: 3.09 us -> 0.01 us  [fast_body(): gram = jnp.stack(grams) * (1.0 / cells)]
  transfers between devices with their start and end apart: 17 -> 9, of which waited for: 9 -> 7; matrix products, arithmetic and copies ran while one was open for 4% -> 0% of each run, Pallas kernels for 0% -> 20%
where the time goes in v1:
time: 40.1 us; the launch traced here: 39.9 us
  starting transfers between devices  17.5 us (44%)
  Pallas kernels  11.4 us (28%)
  waiting for transfers between devices  9.59 us (24%)
  between operations  0.76 us (2%)
  other arithmetic  0.65 us (2%)
    pallas_call x7, Pallas kernels, call(): pl.pallas_call(kernel, out_shape=shapes, in_specs=[vmem() for _ in operan...  11.4 us
    ppermute x5, starting transfers between devices, swapped(): return lax.ppermute(value, axis, [(i, i ^ bit) for i in range(count)])  9 us
    ppermute x4, starting transfers between devices, fast_body(): lax.ppermute(value, 'grid', pairs_b if i % 2 else pairs_a)  8.52 us
    ppermute x5, waiting for transfers between devices, swapped(): return lax.ppermute(value, axis, [(i, i ^ bit) for i in range(count)])  7.25 us
    ppermute x4, waiting for transfers between devices, fast_body(): lax.ppermute(value, 'grid', pairs_b if i % 2 else pairs_a)  2.34 us
  transfers between devices with their start and end apart: 9, of which 7 were waited for; matrix products, arithmetic and copies ran while one was open for 0% of the time, Pallas kernels for 20%

profile of v1, /device:TPU:0, one launch (start us, length us, event | category | flops | bytes accessed | tf_op | source)
XLA Modules:
  0.0 39.9 jit_solution(1964748503470078212)
XLA Ops:
  0.6 1.4 %pack.1 = (f32[6,4,8,256]{3,2,1,0:T(8,128)S(1)}, f32[6,4,8,256]{3,2,1,0:T(8,128)S(1)}, f32[4,4,8,256]{3,2,1,0:T(8,128)S(1)}, f32[4,4,8,256]{3,2,1,0:T(8,128)S(1)...) custom-call(s32[1]{0:T(128)} %bitcast.odd_ref, ...), custom_call_target="tpu_custom_call" | custom-call | tf_op jit(solution)/shard_map/pack/pallas_call | solution.py:394
  2.1 3.1 %collective-permute-start = (f32[6,4,8,256]{3,2,1,0:T(8,128)S(1)}, f32[6,4,8,256]{3,2,1,0:T(8,128)S(1)}, u32[]{:S(2)}, u32[]{:S(2)}) collective-permute-start(f32[6,4,8,256]{3,2,1,0:T(8,128)S(1)} %get-tuple-element.21), channel_id=1, source_target_pairs={{0,1},{1,0},{2,3},{3,2},{4,5},{5,4},{6,7},{7,6},{8,9},{9,8},{10,11... | collective-permute-start | bytes 589832 | tf_op jit(solution)/shard_map/ppermute | solution.py:435
  5.1 3.5 %collective-permute-start.1 = (f32[6,4,8,256]{3,2,1,0:T(8,128)S(1)}, f32[6,4,8,256]{3,2,1,0:T(8,128)S(1)}, u32[]{:S(2)}, u32[]{:S(2)}) collective-permute-start(f32[6,4,8,256]{3,2,1,0:T(8,128)S(1)} %get-tuple-element.22), channel_id=1, source_target_pairs={{0,7},{1,2},{2,1},{3,4},{4,3},{5,6},{6,5},{7,0},{8,15},{9,10},{10,... | collective-permute-start | bytes 589832 | tf_op jit(solution)/shard_map/ppermute | solution.py:435
  8.7 0.0 collective-permute-start.2
  8.7 1.9 %collective-permute-start.3 = (f32[4,4,8,256]{3,2,1,0:T(8,128)S(1)}, f32[4,4,8,256]{3,2,1,0:T(8,128)S(1)}, u32[]{:S(2)}, u32[]{:S(2)}) collective-permute-start(f32[4,4,8,256]{3,2,1,0:T(8,128)S(1)} %get-tuple-element.27), channel_id=1, source_target_pairs={{0,7},{1,2},{2,1},{3,4},{4,3},{5,6},{6,5},{7,0},{8,15},{9,10},{10,... | collective-permute-start | bytes 393224 | tf_op jit(solution)/shard_map/ppermute | solution.py:435
  10.6 4.8 %interior.1 = (f32[16,4,2,8,128]{4,3,2,1,0:T(8,128)S(1)}, f32[8,2,4,2,4,2,8,128]{7,6,5,4,3,2,1,0:T(8,128)S(1)}, f32[2,36,8,128]{3,2,1,0:T(8,128)S(1)}) custom-call(f32[4,16,256]{2,1,0:T(8,128)S(1)} %get-tuple-element.17.pot_ref, f32[3,4,16,256]{3,2,1,0:T(8,128)S(1)} %get-tuple-element.18.kin_ref, f32[16,4,16,256]{3,2,1,0:T(8,128)S(1)} %get-tuple-element.19.orb_ref), custom_call_target="tpu_custom_call" | custom-call | tf_op jit(solution)/shard_map/interior/pallas_call | solution.py:394
  15.4 2.0 %collective-permute-done.ha_ref = f32[6,4,8,256]{3,2,1,0:T(8,128)S(1)} collective-permute-done((f32[6,4,8,256]{3,2,1,0:T(8,128)S(1)}, f32[6,4,8,256]{3,2,1,0:T(8,128)S(1)}, u32[]{:S(2)}, u32[]{:S(2)}) %collective-permute-start) | collective-permute-done | bytes 196640 | tf_op jit(solution)/shard_map/ppermute | solution.py:435
  17.4 0.0 collective-permute-done.1.hb_ref
  17.4 0.3 windows.1.coef_ref
  17.7 1.8 %edge.2 = (f32[8,4,2,8,128]{4,3,2,1,0:T(8,128)S(1)}, f32[8,8]{1,0:T(8,128)S(1)}) custom-call(s32[1]{0:T(128)} %bitcast.odd_ref, f32[6,4,8,256]{3,2,1,0:T(8,128)S(1)} %collective-permute-done.ha_ref, f32[6,4,8,256]{3,2,1,0:T(8,128)S(1)} %collective-permute-done.1.hb_ref, f32[2,4,6,4,2,8,128]{6,5,4,3,2,1,0:T(8,128)S(1)} %windows.1.coef_ref, ...), custom_call_target="tpu_custom_call" | custom-call | tf_op jit(solution)/shard_map/edge/pallas_call | solution.py:394
  19.5 0.0 copy-start.1
  19.5 0.3 collective-permute-done.2.ha_ref
  19.8 0.0 collective-permute-done.3.hb_ref
  19.9 1.8 %edge.3 = (f32[8,4,2,8,128]{4,3,2,1,0:T(8,128)S(1)}, f32[8,8]{1,0:T(8,128)S(1)}) custom-call(s32[1]{0:T(128)} %bitcast.odd_ref, f32[4,4,8,256]{3,2,1,0:T(8,128)S(1)} %collective-permute-done.2.ha_ref, f32[4,4,8,256]{3,2,1,0:T(8,128)S(1)} %collective-permute-done.3.hb_ref, f32[2,4,6,4,2,8,128]{6,5,4,3,2,1,0:T(8,128)S(1)} %windows.1.coef_ref, ...), custom_call_target="tpu_custom_call" | custom-call | tf_op jit(solution)/shard_map/edge/pallas_call | solution.py:394
  21.7 2.2 %collective-permute-start.4 = (f32[2,8,8]{2,1,0:T(8,128)S(1)}, f32[2,8,8]{2,1,0:T(8,128)S(1)}, u32[]{:S(2)}, u32[]{:S(2)}) collective-permute-start(f32[2,8,8]{2,1,0:T(8,128)S(1)} %maximum_multiply_fusion), channel_id=1, source_target_pairs={{0,1},{1,0},{2,3},{3,2},{4,5},{5,4},{6,7},{7,6},{8,9},{9,8},{10,11... | collective-permute-start | bytes 1544 | tf_op jit(solution)/shard_map/ppermute | solution.py:27
  23.9 1.6 %collective-permute-done.4 = f32[2,8,8]{2,1,0:T(8,128)S(1)} collective-permute-done((f32[2,8,8]{2,1,0:T(8,128)S(1)}, f32[2,8,8]{2,1,0:T(8,128)S(1)}, u32[]{:S(2)}, u32[]{:S(2)}) %collective-permute-start.4) | collective-permute-done | bytes 544 | tf_op jit(solution)/shard_map/ppermute | solution.py:27
  25.6 2.1 %collective-permute-start.5 = (f32[2,8,8]{2,1,0:T(8,128)S(1)}, f32[2,8,8]{2,1,0:T(8,128)S(1)}, u32[]{:S(2)}, u32[]{:S(2)}) collective-permute-start(f32[2,8,8]{2,1,0:T(8,128)S(1)} %fusion), channel_id=1, source_target_pairs={{0,2},{1,3},{2,0},{3,1},{4,6},{5,7},{6,4},{7,5},{8,10},{9,11},{10,... | collective-permute-start | bytes 1544 | tf_op jit(solution)/shard_map/ppermute | solution.py:27
  27.7 1.6 %collective-permute-done.5 = f32[2,8,8]{2,1,0:T(8,128)S(1)} collective-permute-done((f32[2,8,8]{2,1,0:T(8,128)S(1)}, f32[2,8,8]{2,1,0:T(8,128)S(1)}, u32[]{:S(2)}, u32[]{:S(2)}) %collective-permute-start.5) | collective-permute-done | bytes 544 | tf_op jit(solution)/shard_map/ppermute | solution.py:27
  29.3 3.0 %collective-permute-start.6 = (f32[2,8,8]{2,1,0:T(8,128)S(1)}, f32[2,8,8]{2,1,0:T(8,128)S(1)}, u32[]{:S(2)}, u32[]{:S(2)}) collective-permute-start(f32[2,8,8]{2,1,0:T(8,128)S(1)} %fusion.1), channel_id=1, source_target_pairs={{0,4},{1,5},{2,6},{3,7},{4,0},{5,1},{6,2},{7,3},{8,12},{9,13},{10,... | collective-permute-start | bytes 1544 | tf_op jit(solution)/shard_map/ppermute | solution.py:27
  32.3 1.6 %collective-permute-done.6 = f32[2,8,8]{2,1,0:T(8,128)S(1)} collective-permute-done((f32[2,8,8]{2,1,0:T(8,128)S(1)}, f32[2,8,8]{2,1,0:T(8,128)S(1)}, u32[]{:S(2)}, u32[]{:S(2)}) %collective-permute-start.6) | collective-permute-done | bytes 544 | tf_op jit(solution)/shard_map/ppermute | solution.py:27
  34.0 0.0 copy-start
  34.0 0.0 copy-done.1
  34.0 0.2 density.1
  34.2 0.1 collective-permute-start.7
  34.3 1.2 %collective-permute-done.7 = f32[4,2,4,256]{3,2,0,1:T(4,128)S(1)} collective-permute-done((f32[4,2,4,256]{3,2,0,1:T(4,128)S(1)}, f32[4,2,4,256]{3,2,0,1:T(4,128)S(1)}, u32[]{:S(2)}, u32[]{:S(2)}) %collective-permute-start.7) | collective-permute-done | bytes 32800 | tf_op jit(solution)/shard_map/ppermute | solution.py:27
  35.5 1.6 %collective-permute-start.8 = (f32[4,1,4,256]{3,2,0,1:T(4,128)S(1)}, f32[4,1,4,256]{3,2,0,1:T(4,128)S(1)}, u32[]{:S(2)}, u32[]{:S(2)}) collective-permute-start(f32[4,1,4,256]{3,2,0,1:T(4,128)S(1)} %constant_dynamic-slice_fusion), channel_id=1, source_target_pairs={{0,16},{8,24},{16,0},{24,8},{1,17},{9,25},{17,1},{25,9},{2,18},{10... | collective-permute-start | bytes 49160 | tf_op jit(solution)/shard_map/ppermute | solution.py:27
  37.1 1.0 %assemble.1 = f32[16,4,16,256]{3,2,1,0:T(8,128)} custom-call(f32[16,4,2,8,128]{4,3,2,1,0:T(8,128)S(1)} %get-tuple-element.20.body_ref, f32[8,4,2,8,128]{4,3,2,1,0:T(8,128)S(1)} %get-tuple-element.25.refs_0_, f32[8,4,2,8,128]{4,3,2,1,0:T(8,128)S(1)} %get-tuple-element.28.refs_1_), custom_call_target="tpu_custom_call" | custom-call | tf_op jit(solution)/shard_map/assemble/pallas_call | solution.py:394
  38.1 1.2 %collective-permute-done.8 = f32[4,1,4,256]{3,2,0,1:T(4,128)S(1)} collective-permute-done((f32[4,1,4,256]{3,2,0,1:T(4,128)S(1)}, f32[4,1,4,256]{3,2,0,1:T(4,128)S(1)}, u32[]{:S(2)}, u32[]{:S(2)}) %collective-permute-start.8) | collective-permute-done | bytes 16416 | tf_op jit(solution)/shard_map/ppermute | solution.py:27
  39.3 0.6 %add_bitcast_fusion = f32[1,4,4,256]{3,2,1,0:T(4,128)} fusion(f32[4,1,4,256]{3,2,0,1:T(4,128)S(1)} %collective-permute-done.8, f32[4,2,4,256]{3,2,0,1:T(4,128)S(1)} %bitcast_add_fusion, s32[]{:T(128)S(6)} %select_n.40), kind=kLoop, calls=%fused_computation.2 | loop fusion | flops 4096 | bytes 49156 | tf_op jit(solution)/shard_map/reshape | solution.py:496
  39.9 0.0 copy-done
  (9 shorter events, 0.1 us)
Async XLA Ops:
  2.1 15.4 %collective-permute-start = (f32[6,4,8,256]{3,2,1,0:T(8,128)S(1)}, f32[6,4,8,256]{3,2,1,0:T(8,128)S(1)}, u32[]{:S(2)}, u32[]{:S(2)}) collective-permute-start(f32[6,4,8,256]{3,2,1,0:T(8,128)S(1)} %get-tuple-element.21), channel_id=1, source_target_pairs={{0,1},{1,0},{2,3},{3,2},{4,5},{5,4},{6,7},{7,6},{8,9},{9,8},{10,11... | collective-permute-start | bytes 589832 | tf_op jit(solution)/shard_map/ppermute | solution.py:435
  5.1 12.3 %collective-permute-start.1 = (f32[6,4,8,256]{3,2,1,0:T(8,128)S(1)}, f32[6,4,8,256]{3,2,1,0:T(8,128)S(1)}, u32[]{:S(2)}, u32[]{:S(2)}) collective-permute-start(f32[6,4,8,256]{3,2,1,0:T(8,128)S(1)} %get-tuple-element.22), channel_id=1, source_target_pairs={{0,7},{1,2},{2,1},{3,4},{4,3},{5,6},{6,5},{7,0},{8,15},{9,10},{10,... | collective-permute-start | bytes 589832 | tf_op jit(solution)/shard_map/ppermute | solution.py:435
  8.7 11.2 %collective-permute-start.2 = (f32[4,4,8,256]{3,2,1,0:T(8,128)S(1)}, f32[4,4,8,256]{3,2,1,0:T(8,128)S(1)}, u32[]{:S(2)}, u32[]{:S(2)}) collective-permute-start(f32[4,4,8,256]{3,2,1,0:T(8,128)S(1)} %get-tuple-element.26), channel_id=1, source_target_pairs={{0,1},{1,0},{2,3},{3,2},{4,5},{5,4},{6,7},{7,6},{8,9},{9,8},{10,11... | collective-permute-start | bytes 393224 | tf_op jit(solution)/shard_map/ppermute | solution.py:435
  8.7 11.2 %collective-permute-start.3 = (f32[4,4,8,256]{3,2,1,0:T(8,128)S(1)}, f32[4,4,8,256]{3,2,1,0:T(8,128)S(1)}, u32[]{:S(2)}, u32[]{:S(2)}) collective-permute-start(f32[4,4,8,256]{3,2,1,0:T(8,128)S(1)} %get-tuple-element.27), channel_id=1, source_target_pairs={{0,7},{1,2},{2,1},{3,4},{4,3},{5,6},{6,5},{7,0},{8,15},{9,10},{10,... | collective-permute-start | bytes 393224 | tf_op jit(solution)/shard_map/ppermute | solution.py:435
  19.5 14.5 %copy-start.1 = (f32[2,8]{1,0:T(2,128)S(1)}, f32[2,8]{1,0:T(2,128)}, u32[]{:S(2)}) copy-start(f32[2,8]{1,0:T(2,128)} %occ_ref.1) | copy-start | bytes 196
  21.7 3.9 %collective-permute-start.4 = (f32[2,8,8]{2,1,0:T(8,128)S(1)}, f32[2,8,8]{2,1,0:T(8,128)S(1)}, u32[]{:S(2)}, u32[]{:S(2)}) collective-permute-start(f32[2,8,8]{2,1,0:T(8,128)S(1)} %maximum_multiply_fusion), channel_id=1, source_target_pairs={{0,1},{1,0},{2,3},{3,2},{4,5},{5,4},{6,7},{7,6},{8,9},{9,8},{10,11... | collective-permute-start | bytes 1544 | tf_op jit(solution)/shard_map/ppermute | solution.py:27
  25.6 3.7 %collective-permute-start.5 = (f32[2,8,8]{2,1,0:T(8,128)S(1)}, f32[2,8,8]{2,1,0:T(8,128)S(1)}, u32[]{:S(2)}, u32[]{:S(2)}) collective-permute-start(f32[2,8,8]{2,1,0:T(8,128)S(1)} %fusion), channel_id=1, source_target_pairs={{0,2},{1,3},{2,0},{3,1},{4,6},{5,7},{6,4},{7,5},{8,10},{9,11},{10,... | collective-permute-start | bytes 1544 | tf_op jit(solution)/shard_map/ppermute | solution.py:27
  29.3 4.7 %collective-permute-start.6 = (f32[2,8,8]{2,1,0:T(8,128)S(1)}, f32[2,8,8]{2,1,0:T(8,128)S(1)}, u32[]{:S(2)}, u32[]{:S(2)}) collective-permute-start(f32[2,8,8]{2,1,0:T(8,128)S(1)} %fusion.1), channel_id=1, source_target_pairs={{0,4},{1,5},{2,6},{3,7},{4,0},{5,1},{6,2},{7,3},{8,12},{9,13},{10,... | collective-permute-start | bytes 1544 | tf_op jit(solution)/shard_map/ppermute | solution.py:27
  34.0 6.0 %copy-start = (f32[2,8,8]{2,1,0:T(8,128)}, f32[2,8,8]{2,1,0:T(8,128)S(1)}, u32[]{:S(2)}) copy-start(f32[2,8,8]{2,1,0:T(8,128)S(1)} %add.46.gram_ref) | copy-start | bytes 1540
  34.2 1.3 %collective-permute-start.7 = (f32[4,2,4,256]{3,2,0,1:T(4,128)S(1)}, f32[4,2,4,256]{3,2,0,1:T(4,128)S(1)}, u32[]{:S(2)}, u32[]{:S(2)}) collective-permute-start(f32[4,2,4,256]{3,2,0,1:T(4,128)S(1)} %bitcast.26), channel_id=1, source_target_pairs={{0,8},{8,0},{16,24},{24,16},{1,9},{9,1},{17,25},{25,17},{2,10},{10... | collective-permute-start | bytes 98312 | tf_op jit(solution)/shard_map/ppermute | solution.py:27
  35.5 3.8 %collective-permute-start.8 = (f32[4,1,4,256]{3,2,0,1:T(4,128)S(1)}, f32[4,1,4,256]{3,2,0,1:T(4,128)S(1)}, u32[]{:S(2)}, u32[]{:S(2)}) collective-permute-start(f32[4,1,4,256]{3,2,0,1:T(4,128)S(1)} %constant_dynamic-slice_fusion), channel_id=1, source_target_pairs={{0,16},{8,24},{16,0},{24,8},{1,17},{9,25},{17,1},{25,9},{2,18},{10... | collective-permute-start | bytes 49160 | tf_op jit(solution)/shard_map/ppermute | solution.py:27

commit v2 on v1

--- a/solution.py
+++ b/solution.py
@@ -193,7 +193,7 @@
         one(pair, 1)
         return carry
 
-    lax.fori_loop(0, count // 2, both, 0)
+    lax.fori_loop(0, count // 2, both, 0, unroll=True)
 
     pairs = pairs_of(members)
     for k in range(count // members):
@@ -206,7 +206,7 @@
                     sums[i] = sums[i] + f[a] * f[b]
             return tuple(sums)
 
-        sums = lax.fori_loop(0, rows_x, gather, tuple(jnp.zeros((SUB, LANES), jnp.float32) for _ in pairs))
+        sums = lax.fori_loop(0, rows_x, gather, tuple(jnp.zeros((SUB, LANES), jnp.float32) for _ in pairs), unroll=True)
         for i, value in enumerate(sums):
             sums_ref[k, i] = value
 
@@ -313,7 +313,7 @@
                 edge_ref[2 * pair + 1, x, h] = jnp.where(upper, pltpu.roll(top[x][h], DEGREE, 0), bottom[x][h])
         return carry
 
-    lax.fori_loop(0, members // 2, both, 0)
+    lax.fori_loop(0, members // 2, both, 0, unroll=True)
 
     pairs = pairs_of(members)
 
@@ -325,7 +325,7 @@
                 sums[i] = sums[i] + f[a] * f[b]
         return tuple(sums)
 
-    sums = lax.fori_loop(0, rows_x, gather, tuple(sums_ref[k, i] for i in range(len(pairs))))
+    sums = lax.fori_loop(0, rows_x, gather, tuple(sums_ref[k, i] for i in range(len(pairs))), unroll=True)
     at = {pair: jnp.sum(s, axis=0, keepdims=True) for pair, s in zip(pairs, sums)}
     column_of = lax.broadcasted_iota(jnp.int32, (members, members), 1)
     gram = jnp.zeros((members, members), jnp.float32)

time: 40.1 us -> 39.3 us (0.980)
  Pallas kernels: 11.4 us -> 9.33 us
  waiting for transfers between devices: 9.59 us -> 11.5 us
  starting transfers between devices: 17.5 us -> 16.9 us
    pallas_call x7, Pallas kernels: 11.4 us -> 9.33 us  [call(): pl.pallas_call(kernel, out_shape=shapes, in_specs=[vmem() for _ in operan...]
    ppermute x4, waiting for transfers between devices: 2.34 us -> 3.94 us  [fast_body(): lax.ppermute(value, 'grid', pairs_b if i % 2 else pairs_a)]
    ppermute x5, starting transfers between devices: 9 us -> 8.38 us  [swapped(): return lax.ppermute(value, axis, [(i, i ^ bit) for i in range(count)])]
  transfers between devices with their start and end apart: 9 -> 9, of which waited for: 7 -> 7; matrix products, arithmetic and copies ran while one was open for 0% -> 0% of each run, Pallas kernels for 20% -> 16%
where the time goes in v2:
time: 39.3 us; the launch traced here: 39.2 us
  starting transfers between devices  16.9 us (43%)
  waiting for transfers between devices  11.5 us (29%)
  Pallas kernels  9.33 us (24%)
  between operations  0.77 us (2%)
  other arithmetic  0.65 us (2%)
    pallas_call x7, Pallas kernels, call(): pl.pallas_call(kernel, out_shape=shapes, in_specs=[vmem() for _ in operan...  9.33 us
    ppermute x4, starting transfers between devices, fast_body(): lax.ppermute(value, 'grid', pairs_b if i % 2 else pairs_a)  8.52 us
    ppermute x5, starting transfers between devices, swapped(): return lax.ppermute(value, axis, [(i, i ^ bit) for i in range(count)])  8.38 us
    ppermute x5, waiting for transfers between devices, swapped(): return lax.ppermute(value, axis, [(i, i ^ bit) for i in range(count)])  7.53 us
    ppermute x4, waiting for transfers between devices, fast_body(): lax.ppermute(value, 'grid', pairs_b if i % 2 else pairs_a)  3.94 us
  transfers between devices with their start and end apart: 9, of which 7 were waited for; matrix products, arithmetic and copies ran while one was open for 0% of the time, Pallas kernels for 16%

profile of v2, /device:TPU:0, one launch (start us, length us, event | category | flops | bytes accessed | tf_op | source)
XLA Modules:
  0.0 39.2 jit_solution(14875407476047272868)
XLA Ops:
  0.6 1.4 %pack.1 = (f32[6,4,8,256]{3,2,1,0:T(8,128)S(1)}, f32[6,4,8,256]{3,2,1,0:T(8,128)S(1)}, f32[4,4,8,256]{3,2,1,0:T(8,128)S(1)}, f32[4,4,8,256]{3,2,1,0:T(8,128)S(1)...) custom-call(s32[1]{0:T(128)} %bitcast.odd_ref, ...), custom_call_target="tpu_custom_call" | custom-call | tf_op jit(solution)/shard_map/pack/pallas_call | solution.py:394
  2.1 3.1 %collective-permute-start = (f32[6,4,8,256]{3,2,1,0:T(8,128)S(1)}, f32[6,4,8,256]{3,2,1,0:T(8,128)S(1)}, u32[]{:S(2)}, u32[]{:S(2)}) collective-permute-start(f32[6,4,8,256]{3,2,1,0:T(8,128)S(1)} %get-tuple-element.21), channel_id=1, source_target_pairs={{0,1},{1,0},{2,3},{3,2},{4,5},{5,4},{6,7},{7,6},{8,9},{9,8},{10,11... | collective-permute-start | bytes 589832 | tf_op jit(solution)/shard_map/ppermute | solution.py:435
  5.1 3.5 %collective-permute-start.1 = (f32[6,4,8,256]{3,2,1,0:T(8,128)S(1)}, f32[6,4,8,256]{3,2,1,0:T(8,128)S(1)}, u32[]{:S(2)}, u32[]{:S(2)}) collective-permute-start(f32[6,4,8,256]{3,2,1,0:T(8,128)S(1)} %get-tuple-element.22), channel_id=1, source_target_pairs={{0,7},{1,2},{2,1},{3,4},{4,3},{5,6},{6,5},{7,0},{8,15},{9,10},{10,... | collective-permute-start | bytes 589832 | tf_op jit(solution)/shard_map/ppermute | solution.py:435
  8.7 0.0 collective-permute-start.2
  8.7 1.9 %collective-permute-start.3 = (f32[4,4,8,256]{3,2,1,0:T(8,128)S(1)}, f32[4,4,8,256]{3,2,1,0:T(8,128)S(1)}, u32[]{:S(2)}, u32[]{:S(2)}) collective-permute-start(f32[4,4,8,256]{3,2,1,0:T(8,128)S(1)} %get-tuple-element.27), channel_id=1, source_target_pairs={{0,7},{1,2},{2,1},{3,4},{4,3},{5,6},{6,5},{7,0},{8,15},{9,10},{10,... | collective-permute-start | bytes 393224 | tf_op jit(solution)/shard_map/ppermute | solution.py:435
  10.6 3.6 %interior.1 = (f32[16,4,2,8,128]{4,3,2,1,0:T(8,128)S(1)}, f32[8,2,4,2,4,2,8,128]{7,6,5,4,3,2,1,0:T(8,128)S(1)}, f32[2,36,8,128]{3,2,1,0:T(8,128)S(1)}) custom-call(f32[4,16,256]{2,1,0:T(8,128)S(1)} %get-tuple-element.17.pot_ref, f32[3,4,16,256]{3,2,1,0:T(8,128)S(1)} %get-tuple-element.18.kin_ref, f32[16,4,16,256]{3,2,1,0:T(8,128)S(1)} %get-tuple-element.19.orb_ref), custom_call_target="tpu_custom_call" | custom-call | tf_op jit(solution)/shard_map/interior/pallas_call | solution.py:394
  14.2 3.2 %collective-permute-done.ha_ref = f32[6,4,8,256]{3,2,1,0:T(8,128)S(1)} collective-permute-done((f32[6,4,8,256]{3,2,1,0:T(8,128)S(1)}, f32[6,4,8,256]{3,2,1,0:T(8,128)S(1)}, u32[]{:S(2)}, u32[]{:S(2)}) %collective-permute-start) | collective-permute-done | bytes 196640 | tf_op jit(solution)/shard_map/ppermute | solution.py:435
  17.4 0.0 collective-permute-done.1.hb_ref
  17.4 0.3 windows.1.coef_ref
  17.7 1.4 %edge.2 = (f32[8,4,2,8,128]{4,3,2,1,0:T(8,128)S(1)}, f32[8,8]{1,0:T(8,128)S(1)}) custom-call(s32[1]{0:T(128)} %bitcast.odd_ref, f32[6,4,8,256]{3,2,1,0:T(8,128)S(1)} %collective-permute-done.ha_ref, f32[6,4,8,256]{3,2,1,0:T(8,128)S(1)} %collective-permute-done.1.hb_ref, f32[2,4,6,4,2,8,128]{6,5,4,3,2,1,0:T(8,128)S(1)} %windows.1.coef_ref, ...), custom_call_target="tpu_custom_call" | custom-call | tf_op jit(solution)/shard_map/edge/pallas_call | solution.py:394
  19.1 0.0 copy-start.1
  19.1 0.7 %collective-permute-done.2.ha_ref = f32[4,4,8,256]{3,2,1,0:T(8,128)S(1)} collective-permute-done((f32[4,4,8,256]{3,2,1,0:T(8,128)S(1)}, f32[4,4,8,256]{3,2,1,0:T(8,128)S(1)}, u32[]{:S(2)}, u32[]{:S(2)}) %collective-permute-start.2) | collective-permute-done | bytes 131104 | tf_op jit(solution)/shard_map/ppermute | solution.py:435
  19.8 0.0 collective-permute-done.3.hb_ref
  19.9 1.4 %edge.3 = (f32[8,4,2,8,128]{4,3,2,1,0:T(8,128)S(1)}, f32[8,8]{1,0:T(8,128)S(1)}) custom-call(s32[1]{0:T(128)} %bitcast.odd_ref, f32[4,4,8,256]{3,2,1,0:T(8,128)S(1)} %collective-permute-done.2.ha_ref, f32[4,4,8,256]{3,2,1,0:T(8,128)S(1)} %collective-permute-done.3.hb_ref, f32[2,4,6,4,2,8,128]{6,5,4,3,2,1,0:T(8,128)S(1)} %windows.1.coef_ref, ...), custom_call_target="tpu_custom_call" | custom-call | tf_op jit(solution)/shard_map/edge/pallas_call | solution.py:394
  21.3 1.8 %collective-permute-start.4 = (f32[2,8,8]{2,1,0:T(8,128)S(1)}, f32[2,8,8]{2,1,0:T(8,128)S(1)}, u32[]{:S(2)}, u32[]{:S(2)}) collective-permute-start(f32[2,8,8]{2,1,0:T(8,128)S(1)} %maximum_multiply_fusion), channel_id=1, source_target_pairs={{0,1},{1,0},{2,3},{3,2},{4,5},{5,4},{6,7},{7,6},{8,9},{9,8},{10,11... | collective-permute-start | bytes 1544 | tf_op jit(solution)/shard_map/ppermute | solution.py:27
  23.1 1.9 %collective-permute-done.4 = f32[2,8,8]{2,1,0:T(8,128)S(1)} collective-permute-done((f32[2,8,8]{2,1,0:T(8,128)S(1)}, f32[2,8,8]{2,1,0:T(8,128)S(1)}, u32[]{:S(2)}, u32[]{:S(2)}) %collective-permute-start.4) | collective-permute-done | bytes 544 | tf_op jit(solution)/shard_map/ppermute | solution.py:27
  25.0 1.8 %collective-permute-start.5 = (f32[2,8,8]{2,1,0:T(8,128)S(1)}, f32[2,8,8]{2,1,0:T(8,128)S(1)}, u32[]{:S(2)}, u32[]{:S(2)}) collective-permute-start(f32[2,8,8]{2,1,0:T(8,128)S(1)} %fusion), channel_id=1, source_target_pairs={{0,2},{1,3},{2,0},{3,1},{4,6},{5,7},{6,4},{7,5},{8,10},{9,11},{10,... | collective-permute-start | bytes 1544 | tf_op jit(solution)/shard_map/ppermute | solution.py:27
  26.8 1.8 %collective-permute-done.5 = f32[2,8,8]{2,1,0:T(8,128)S(1)} collective-permute-done((f32[2,8,8]{2,1,0:T(8,128)S(1)}, f32[2,8,8]{2,1,0:T(8,128)S(1)}, u32[]{:S(2)}, u32[]{:S(2)}) %collective-permute-start.5) | collective-permute-done | bytes 544 | tf_op jit(solution)/shard_map/ppermute | solution.py:27
  28.7 2.9 %collective-permute-start.6 = (f32[2,8,8]{2,1,0:T(8,128)S(1)}, f32[2,8,8]{2,1,0:T(8,128)S(1)}, u32[]{:S(2)}, u32[]{:S(2)}) collective-permute-start(f32[2,8,8]{2,1,0:T(8,128)S(1)} %fusion.1), channel_id=1, source_target_pairs={{0,4},{1,5},{2,6},{3,7},{4,0},{5,1},{6,2},{7,3},{8,12},{9,13},{10,... | collective-permute-start | bytes 1544 | tf_op jit(solution)/shard_map/ppermute | solution.py:27
  31.5 1.7 %collective-permute-done.6 = f32[2,8,8]{2,1,0:T(8,128)S(1)} collective-permute-done((f32[2,8,8]{2,1,0:T(8,128)S(1)}, f32[2,8,8]{2,1,0:T(8,128)S(1)}, u32[]{:S(2)}, u32[]{:S(2)}) %collective-permute-start.6) | collective-permute-done | bytes 544 | tf_op jit(solution)/shard_map/ppermute | solution.py:27
  33.2 0.0 copy-start
  33.2 0.0 copy-done.1
  33.2 0.2 density.1
  33.5 0.1 collective-permute-start.7
  33.6 1.2 %collective-permute-done.7 = f32[4,2,4,256]{3,2,0,1:T(4,128)S(1)} collective-permute-done((f32[4,2,4,256]{3,2,0,1:T(4,128)S(1)}, f32[4,2,4,256]{3,2,0,1:T(4,128)S(1)}, u32[]{:S(2)}, u32[]{:S(2)}) %collective-permute-start.7) | collective-permute-done | bytes 32800 | tf_op jit(solution)/shard_map/ppermute | solution.py:27
  34.8 1.8 %collective-permute-start.8 = (f32[4,1,4,256]{3,2,0,1:T(4,128)S(1)}, f32[4,1,4,256]{3,2,0,1:T(4,128)S(1)}, u32[]{:S(2)}, u32[]{:S(2)}) collective-permute-start(f32[4,1,4,256]{3,2,0,1:T(4,128)S(1)} %constant_dynamic-slice_fusion), channel_id=1, source_target_pairs={{0,16},{8,24},{16,0},{24,8},{1,17},{9,25},{17,1},{25,9},{2,18},{10... | collective-permute-start | bytes 49160 | tf_op jit(solution)/shard_map/ppermute | solution.py:27
  36.5 1.0 %assemble.1 = f32[16,4,16,256]{3,2,1,0:T(8,128)} custom-call(f32[16,4,2,8,128]{4,3,2,1,0:T(8,128)S(1)} %get-tuple-element.20.body_ref, f32[8,4,2,8,128]{4,3,2,1,0:T(8,128)S(1)} %get-tuple-element.25.refs_0_, f32[8,4,2,8,128]{4,3,2,1,0:T(8,128)S(1)} %get-tuple-element.28.refs_1_), custom_call_target="tpu_custom_call" | custom-call | tf_op jit(solution)/shard_map/assemble/pallas_call | solution.py:394
  37.6 1.0 %collective-permute-done.8 = f32[4,1,4,256]{3,2,0,1:T(4,128)S(1)} collective-permute-done((f32[4,1,4,256]{3,2,0,1:T(4,128)S(1)}, f32[4,1,4,256]{3,2,0,1:T(4,128)S(1)}, u32[]{:S(2)}, u32[]{:S(2)}) %collective-permute-start.8) | collective-permute-done | bytes 16416 | tf_op jit(solution)/shard_map/ppermute | solution.py:27
  38.6 0.6 %add_bitcast_fusion = f32[1,4,4,256]{3,2,1,0:T(4,128)} fusion(f32[4,1,4,256]{3,2,0,1:T(4,128)S(1)} %collective-permute-done.8, f32[4,2,4,256]{3,2,0,1:T(4,128)S(1)} %bitcast_add_fusion, s32[]{:T(128)S(6)} %select_n.40), kind=kLoop, calls=%fused_computation.2 | loop fusion | flops 4096 | bytes 49156 | tf_op jit(solution)/shard_map/reshape | solution.py:496
  39.2 0.0 copy-done
  (9 shorter events, 0.1 us)
Async XLA Ops:
  2.1 15.4 %collective-permute-start = (f32[6,4,8,256]{3,2,1,0:T(8,128)S(1)}, f32[6,4,8,256]{3,2,1,0:T(8,128)S(1)}, u32[]{:S(2)}, u32[]{:S(2)}) collective-permute-start(f32[6,4,8,256]{3,2,1,0:T(8,128)S(1)} %get-tuple-element.21), channel_id=1, source_target_pairs={{0,1},{1,0},{2,3},{3,2},{4,5},{5,4},{6,7},{7,6},{8,9},{9,8},{10,11... | collective-permute-start | bytes 589832 | tf_op jit(solution)/shard_map/ppermute | solution.py:435
  5.1 12.3 %collective-permute-start.1 = (f32[6,4,8,256]{3,2,1,0:T(8,128)S(1)}, f32[6,4,8,256]{3,2,1,0:T(8,128)S(1)}, u32[]{:S(2)}, u32[]{:S(2)}) collective-permute-start(f32[6,4,8,256]{3,2,1,0:T(8,128)S(1)} %get-tuple-element.22), channel_id=1, source_target_pairs={{0,7},{1,2},{2,1},{3,4},{4,3},{5,6},{6,5},{7,0},{8,15},{9,10},{10,... | collective-permute-start | bytes 589832 | tf_op jit(solution)/shard_map/ppermute | solution.py:435
  8.7 11.2 %collective-permute-start.2 = (f32[4,4,8,256]{3,2,1,0:T(8,128)S(1)}, f32[4,4,8,256]{3,2,1,0:T(8,128)S(1)}, u32[]{:S(2)}, u32[]{:S(2)}) collective-permute-start(f32[4,4,8,256]{3,2,1,0:T(8,128)S(1)} %get-tuple-element.26), channel_id=1, source_target_pairs={{0,1},{1,0},{2,3},{3,2},{4,5},{5,4},{6,7},{7,6},{8,9},{9,8},{10,11... | collective-permute-start | bytes 393224 | tf_op jit(solution)/shard_map/ppermute | solution.py:435
  8.7 11.2 %collective-permute-start.3 = (f32[4,4,8,256]{3,2,1,0:T(8,128)S(1)}, f32[4,4,8,256]{3,2,1,0:T(8,128)S(1)}, u32[]{:S(2)}, u32[]{:S(2)}) collective-permute-start(f32[4,4,8,256]{3,2,1,0:T(8,128)S(1)} %get-tuple-element.27), channel_id=1, source_target_pairs={{0,7},{1,2},{2,1},{3,4},{4,3},{5,6},{6,5},{7,0},{8,15},{9,10},{10,... | collective-permute-start | bytes 393224 | tf_op jit(solution)/shard_map/ppermute | solution.py:435
  19.1 14.1 %copy-start.1 = (f32[2,8]{1,0:T(2,128)S(1)}, f32[2,8]{1,0:T(2,128)}, u32[]{:S(2)}) copy-start(f32[2,8]{1,0:T(2,128)} %occ_ref.1) | copy-start | bytes 196
  21.3 3.7 %collective-permute-start.4 = (f32[2,8,8]{2,1,0:T(8,128)S(1)}, f32[2,8,8]{2,1,0:T(8,128)S(1)}, u32[]{:S(2)}, u32[]{:S(2)}) collective-permute-start(f32[2,8,8]{2,1,0:T(8,128)S(1)} %maximum_multiply_fusion), channel_id=1, source_target_pairs={{0,1},{1,0},{2,3},{3,2},{4,5},{5,4},{6,7},{7,6},{8,9},{9,8},{10,11... | collective-permute-start | bytes 1544 | tf_op jit(solution)/shard_map/ppermute | solution.py:27
  25.0 3.7 %collective-permute-start.5 = (f32[2,8,8]{2,1,0:T(8,128)S(1)}, f32[2,8,8]{2,1,0:T(8,128)S(1)}, u32[]{:S(2)}, u32[]{:S(2)}) collective-permute-start(f32[2,8,8]{2,1,0:T(8,128)S(1)} %fusion), channel_id=1, source_target_pairs={{0,2},{1,3},{2,0},{3,1},{4,6},{5,7},{6,4},{7,5},{8,10},{9,11},{10,... | collective-permute-start | bytes 1544 | tf_op jit(solution)/shard_map/ppermute | solution.py:27
  28.7 4.5 %collective-permute-start.6 = (f32[2,8,8]{2,1,0:T(8,128)S(1)}, f32[2,8,8]{2,1,0:T(8,128)S(1)}, u32[]{:S(2)}, u32[]{:S(2)}) collective-permute-start(f32[2,8,8]{2,1,0:T(8,128)S(1)} %fusion.1), channel_id=1, source_target_pairs={{0,4},{1,5},{2,6},{3,7},{4,0},{5,1},{6,2},{7,3},{8,12},{9,13},{10,... | collective-permute-start | bytes 1544 | tf_op jit(solution)/shard_map/ppermute | solution.py:27
  33.2 6.0 %copy-start = (f32[2,8,8]{2,1,0:T(8,128)}, f32[2,8,8]{2,1,0:T(8,128)S(1)}, u32[]{:S(2)}) copy-start(f32[2,8,8]{2,1,0:T(8,128)S(1)} %add.46.gram_ref) | copy-start | bytes 1540
  33.5 1.3 %collective-permute-start.7 = (f32[4,2,4,256]{3,2,0,1:T(4,128)S(1)}, f32[4,2,4,256]{3,2,0,1:T(4,128)S(1)}, u32[]{:S(2)}, u32[]{:S(2)}) collective-permute-start(f32[4,2,4,256]{3,2,0,1:T(4,128)S(1)} %bitcast.26), channel_id=1, source_target_pairs={{0,8},{8,0},{16,24},{24,16},{1,9},{9,1},{17,25},{25,17},{2,10},{10... | collective-permute-start | bytes 98312 | tf_op jit(solution)/shard_map/ppermute | solution.py:27
  34.8 3.8 %collective-permute-start.8 = (f32[4,1,4,256]{3,2,0,1:T(4,128)S(1)}, f32[4,1,4,256]{3,2,0,1:T(4,128)S(1)}, u32[]{:S(2)}, u32[]{:S(2)}) collective-permute-start(f32[4,1,4,256]{3,2,0,1:T(4,128)S(1)} %constant_dynamic-slice_fusion), channel_id=1, source_target_pairs={{0,16},{8,24},{16,0},{24,8},{1,17},{9,25},{17,1},{25,9},{2,18},{10... | collective-permute-start | bytes 49160 | tf_op jit(solution)/shard_map/ppermute | solution.py:27

commit v3 on v2

v3 whole, which is shorter than its diff:
```python
import functools

import jax
import jax.numpy as jnp
from jax import lax
from jax.experimental import pallas as pl
from jax.experimental.pallas import tpu as pltpu
from jax.sharding import PartitionSpec as P


DEGREE = 4

CENTRE = 6.0
HALF_WIDTH = 4.0
EPSILON = 1e-06
SUB = 8
LANES = 128


def shifted(value, axis, steps):
    count = lax.axis_size(axis)
    pairs = [(source, (source + steps) % count) for source in range(count)]
    return lax.ppermute(value, axis, pairs)


def swapped(value, axis, bit):
    count = lax.axis_size(axis)
    return lax.ppermute(value, axis, [(i, i ^ bit) for i in range(count)])


def cut(h):
    return slice(LANES * h, LANES * (h + 1))


def iotas():
    return tuple(lax.broadcasted_iota(jnp.int32, (SUB, LANES), axis) for axis in range(2))


def ahead(line, lane):
    turned = [pltpu.roll(block, LANES - 1, 1) for block in line]
    return [jnp.where(lane == LANES - 1, turned[(h + 1) % len(line)], turned[h]) for h in range(len(line))]


def behind(line, lane):
    turned = [pltpu.roll(block, 1, 1) for block in line]
    return [jnp.where(lane == 0, turned[h - 1], turned[h]) for h in range(len(line))]


def pack_kernel(blocks, odd_ref, pot_any, kin_any, orb_any, *refs):
    a_refs, b_ref = refs[:blocks], refs[blocks]
    pot_ref, kin_ref, orb_ref, arrivals = refs[blocks + 1 :]
    count, rows_x, rows_y, depth = orb_ref.shape
    odd = odd_ref[0] == 1
    row, _ = iotas()
    upper = row < DEGREE
    size = count // blocks
    loads = [pltpu.make_async_copy(pot_any, pot_ref, arrivals.at[0]), pltpu.make_async_copy(kin_any, kin_ref, arrivals.at[1])]
    for k in range(blocks):
        part = pl.ds(k * size, size)
        loads.append(pltpu.make_async_copy(orb_any.at[part], orb_ref.at[part], arrivals.at[2 + k]))
    for load in loads:
        load.start()

    def edges(one, two, x, h):
        tail = slice(rows_y - SUB, rows_y)
        first = jnp.where(upper, one[x, 0:SUB, cut(h)], pltpu.roll(two[x, 0:SUB, cut(h)], DEGREE, 0))
        last = jnp.where(upper, pltpu.roll(one[x, tail, cut(h)], DEGREE, 0), two[x, tail, cut(h)])
        return jnp.where(odd, first, last), jnp.where(odd, last, first)

    places = [(x, h) for x in range(rows_x) for h in range(depth // LANES)]
    loads[0].wait()
    loads[1].wait()
    for x, h in places:
        low_a, low_b = edges(pot_ref, kin_ref.at[0], x, h)
        high_a, high_b = edges(kin_ref.at[1], kin_ref.at[2], x, h)
        a_refs[0][0, x, :, cut(h)] = low_a
        a_refs[0][1, x, :, cut(h)] = high_a
        b_ref[0, x, :, cut(h)] = low_b
        b_ref[1, x, :, cut(h)] = high_b
    for k in range(blocks):
        loads[2 + k].wait()
        for p in range(size // 2):
            m = k * size + 2 * p
            for x, h in places:
                a, b = edges(orb_ref.at[m], orb_ref.at[m + 1], x, h)
                a_refs[k][(0 if k else 2) + p, x, :, cut(h)] = a
                b_ref[2 + m // 2, x, :, cut(h)] = b


def ring_tiles(ref, index, parts):
    return [
        [ref[index + (h, pl.ds(t, SUB, stride=parts), slice(None))] for h in range(ref.shape[-3])]
        for t in range(parts)
    ]


def own_coefficients(pot_ref, kin_ref, coef_ref, ring, lane):
    rows_x, rows_y, depth = pot_ref.shape
    parts = rows_y // SUB
    unit = 1.0 / HALF_WIDTH
    for x in range(rows_x):
        for c in range(4):
            own_ref = pot_ref if c == 0 else kin_ref.at[c - 1]
            for h in range(depth // LANES):
                ring[c, x, h] = own_ref[x, :, cut(h)]
    for x in range(rows_x):
        before = (x - 1) % rows_x
        pot = ring_tiles(ring, (0, x), parts)
        kx = ring_tiles(ring, (1, x), parts)
        kxm = ring_tiles(ring, (1, before), parts)
        ky = ring_tiles(ring, (2, x), parts)
        kz = ring_tiles(ring, (3, x), parts)
        for t in range(parts):
            kzm = behind(kz[t], lane)
            for h in range(depth // LANES):
                kym = ky[t - 1][h] if t > 0 else pltpu.roll(ky[parts - 1][h], 1, 0)
                total = kx[t][h] + kxm[t][h] + ky[t][h] + kym + kz[t][h] + kzm[h]
                coef_ref[0, x, t, h] = unit * total + (2.0 * unit) * (pot[t][h] - CENTRE)
                coef_ref[1, x, t, h] = unit * kx[t][h]
                coef_ref[2, x, t, h] = unit * ky[t][h]
                coef_ref[3, x, t, h] = unit * kz[t][h]
                coef_ref[4, x, t, h] = unit * kzm[h]
                if t == 0:
                    coef_ref[5, x, 0, h] = unit * kym


def apply_own(coef_ref, v, x, t, lane):
    rows_x, parts = len(v), len(v[0])
    up_x, down_x = (x + 1) % rows_x, (x - 1) % rows_x
    own = v[x][t]
    front, back = ahead(own, lane), behind(own, lane)
    result = []
    for h in range(len(own)):
        total = coef_ref[0, x, t, h] * own[h]
        total = total - coef_ref[1, x, t, h] * v[up_x][t][h]
        total = total - coef_ref[1, down_x, t, h] * v[down_x][t][h]
        above = v[x][t + 1][h] if t < parts - 1 else pltpu.roll(v[x][0][h], SUB - 1, 0)
        total = total - coef_ref[2, x, t, h] * above
        if t > 0:
            total = total - coef_ref[2, x, t - 1, h] * v[x][t - 1][h]
        else:
            total = total - coef_ref[5, x, 0, h] * pltpu.roll(v[x][parts - 1][h], 1, 0)
        total = total - coef_ref[3, x, t, h] * front[h]
        result.append(total - coef_ref[4, x, t, h] * back[h])
    return result


def pairs_of(members):
    return [(a, b) for a in range(members) for b in range(a, members)]


def interior_kernel(k, pot_ref, kin_ref, orb_ref, body_ref, seam_ref, sums_ref, coef_ref, coef_ring, ring):
    members, rows_x, blocks_z = body_ref.shape[:3]
    rows_y = orb_ref.shape[2]
    parts = rows_y // SUB
    row, lane = iotas()
    upper = row < DEGREE
    own_coefficients(pot_ref, kin_ref, coef_ref, coef_ring, lane)
    for m in range(members):
        pair, half = m // 2, m % 2
        for x in range(rows_x):
            for h in range(blocks_z):
                ring[half, x, h] = orb_ref[k * members + m, x, :, cut(h)]
        v = [ring_tiles(ring.at[half], (x,), parts) for x in range(rows_x)]
        previous = None
        for step in range(DEGREE):
            for x in range(rows_x):
                for h in range(blocks_z):
                    for side in range(2):
                        for depth_in in range(2):
                            y = step + depth_in if side == 0 else rows_y - 1 - step - depth_in
                            place = DEGREE * half + (DEGREE - 1 if side == 0 else 0)
                            value = v[x][y % parts][h][y // parts : y // parts + 1]
                            seam_ref[side, pair, step, depth_in, x, h, place : place + 1, :] = value
            fresh = []
            for x in range(rows_x):
                rows = []
                for t in range(parts):
                    image = apply_own(coef_ref, v, x, t, lane)
                    if step == 0:
                        rows.append([0.5 * i for i in image])
                    else:
                        rows.append([i - p for i, p in zip(image, previous[x][t])])
                fresh.append(rows)
            previous, v = v, fresh
        for x in range(rows_x):
            for t in range(parts):
                for h in range(blocks_z):
                    ring[half, x, h, pl.ds(t, SUB, stride=parts), :] = v[x][t][h]
        for x in range(rows_x):
            for h in range(blocks_z):
                body_ref[m, x, h] = jnp.where(upper, ring[half, x, h, rows_y - SUB :], ring[half, x, h, 0:SUB])
    pairs = pairs_of(members)
    sums = [jnp.zeros((SUB, LANES), jnp.float32) for _ in pairs]
    for x in range(rows_x):
        for h in range(blocks_z):
            f = [body_ref[a, x, h] for a in range(members)]
            for i, (a, b) in enumerate(pairs):
                sums[i] = sums[i] + f[a] * f[b]
    for i, value in enumerate(sums):
        sums_ref[i] = value


def windows_kernel(second, odd_ref, pot_ref, kin_ref, halo_ref, coef_ref):
    rows_x, rows_y, depth = pot_ref.shape
    side = odd_ref[0] if second else 1 - odd_ref[0]
    top = side == 0
    row, lane = iotas()
    upper = row < DEGREE
    blocks_z = depth // LANES
    unit = 1.0 / HALF_WIDTH

    def window(tile, start):
        low = pltpu.roll(tile, lax.rem(SUB - start, SUB), 0)
        high = pltpu.roll(tile, lax.rem(SUB + DEGREE - start, SUB), 0)
        return jnp.where(upper, low, high)

    def field(c, x, h):
        own_ref = pot_ref if c == 0 else kin_ref.at[c - 1]
        halo = halo_ref[c // 2, x, :, cut(h)]
        head, tail = own_ref[x, 0:SUB, cut(h)], own_ref[x, rows_y - SUB :, cut(h)]
        before = pltpu.roll(halo, DEGREE, 0) if c % 2 else halo
        after = pltpu.roll(halo, 1 if c % 2 else DEGREE + 1, 0)
        above = jnp.where(upper, before, pltpu.roll(head, DEGREE, 0))
        below = jnp.where(row < DEGREE + 1, pltpu.roll(tail, DEGREE + 1, 0), after)
        return jnp.where(top, above, below)

    tiles = [[[field(c, x, h) for h in range(blocks_z)] for x in range(rows_x)] for c in range(4)]
    for step in range(DEGREE):
        start = jnp.where(top, step + 1, DEGREE - step)
        kx = [[window(tiles[1][x][h], start) for h in range(blocks_z)] for x in range(rows_x)]
        for x in range(rows_x):
            kz = [window(tiles[3][x][h], start) for h in range(blocks_z)]
            kzm = behind(kz, lane)
            for h in range(blocks_z):
                pot = window(tiles[0][x][h], start)
                ky = window(tiles[2][x][h], start)
                kym = window(tiles[2][x][h], start - 1)
                total = kx[x][h] + kx[(x - 1) % rows_x][h] + ky + kym + kz[h] + kzm[h]
                coef_ref[step, 0, x, h] = unit * total + (2.0 * unit) * (pot - CENTRE)
                coef_ref[step, 1, x, h] = unit * kx[x][h]
                coef_ref[step, 2, x, h] = unit * jnp.where(top, ky, kym)
                coef_ref[step, 3, x, h] = unit * jnp.where(top, kym, ky)
                coef_ref[step, 4, x, h] = unit * kz[h]
                coef_ref[step, 5, x, h] = unit * kzm[h]


def run_side(side, pair, w, seam_ref, coef_ref, lane, mark):
    rows_x, blocks_z = len(w), len(w[0])
    turn = jnp.where(side == 0, SUB - 1, 1)
    last = None
    for step in range(DEGREE):
        seam = seam_ref.at[side, pair, step]
        coef = coef_ref.at[step]
        centre, inner = [], []
        for x in range(rows_x):
            centre.append([jnp.where(mark, seam[0, x, h], pltpu.roll(w[x][h], turn, 0)) for h in range(blocks_z)])
            inner.append([jnp.where(mark, seam[1, x, h], pltpu.roll(centre[x][h], turn, 0)) for h in range(blocks_z)])
        fresh = []
        for x in range(rows_x):
            up_x, down_x = (x + 1) % rows_x, (x - 1) % rows_x
            front, back = ahead(centre[x], lane), behind(centre[x], lane)
            line = []
            for h in range(blocks_z):
                total = coef[0, x, h] * centre[x][h]
                total = total - coef[1, x, h] * centre[up_x][h]
                total = total - coef[1, down_x, h] * centre[down_x][h]
                total = total - coef[2, x, h] * inner[x][h]
                total = total - coef[3, x, h] * w[x][h]
                total = total - coef[4, x, h] * front[h]
                total = total - coef[5, x, h] * back[h]
                line.append(0.5 * total if step == 0 else total - last[x][h])
            fresh.append(line)
        last, w = inner, fresh
    return w


def edge_kernel(start, odd_ref, halo_ref, coef_ref, seam_ref, edge_ref):
    pairs, rows_x, blocks_z = edge_ref.shape[:3]
    row, lane = iotas()
    side = odd_ref[0]
    mark = row % DEGREE == jnp.where(side == 0, DEGREE - 1, 0)
    for pair in range(pairs):
        w = [[halo_ref[start + pair, x, :, cut(h)] for h in range(blocks_z)] for x in range(rows_x)]
        w = run_side(side, pair, w, seam_ref, coef_ref, lane, mark)
        for x in range(rows_x):
            for h in range(blocks_z):
                edge_ref[pair, x, h] = w[x][h]


def merge(first, second, place, odd, upper, edge_ref):
    for x in range(len(first)):
        for h in range(len(first[x])):
            a, b = first[x][h], second[x][h]
            top, bottom = jnp.where(odd, a, b), jnp.where(odd, b, a)
            edge_ref[place, x, h] = jnp.where(upper, top, pltpu.roll(bottom, DEGREE, 0))
            edge_ref[place + 1, x, h] = jnp.where(upper, pltpu.roll(top, DEGREE, 0), bottom)


def finish_kernel(start, odd_ref, halo_ref, coef_ref, seam_ref, sums_ref, second_ref, edge_ref, gram_ref):
    members, rows_x, blocks_z = edge_ref.shape[:3]
    row, lane = iotas()
    upper = row < DEGREE
    odd, side = odd_ref[0] == 1, 1 - odd_ref[0]
    mark = row % DEGREE == jnp.where(side == 0, DEGREE - 1, 0)
    for pair in range(members // 2):
        w = [[halo_ref[start + pair, x, :, cut(h)] for h in range(blocks_z)] for x in range(rows_x)]
        w = run_side(side, pair, w, seam_ref, coef_ref, lane, mark)
        second = [[second_ref[pair, x, h] for h in range(blocks_z)] for x in range(rows_x)]
        merge(w, second, 2 * pair, odd, upper, edge_ref)
    pairs = pairs_of(members)
    sums = [sums_ref[i] for i in range(len(pairs))]
    for x in range(rows_x):
        for h in range(blocks_z):
            f = [edge_ref[a, x, h] for a in range(members)]
            for i, (a, b) in enumerate(pairs):
                sums[i] = sums[i] + f[a] * f[b]
    at = {pair: jnp.sum(s, axis=0, keepdims=True) for pair, s in zip(pairs, sums)}
    column_of = lax.broadcasted_iota(jnp.int32, (members, members), 1)
    gram = jnp.zeros((members, members), jnp.float32)
    for a in range(members):
        column = jnp.concatenate([at[min(a, b), max(a, b)] for b in range(members)], 0)
        gram = jnp.where(column_of == a, jnp.sum(column, axis=1, keepdims=True), gram)
    gram_ref[...] = gram


def assemble_kernel(*refs):
    out_ref = refs[-1]
    rows_x, rows_y, depth = out_ref.shape[1:]
    row, _ = iotas()
    upper = row < DEGREE
    i = 0
    for body_ref, edge_ref in zip(refs[:-1:2], refs[1:-1:2]):
        for a in range(edge_ref.shape[0]):
            for x in range(rows_x):
                for h in range(depth // LANES):
                    body, edge = body_ref[a, x, h], edge_ref[a, x, h]
                    out_ref[i, x, 0:SUB, cut(h)] = jnp.where(upper, edge, body)
                    out_ref[i, x, rows_y - SUB :, cut(h)] = jnp.where(upper, body, edge)
            i += 1


def density_kernel(gram_ref, occ_ref, *refs):
    body_refs, edge_refs, out_ref = refs[:-1:2], refs[1:-1:2], refs[-1]
    rows_x, rows_y, depth = out_ref.shape
    blocks, members, _ = gram_ref.shape
    row, _ = iotas()
    upper = row < DEGREE
    down = lax.broadcasted_iota(jnp.int32, (members, members), 0)
    along = lax.broadcasted_iota(jnp.int32, (members, members), 1)
    w = []
    for k in range(blocks):
        ratio = jnp.broadcast_to(occ_ref[k : k + 1, :], (members, members)) / (gram_ref[k] + EPSILON)
        column = jnp.sum(jnp.where(down == along, ratio, 0.0), axis=1, keepdims=True)
        w += [jnp.broadcast_to(column[a : a + 1, :], (SUB, LANES)) for a in range(members)]
    for x in range(rows_x):
        for h in range(depth // LANES):
            body = edge = None
            for i in range(blocks * members):
                k, a = divmod(i, members)
                f, g = body_refs[k][a, x, h], edge_refs[k][a, x, h]
                f, g = w[i] * (f * f), w[i] * (g * g)
                body, edge = (f, g) if body is None else (body + f, edge + g)
            out_ref[x, 0:SUB, cut(h)] = jnp.where(upper, edge, body)
            out_ref[x, rows_y - SUB :, cut(h)] = jnp.where(upper, body, edge)


def vmem():
    return pl.BlockSpec(memory_space=pltpu.VMEM)


def smem():
    return pl.BlockSpec(memory_space=pltpu.SMEM)


def anywhere():
    return pl.BlockSpec(memory_space=pltpu.HBM)


def call(kernel, operands, outs, scratch=(), specs=None, place=jax.ShapeDtypeStruct, limit=8):
    shapes = tuple(place(shape, jnp.float32) for shape in outs)
    return pl.pallas_call(
        kernel,
        out_shape=shapes,
        in_specs=[vmem() for _ in operands] if specs is None else specs,
        out_specs=tuple(vmem() for _ in outs),
        scratch_shapes=[pltpu.VMEM(shape, jnp.float32) if isinstance(shape, tuple) else shape for shape in scratch],
        compiler_params=pltpu.CompilerParams(vmem_limit_bytes=limit * 1024 * 1024),
    )(*operands)


def fast_body(orbitals, potential, kinetic, occupations):
    blocks, members, _, rows_x, rows_y, depth = orbitals.shape
    count = blocks * members
    domains = lax.axis_size("grid")
    position = lax.axis_index("grid")
    parts = rows_y // SUB
    blocks_z = depth // LANES
    tile = (SUB, LANES)
    band = lax.axis_index("band")
    bands = lax.axis_size("band")
    odd = lax.rem(position, 2).astype(jnp.int32).reshape(1)

    pairs_a = [(i, i ^ 1) for i in range(domains)]
    pairs_b = [(i, (i + 1) % domains if i % 2 else (i - 1) % domains) for i in range(domains)]
    half = members // 2
    *halos, pot, kin, fields = call(
        functools.partial(pack_kernel, blocks),
        (
            odd,
            pltpu.with_memory_space_constraint(potential[0], pltpu.HBM),
            pltpu.with_memory_space_constraint(kinetic[:, 0], pltpu.HBM),
            pltpu.with_memory_space_constraint(orbitals.reshape(count, rows_x, rows_y, depth), pltpu.HBM),
        ),
        [(size, rows_x, SUB, depth) for size in [2 + half] + [half] * (blocks - 1) + [2 + count // 2]]
        + [(rows_x, rows_y, depth), (3, rows_x, rows_y, depth), (count, rows_x, rows_y, depth)],
        [pltpu.SemaphoreType.DMA((2 + blocks,))],
        specs=[smem()] + [anywhere()] * 3,
        place=pltpu.VMEM,
    )
    halos_a = []
    for k in range(blocks):
        halos_a.append(lax.ppermute(halos[k], "grid", pairs_a))
    halo_b = lax.ppermute(halos[blocks], "grid", pairs_b)

    inner = [
        call(
            functools.partial(interior_kernel, k),
            (pot, kin, fields),
            [
                (members, rows_x, blocks_z) + tile,
                (2, half, DEGREE, 2, rows_x, blocks_z) + tile,
                (len(pairs_of(members)),) + tile,
            ],
            [
                (6, rows_x, parts, blocks_z) + tile,
                (4, rows_x, blocks_z, rows_y, LANES),
                (2, rows_x, blocks_z, rows_y, LANES),
            ],
        )
        for k in range(blocks)
    ]
    coef_shape = (DEGREE, 6, rows_x, blocks_z) + tile
    (coef_a,) = call(
        functools.partial(windows_kernel, 0), (odd, pot, kin, halos_a[0]), [coef_shape], specs=[smem()] + [vmem()] * 3
    )
    (coef_b,) = call(
        functools.partial(windows_kernel, 1), (odd, pot, kin, halo_b), [coef_shape], specs=[smem()] + [vmem()] * 3
    )
    rows, grams = [], []
    for k in range(blocks):
        body, seam, sums = inner[k]
        (second,) = call(
            functools.partial(edge_kernel, 2 + k * half),
            (odd, halo_b, coef_b, seam),
            [(half, rows_x, blocks_z) + tile],
            specs=[smem()] + [vmem()] * 3,
        )
        edge, gram = call(
            functools.partial(finish_kernel, 0 if k else 2),
            (odd, halos_a[k], coef_a, seam, sums, second),
            [(members, rows_x, blocks_z) + tile, (members, members)],
            specs=[smem()] + [vmem()] * 5,
        )
        rows += [body, edge]
        grams.append(gram)
    gram = jnp.stack(grams)

    cells = rows_x * rows_y * depth * domains
    gram = gram * (1.0 / cells)
    bit = 1
    while bit < domains:
        gram = gram + swapped(gram, "grid", bit)
        bit *= 2

    (filtered,) = call(assemble_kernel, rows, [fields.shape])
    (partial_value,) = call(density_kernel, (gram, occupations, *rows), [pot.shape])

    share = rows_y // bands
    value = partial_value.reshape(rows_x, bands, share, depth)
    bit = 1
    width = bands
    while bit < bands:
        value = value.reshape(rows_x, width // 2, 2, share, depth)
        mine = (band // bit) % 2
        keep = lax.dynamic_index_in_dim(value, mine, 2, False)
        send = lax.dynamic_index_in_dim(value, 1 - mine, 2, False)
        value = keep + swapped(send, "band", bit)
        bit *= 2
        width //= 2
    density = value.reshape(1, rows_x, share, depth)
    return filtered.reshape(orbitals.shape), gram, density


def extend(field, width, across):
    lower = shifted(field[..., -width:, :, :], "grid", across)
    upper = shifted(field[..., :width, :, :], "grid", -across)
    widened = jnp.concatenate([lower, field, upper], -3)
    column = lax.axis_index("grid") % across
    left_plain = shifted(widened[..., :, -width:, :], "grid", 1)
    left_wrap = shifted(widened[..., :, -width:, :], "grid", -(across - 1))
    left = jnp.where(column == 0, left_wrap, left_plain)
    right_plain = shifted(widened[..., :, :width, :], "grid", -1)
    right_wrap = shifted(widened[..., :, :width, :], "grid", across - 1)
    right = jnp.where(column == across - 1, right_wrap, right_plain)
    return jnp.concatenate([left, widened, right], -2)


def hamilton(field, coeffs):
    inner = field[..., 1:-1, 1:-1, :]
    kin_x = coeffs[1]
    total = kin_x[1:-1, 1:-1] * (inner - field[..., 2:, 1:-1, :])
    total = total + kin_x[:-2, 1:-1] * (inner - field[..., :-2, 1:-1, :])
    kin_y = coeffs[2]
    total = total + kin_y[1:-1, 1:-1] * (inner - field[..., 1:-1, 2:, :])
    total = total + kin_y[1:-1, :-2] * (inner - field[..., 1:-1, :-2, :])
    kin_z = coeffs[3, 1:-1, 1:-1]
    total = total + kin_z * (inner - jnp.roll(inner, -1, -1))
    total = total + jnp.roll(kin_z, 1, -1) * (inner - jnp.roll(inner, 1, -1))
    return 0.5 * total + coeffs[0, 1:-1, 1:-1] * inner


def general_body(across, orbitals, potential, kinetic, occupations):
    blocks = orbitals.shape[0]
    members = orbitals.shape[1]
    rows_x = orbitals.shape[3]
    rows_y = orbitals.shape[4]
    coeffs = jnp.concatenate([potential, kinetic[:, 0]], 0)
    current = orbitals[:, :, 0]
    previous = current
    coeff_ext = None
    for degree_step in range(DEGREE):
        if degree_step == 0:
            stacked = jnp.concatenate(
                [coeffs, current.reshape((blocks * members,) + current.shape[2:])], 0
            )
            wide = extend(stacked, 1, across)
            coeff_ext = wide[:4]
            extended = wide[4:].reshape((blocks, members) + wide.shape[1:])
        else:
            extended = extend(current, 1, across)
        image = hamilton(extended, coeff_ext)
        inner = extended[..., 1:-1, 1:-1, :]
        if degree_step == 0:
            fresh = (image - CENTRE * inner) / HALF_WIDTH
        else:
            fresh = 2.0 / HALF_WIDTH * (image - CENTRE * inner) - previous
        previous = current
        current = fresh
    cells = rows_x * rows_y * orbitals.shape[5] * lax.axis_size("grid")
    flat = current.reshape(blocks, members, -1)
    local_gram = jnp.einsum("kbx,kcx->kbc", flat, flat, precision=lax.Precision.HIGHEST) / cells
    gram = lax.psum(local_gram, "grid")
    diagonal = jnp.diagonal(gram, axis1=1, axis2=2)
    weight = occupations / (diagonal + EPSILON)
    partial_value = jnp.einsum(
        "kb,kbxyz->xyz", weight, current * current, precision=lax.Precision.HIGHEST
    )
    density = lax.psum_scatter(partial_value[None], "band", scatter_dimension=2, tiled=True)
    return (current[:, :, None], gram, density)


def solution(mesh):
    domains = mesh.shape["grid"]
    across = min(domains, 8)
    even = all(size > 1 and size & (size - 1) == 0 for size in mesh.shape.values())
    fast = domains == across and even
    whole = fast_body if fast else functools.partial(general_body, across)

    placed = (
        P("band", None, "grid", None, None, None),
        P("grid", None, None, None),
        P(None, "grid", None, None, None),
        P("band", None),
    )
    return jax.shard_map(
        whole,
        mesh=mesh,
        in_specs=placed,
        out_specs=(
            P("band", None, "grid", None, None, None),
            P("band", None, None),
            P("grid", None, "band", None),
        ),
        check_vma=False,
    )
```

time: 39.3 us -> 41.5 us (1.056)
  waiting for transfers between devices: 11.5 us -> 20.3 us
  starting transfers between devices: 16.9 us -> 10.5 us
    ppermute x5, starting transfers between devices: 8.38 us -> 2.37 us  [swapped(): return lax.ppermute(value, axis, [(i, i ^ bit) for i in range(count)])]
    ppermute x5, waiting for transfers between devices: 7.53 us -> 13.5 us  [swapped(): return lax.ppermute(value, axis, [(i, i ^ bit) for i in range(count)])]
    ppermute x4 -> x3, waiting for transfers between devices: 3.94 us -> 6.75 us  [the longest x2 6.74 us: fast_body(): halos_a.append(lax.ppermute(halos[k], 'grid', pairs_a))]
    ppermute x4 -> x3, starting transfers between devices: 8.52 us -> 8.12 us  [the longest x1 6.1 us: fast_body(): halo_b = lax.ppermute(halos[blocks], 'grid', pairs_b)]
    pallas_call x7 -> x11, Pallas kernels: 9.33 us -> 9.12 us  [call(): pl.pallas_call(kernel, out_shape=shapes, in_specs=[vmem() for _ in operan...]
  transfers between devices with their start and end apart: 9 -> 8, of which waited for: 7 -> 7; matrix products, arithmetic and copies ran while one was open for 0% -> 0% of each run, Pallas kernels for 16% -> 17%
where the time goes in v3:
time: 41.5 us; the launch traced here: 41.4 us
  waiting for transfers between devices  20.3 us (49%)
  starting transfers between devices  10.5 us (25%)
  Pallas kernels  9.12 us (22%)
  between operations  0.81 us (2%)
  other arithmetic  0.66 us (2%)
    ppermute x5, waiting for transfers between devices, swapped(): return lax.ppermute(value, axis, [(i, i ^ bit) for i in range(count)])  13.5 us
    pallas_call x11, Pallas kernels, call(): pl.pallas_call(kernel, out_shape=shapes, in_specs=[vmem() for _ in operan...  9.12 us
    ppermute x2, waiting for transfers between devices, fast_body(): halos_a.append(lax.ppermute(halos[k], 'grid', pairs_a))  6.74 us
    ppermute x1, starting transfers between devices, fast_body(): halo_b = lax.ppermute(halos[blocks], 'grid', pairs_b)  6.1 us
    ppermute x5, starting transfers between devices, swapped(): return lax.ppermute(value, axis, [(i, i ^ bit) for i in range(count)])  2.37 us
    ppermute x2, starting transfers between devices, fast_body(): halos_a.append(lax.ppermute(halos[k], 'grid', pairs_a))  2.03 us
  transfers between devices with their start and end apart: 8, of which 7 were waited for; matrix products, arithmetic and copies ran while one was open for 0% of the time, Pallas kernels for 17%

profile of v3, /device:TPU:0, one launch (start us, length us, event | category | flops | bytes accessed | tf_op | source)
XLA Modules:
  0.0 41.4 jit_solution(3441546640687126705)
XLA Ops:
  0.6 1.4 %shard_map.67 = (f32[6,4,8,256]{3,2,1,0:T(8,128)S(1)}, f32[4,4,8,256]{3,2,1,0:T(8,128)S(1)}, f32[10,4,8,256]{3,2,1,0:T(8,128)S(1)}, f32[4,16,256]{2,1,0:T(8,128)...) custom-call(s32[1]{0:T(128)} %bitcast.odd_ref, f32[4,16,256]{2,1,0:T(8,128)} %bitcast.25, ...), custom_call_target="tpu_custom_call" | custom-call | tf_op jit(solution)/shard_map/pallas_call | solution.py:382
  2.0 6.1 %collective-permute-start.1 = (f32[10,4,8,256]{3,2,1,0:T(8,128)S(1)}, f32[10,4,8,256]{3,2,1,0:T(8,128)S(1)}, u32[]{:S(2)}, u32[]{:S(2)}) collective-permute-start(f32[10,4,8,256]{3,2,1,0:T(8,128)S(1)} %get-tuple-element.26), channel_id=1, source_target_pairs={{0,7},{1,2},{2,1},{3,4},{4,3},{5,6},{6,5},{7,0},{8,15},{9,10},{10,... | collective-permute-start | bytes 983048 | tf_op jit(solution)/shard_map/ppermute | solution.py:424
  8.1 0.0 collective-permute-start
  8.2 2.0 %collective-permute-start.2 = (f32[4,4,8,256]{3,2,1,0:T(8,128)S(1)}, f32[4,4,8,256]{3,2,1,0:T(8,128)S(1)}, u32[]{:S(2)}, u32[]{:S(2)}) collective-permute-start(f32[4,4,8,256]{3,2,1,0:T(8,128)S(1)} %get-tuple-element.29), channel_id=1, source_target_pairs={{0,1},{1,0},{2,3},{3,2},{4,5},{5,4},{6,7},{7,6},{8,9},{9,8},{10,11... | collective-permute-start | bytes 393224 | tf_op jit(solution)/shard_map/ppermute | solution.py:423
  10.2 1.9 %shard_map.68 = (f32[8,4,2,8,128]{4,3,2,1,0:T(8,128)S(1)}, f32[2,4,4,2,4,2,8,128]{7,6,5,4,3,2,1,0:T(8,128)S(1)}, f32[36,8,128]{2,1,0:T(8,128)S(1)}) custom-call(f32[4,16,256]{2,1,0:T(8,128)S(1)} %get-tuple-element.19.pot_ref, f32[3,4,16,256]{3,2,1,0:T(8,128)S(1)} %get-tuple-element.20.kin_ref, f32[16,4,16,256]{3,2,1,0:T(8,128)S(1)} %get-tuple-element.21.orb_ref), custom_call_target="tpu_custom_call" | custom-call | tf_op jit(solution)/shard_map/pallas_call | solution.py:382
  12.1 1.9 %shard_map.73 = (f32[8,4,2,8,128]{4,3,2,1,0:T(8,128)S(1)}, f32[2,4,4,2,4,2,8,128]{7,6,5,4,3,2,1,0:T(8,128)S(1)}, f32[36,8,128]{2,1,0:T(8,128)S(1)}) custom-call(f32[4,16,256]{2,1,0:T(8,128)S(1)} %get-tuple-element.19.pot_ref, f32[3,4,16,256]{3,2,1,0:T(8,128)S(1)} %get-tuple-element.20.kin_ref, f32[16,4,16,256]{3,2,1,0:T(8,128)S(1)} %get-tuple-element.21.orb_ref), custom_call_target="tpu_custom_call" | custom-call | tf_op jit(solution)/shard_map/pallas_call | solution.py:382
  14.0 6.2 %collective-permute-done.halo_ref = f32[6,4,8,256]{3,2,1,0:T(8,128)S(1)} collective-permute-done((f32[6,4,8,256]{3,2,1,0:T(8,128)S(1)}, f32[6,4,8,256]{3,2,1,0:T(8,128)S(1)}, u32[]{:S(2)}, u32[]{:S(2)}) %collective-permute-start) | collective-permute-done | bytes 196640 | tf_op jit(solution)/shard_map/ppermute | solution.py:423
  20.2 0.2 shard_map.69.coef_ref
  20.4 0.0 collective-permute-done.1.halo_ref
  20.4 0.2 shard_map.70.coef_ref
  20.6 0.6 %shard_map.71.second_ref = f32[4,4,2,8,128]{4,3,2,1,0:T(8,128)S(1)} custom-call(s32[1]{0:T(128)} %bitcast.odd_ref, f32[10,4,8,256]{3,2,1,0:T(8,128)S(1)} %collective-permute-done.1.halo_ref, f32[4,6,4,2,8,128]{5,4,3,2,1,0:T(8,128)S(1)} %shard_map.70.coef_ref, f32[2,4,4,2,4,2,8,128]{7,6,5,4,3,2,1,0:T(8,128)S(1)} %get-tuple-element.24.seam_ref), custom_call_target="tpu_custom_call" | custom-call | tf_op jit(solution)/shard_map/pallas_call | solution.py:382
  21.1 0.6 %shard_map.74.second_ref = f32[4,4,2,8,128]{4,3,2,1,0:T(8,128)S(1)} custom-call(s32[1]{0:T(128)} %bitcast.odd_ref, f32[10,4,8,256]{3,2,1,0:T(8,128)S(1)} %collective-permute-done.1.halo_ref, f32[4,6,4,2,8,128]{5,4,3,2,1,0:T(8,128)S(1)} %shard_map.70.coef_ref, f32[2,4,4,2,4,2,8,128]{7,6,5,4,3,2,1,0:T(8,128)S(1)} %get-tuple-element.30.seam_ref), custom_call_target="tpu_custom_call" | custom-call | tf_op jit(solution)/shard_map/pallas_call | solution.py:382
  21.7 0.6 %shard_map.72 = (f32[8,4,2,8,128]{4,3,2,1,0:T(8,128)S(1)}, f32[8,8]{1,0:T(8,128)S(1)}) custom-call(s32[1]{0:T(128)} %bitcast.odd_ref, f32[6,4,8,256]{3,2,1,0:T(8,128)S(1)} %collective-permute-done.halo_ref, f32[4,6,4,2,8,128]{5,4,3,2,1,0:T(8,128)S(1)} %shard_map.69.coef_ref, f32[2,4,4,2,4,2,8,128]{7,6,5,4,3,2,1,0:T(8,128)S(1)} %get-tuple-element.24.seam_ref, ...), custom_call_target="tpu_custom_call" | custom-call | tf_op jit(solution)/shard_map/pallas_call | solution.py:382
  22.3 0.0 copy-start.1
  22.3 0.6 %collective-permute-done.2.halo_ref = f32[4,4,8,256]{3,2,1,0:T(8,128)S(1)} collective-permute-done((f32[4,4,8,256]{3,2,1,0:T(8,128)S(1)}, f32[4,4,8,256]{3,2,1,0:T(8,128)S(1)}, u32[]{:S(2)}, u32[]{:S(2)}) %collective-permute-start.2) | collective-permute-done | bytes 131104 | tf_op jit(solution)/shard_map/ppermute | solution.py:423
  22.9 0.6 %shard_map.75 = (f32[8,4,2,8,128]{4,3,2,1,0:T(8,128)S(1)}, f32[8,8]{1,0:T(8,128)S(1)}) custom-call(s32[1]{0:T(128)} %bitcast.odd_ref, f32[4,4,8,256]{3,2,1,0:T(8,128)S(1)} %collective-permute-done.2.halo_ref, f32[4,6,4,2,8,128]{5,4,3,2,1,0:T(8,128)S(1)} %shard_map.69.coef_ref, f32[2,4,4,2,4,2,8,128]{7,6,5,4,3,2,1,0:T(8,128)S(1)} %get-tuple-element.30.seam_ref, ...), custom_call_target="tpu_custom_call" | custom-call | tf_op jit(solution)/shard_map/pallas_call | solution.py:382
  23.5 0.1 collective-permute-start.3
  23.6 3.6 %collective-permute-done.3 = f32[2,8,8]{2,1,0:T(8,128)S(1)} collective-permute-done((f32[2,8,8]{2,1,0:T(8,128)S(1)}, f32[2,8,8]{2,1,0:T(8,128)S(1)}, u32[]{:S(2)}, u32[]{:S(2)}) %collective-permute-start.3) | collective-permute-done | bytes 544 | tf_op jit(solution)/shard_map/ppermute | solution.py:28
  27.2 0.0 collective-permute-start.4
  27.2 3.6 %collective-permute-done.4 = f32[2,8,8]{2,1,0:T(8,128)S(1)} collective-permute-done((f32[2,8,8]{2,1,0:T(8,128)S(1)}, f32[2,8,8]{2,1,0:T(8,128)S(1)}, u32[]{:S(2)}, u32[]{:S(2)}) %collective-permute-start.4) | collective-permute-done | bytes 544 | tf_op jit(solution)/shard_map/ppermute | solution.py:28
  30.9 0.7 %collective-permute-start.5 = (f32[2,8,8]{2,1,0:T(8,128)S(1)}, f32[2,8,8]{2,1,0:T(8,128)S(1)}, u32[]{:S(2)}, u32[]{:S(2)}) collective-permute-start(f32[2,8,8]{2,1,0:T(8,128)S(1)} %fusion.1), channel_id=1, source_target_pairs={{0,4},{1,5},{2,6},{3,7},{4,0},{5,1},{6,2},{7,3},{8,12},{9,13},{10,... | collective-permute-start | bytes 1544 | tf_op jit(solution)/shard_map/ppermute | solution.py:28
  31.6 3.9 %collective-permute-done.5 = f32[2,8,8]{2,1,0:T(8,128)S(1)} collective-permute-done((f32[2,8,8]{2,1,0:T(8,128)S(1)}, f32[2,8,8]{2,1,0:T(8,128)S(1)}, u32[]{:S(2)}, u32[]{:S(2)}) %collective-permute-start.5) | collective-permute-done | bytes 544 | tf_op jit(solution)/shard_map/ppermute | solution.py:28
  35.4 0.0 copy-start
  35.4 0.0 copy-done.1
  35.4 0.2 shard_map.77
  35.7 0.1 collective-permute-start.6
  35.8 1.2 %collective-permute-done.6 = f32[4,2,4,256]{3,2,0,1:T(4,128)S(1)} collective-permute-done((f32[4,2,4,256]{3,2,0,1:T(4,128)S(1)}, f32[4,2,4,256]{3,2,0,1:T(4,128)S(1)}, u32[]{:S(2)}, u32[]{:S(2)}) %collective-permute-start.6) | collective-permute-done | bytes 32800 | tf_op jit(solution)/shard_map/ppermute | solution.py:28
  37.0 1.6 %collective-permute-start.7 = (f32[4,1,4,256]{3,2,0,1:T(4,128)S(1)}, f32[4,1,4,256]{3,2,0,1:T(4,128)S(1)}, u32[]{:S(2)}, u32[]{:S(2)}) collective-permute-start(f32[4,1,4,256]{3,2,0,1:T(4,128)S(1)} %constant_dynamic-slice_fusion), channel_id=1, source_target_pairs={{0,16},{8,24},{16,0},{24,8},{1,17},{9,25},{17,1},{25,9},{2,18},{10... | collective-permute-start | bytes 49160 | tf_op jit(solution)/shard_map/ppermute | solution.py:28
  38.5 1.0 %shard_map.76 = f32[16,4,16,256]{3,2,1,0:T(8,128)} custom-call(f32[8,4,2,8,128]{4,3,2,1,0:T(8,128)S(1)} %get-tuple-element.22.refs_0_, f32[8,4,2,8,128]{4,3,2,1,0:T(8,128)S(1)} %get-tuple-element.27.refs_1_, f32[8,4,2,8,128]{4,3,2,1,0:T(8,128)S(1)} %get-tuple-element.28.refs_2_, f32[8,4,2,8,128]{4,3,2,1,0:T(8,128)S(1)} %get-tuple-element.32.refs_3_), custom_call_target="tpu_custom_call" | custom-call | tf_op jit(solution)/shard_map/pallas_call | solution.py:382
  39.6 1.2 %collective-permute-done.7 = f32[4,1,4,256]{3,2,0,1:T(4,128)S(1)} collective-permute-done((f32[4,1,4,256]{3,2,0,1:T(4,128)S(1)}, f32[4,1,4,256]{3,2,0,1:T(4,128)S(1)}, u32[]{:S(2)}, u32[]{:S(2)}) %collective-permute-start.7) | collective-permute-done | bytes 16416 | tf_op jit(solution)/shard_map/ppermute | solution.py:28
  40.8 0.6 %add_bitcast_fusion = f32[1,4,4,256]{3,2,1,0:T(4,128)} fusion(f32[4,1,4,256]{3,2,0,1:T(4,128)S(1)} %collective-permute-done.7, f32[4,2,4,256]{3,2,0,1:T(4,128)S(1)} %bitcast_add_fusion, s32[]{:T(128)S(6)} %select_n.35), kind=kLoop, calls=%fused_computation.2 | loop fusion | flops 4096 | bytes 49156 | tf_op jit(solution)/shard_map/reshape | solution.py:491
  41.4 0.0 copy-done
  (9 shorter events, 0.1 us)
Async XLA Ops:
  2.0 18.3 %collective-permute-start.1 = (f32[10,4,8,256]{3,2,1,0:T(8,128)S(1)}, f32[10,4,8,256]{3,2,1,0:T(8,128)S(1)}, u32[]{:S(2)}, u32[]{:S(2)}) collective-permute-start(f32[10,4,8,256]{3,2,1,0:T(8,128)S(1)} %get-tuple-element.26), channel_id=1, source_target_pairs={{0,7},{1,2},{2,1},{3,4},{4,3},{5,6},{6,5},{7,0},{8,15},{9,10},{10,... | collective-permute-start | bytes 983048 | tf_op jit(solution)/shard_map/ppermute | solution.py:424
  8.1 12.0 %collective-permute-start = (f32[6,4,8,256]{3,2,1,0:T(8,128)S(1)}, f32[6,4,8,256]{3,2,1,0:T(8,128)S(1)}, u32[]{:S(2)}, u32[]{:S(2)}) collective-permute-start(f32[6,4,8,256]{3,2,1,0:T(8,128)S(1)} %get-tuple-element.23), channel_id=1, source_target_pairs={{0,1},{1,0},{2,3},{3,2},{4,5},{5,4},{6,7},{7,6},{8,9},{9,8},{10,11... | collective-permute-start | bytes 589832 | tf_op jit(solution)/shard_map/ppermute | solution.py:423
  8.2 14.7 %collective-permute-start.2 = (f32[4,4,8,256]{3,2,1,0:T(8,128)S(1)}, f32[4,4,8,256]{3,2,1,0:T(8,128)S(1)}, u32[]{:S(2)}, u32[]{:S(2)}) collective-permute-start(f32[4,4,8,256]{3,2,1,0:T(8,128)S(1)} %get-tuple-element.29), channel_id=1, source_target_pairs={{0,1},{1,0},{2,3},{3,2},{4,5},{5,4},{6,7},{7,6},{8,9},{9,8},{10,11... | collective-permute-start | bytes 393224 | tf_op jit(solution)/shard_map/ppermute | solution.py:423
  22.3 13.2 %copy-start.1 = (f32[2,8]{1,0:T(2,128)S(1)}, f32[2,8]{1,0:T(2,128)}, u32[]{:S(2)}) copy-start(f32[2,8]{1,0:T(2,128)} %occ_ref.1) | copy-start | bytes 196
  23.5 3.7 %collective-permute-start.3 = (f32[2,8,8]{2,1,0:T(8,128)S(1)}, f32[2,8,8]{2,1,0:T(8,128)S(1)}, u32[]{:S(2)}, u32[]{:S(2)}) collective-permute-start(f32[2,8,8]{2,1,0:T(8,128)S(1)} %maximum_multiply_fusion), channel_id=1, source_target_pairs={{0,1},{1,0},{2,3},{3,2},{4,5},{5,4},{6,7},{7,6},{8,9},{9,8},{10,11... | collective-permute-start | bytes 1544 | tf_op jit(solution)/shard_map/ppermute | solution.py:28
  27.2 3.7 %collective-permute-start.4 = (f32[2,8,8]{2,1,0:T(8,128)S(1)}, f32[2,8,8]{2,1,0:T(8,128)S(1)}, u32[]{:S(2)}, u32[]{:S(2)}) collective-permute-start(f32[2,8,8]{2,1,0:T(8,128)S(1)} %fusion), channel_id=1, source_target_pairs={{0,2},{1,3},{2,0},{3,1},{4,6},{5,7},{6,4},{7,5},{8,10},{9,11},{10,... | collective-permute-start | bytes 1544 | tf_op jit(solution)/shard_map/ppermute | solution.py:28
  30.9 4.5 %collective-permute-start.5 = (f32[2,8,8]{2,1,0:T(8,128)S(1)}, f32[2,8,8]{2,1,0:T(8,128)S(1)}, u32[]{:S(2)}, u32[]{:S(2)}) collective-permute-start(f32[2,8,8]{2,1,0:T(8,128)S(1)} %fusion.1), channel_id=1, source_target_pairs={{0,4},{1,5},{2,6},{3,7},{4,0},{5,1},{6,2},{7,3},{8,12},{9,13},{10,... | collective-permute-start | bytes 1544 | tf_op jit(solution)/shard_map/ppermute | solution.py:28
  35.4 6.0 %copy-start = (f32[2,8,8]{2,1,0:T(8,128)}, f32[2,8,8]{2,1,0:T(8,128)S(1)}, u32[]{:S(2)}) copy-start(f32[2,8,8]{2,1,0:T(8,128)S(1)} %add.42.gram_ref) | copy-start | bytes 1540
  35.7 1.3 %collective-permute-start.6 = (f32[4,2,4,256]{3,2,0,1:T(4,128)S(1)}, f32[4,2,4,256]{3,2,0,1:T(4,128)S(1)}, u32[]{:S(2)}, u32[]{:S(2)}) collective-permute-start(f32[4,2,4,256]{3,2,0,1:T(4,128)S(1)} %bitcast.26), channel_id=1, source_target_pairs={{0,8},{8,0},{16,24},{24,16},{1,9},{9,1},{17,25},{25,17},{2,10},{10... | collective-permute-start | bytes 98312 | tf_op jit(solution)/shard_map/ppermute | solution.py:28
  37.0 3.8 %collective-permute-start.7 = (f32[4,1,4,256]{3,2,0,1:T(4,128)S(1)}, f32[4,1,4,256]{3,2,0,1:T(4,128)S(1)}, u32[]{:S(2)}, u32[]{:S(2)}) collective-permute-start(f32[4,1,4,256]{3,2,0,1:T(4,128)S(1)} %constant_dynamic-slice_fusion), channel_id=1, source_target_pairs={{0,16},{8,24},{16,0},{24,8},{1,17},{9,25},{17,1},{25,9},{2,18},{10... | collective-permute-start | bytes 49160 | tf_op jit(solution)/shard_map/ppermute | solution.py:28

commit v4 on v3

--- a/solution.py
+++ b/solution.py
@@ -46,11 +46,11 @@
     return [jnp.where(lane == 0, turned[h - 1], turned[h]) for h in range(len(line))]
 
 
-def pack_kernel(blocks, odd_ref, pot_any, kin_any, orb_any, *refs):
-    a_refs, b_ref = refs[:blocks], refs[blocks]
-    pot_ref, kin_ref, orb_ref, arrivals = refs[blocks + 1 :]
+def pack_kernel(blocks, odd_ref, core_ref, pot_any, kin_any, orb_any, *refs):
+    a_refs, b_refs = refs[:blocks], refs[blocks : 2 * blocks]
+    pot_ref, kin_ref, orb_ref, arrivals = refs[2 * blocks :]
     count, rows_x, rows_y, depth = orb_ref.shape
-    odd = odd_ref[0] == 1
+    odd, core = odd_ref[0] == 1, core_ref[0] == 1
     row, _ = iotas()
     upper = row < DEGREE
     size = count // blocks
@@ -75,8 +75,7 @@
         high_a, high_b = edges(kin_ref.at[1], kin_ref.at[2], x, h)
         a_refs[0][0, x, :, cut(h)] = low_a
         a_refs[0][1, x, :, cut(h)] = high_a
-        b_ref[0, x, :, cut(h)] = low_b
-        b_ref[1, x, :, cut(h)] = high_b
+        b_refs[0][0, x, :, cut(h)] = jnp.where(core, high_b, low_b)
     for k in range(blocks):
         loads[2 + k].wait()
         for p in range(size // 2):
@@ -84,7 +83,7 @@
             for x, h in places:
                 a, b = edges(orb_ref.at[m], orb_ref.at[m + 1], x, h)
                 a_refs[k][(0 if k else 2) + p, x, :, cut(h)] = a
-                b_ref[2 + m // 2, x, :, cut(h)] = b
+                b_refs[k][(0 if k else 1) + p, x, :, cut(h)] = b
 
 
 def ring_tiles(ref, index, parts):
@@ -201,8 +200,10 @@
         sums_ref[i] = value
 
 
-def windows_kernel(second, odd_ref, pot_ref, kin_ref, halo_ref, coef_ref):
+def windows_kernel(second, odd_ref, core_ref, pot_ref, kin_ref, *refs):
+    halo_refs, coef_ref = refs[:-1], refs[-1]
     rows_x, rows_y, depth = pot_ref.shape
+    core = core_ref[0] == 1
     side = odd_ref[0] if second else 1 - odd_ref[0]
     top = side == 0
     row, lane = iotas()
@@ -217,7 +218,11 @@
 
     def field(c, x, h):
         own_ref = pot_ref if c == 0 else kin_ref.at[c - 1]
-        halo = halo_ref[c // 2, x, :, cut(h)]
+        if second:
+            mine = core if c // 2 else jnp.logical_not(core)
+            halo = jnp.where(mine, halo_refs[0][0, x, :, cut(h)], halo_refs[1][0, x, :, cut(h)])
+        else:
+            halo = halo_refs[0][c // 2, x, :, cut(h)]
         head, tail = own_ref[x, 0:SUB, cut(h)], own_ref[x, rows_y - SUB :, cut(h)]
         before = pltpu.roll(halo, DEGREE, 0) if c % 2 else halo
         after = pltpu.roll(halo, 1 if c % 2 else DEGREE + 1, 0)
@@ -400,6 +405,7 @@
     band = lax.axis_index("band")
     bands = lax.axis_size("band")
     odd = lax.rem(position, 2).astype(jnp.int32).reshape(1)
+    core = lax.rem(band, 2).astype(jnp.int32).reshape(1)
 
     pairs_a = [(i, i ^ 1) for i in range(domains)]
     pairs_b = [(i, (i + 1) % domains if i % 2 else (i - 1) % domains) for i in range(domains)]
@@ -408,20 +414,24 @@
         functools.partial(pack_kernel, blocks),
         (
             odd,
+            core,
             pltpu.with_memory_space_constraint(potential[0], pltpu.HBM),
             pltpu.with_memory_space_constraint(kinetic[:, 0], pltpu.HBM),
             pltpu.with_memory_space_constraint(orbitals.reshape(count, rows_x, rows_y, depth), pltpu.HBM),
         ),
-        [(size, rows_x, SUB, depth) for size in [2 + half] + [half] * (blocks - 1) + [2 + count // 2]]
+        [(size, rows_x, SUB, depth) for size in [2 + half] + [half] * (blocks - 1) + [1 + half] + [half] * (blocks - 1)]
         + [(rows_x, rows_y, depth), (3, rows_x, rows_y, depth), (count, rows_x, rows_y, depth)],
         [pltpu.SemaphoreType.DMA((2 + blocks,))],
-        specs=[smem()] + [anywhere()] * 3,
+        specs=[smem()] * 2 + [anywhere()] * 3,
         place=pltpu.VMEM,
     )
     halos_a = []
     for k in range(blocks):
         halos_a.append(lax.ppermute(halos[k], "grid", pairs_a))
-    halo_b = lax.ppermute(halos[blocks], "grid", pairs_b)
+    halos_b = []
+    for k in range(blocks):
+        halos_b.append(lax.ppermute(halos[blocks + k], "grid", pairs_b))
+    other = swapped(halos_b[0][:1], "band", 1)
 
     inner = [
         call(
@@ -442,17 +452,23 @@
     ]
     coef_shape = (DEGREE, 6, rows_x, blocks_z) + tile
     (coef_a,) = call(
-        functools.partial(windows_kernel, 0), (odd, pot, kin, halos_a[0]), [coef_shape], specs=[smem()] + [vmem()] * 3
+        functools.partial(windows_kernel, 0),
+        (odd, core, pot, kin, halos_a[0]),
+        [coef_shape],
+        specs=[smem()] * 2 + [vmem()] * 3,
     )
     (coef_b,) = call(
-        functools.partial(windows_kernel, 1), (odd, pot, kin, halo_b), [coef_shape], specs=[smem()] + [vmem()] * 3
+        functools.partial(windows_kernel, 1),
+        (odd, core, pot, kin, halos_b[0], other),
+        [coef_shape],
+        specs=[smem()] * 2 + [vmem()] * 4,
     )
     rows, grams = [], []
     for k in range(blocks):
         body, seam, sums = inner[k]
         (second,) = call(
-            functools.partial(edge_kernel, 2 + k * half),
-            (odd, halo_b, coef_b, seam),
+            functools.partial(edge_kernel, 0 if k else 1),
+            (odd, halos_b[k], coef_b, seam),
             [(half, rows_x, blocks_z) + tile],
             specs=[smem()] + [vmem()] * 3,
         )

time: 41.5 us -> 38.5 us (0.928)
  waiting for transfers between devices: 20.3 us -> 12.5 us
  starting transfers between devices: 10.5 us -> 15.2 us
    ppermute x2, waiting for transfers between devices: 6.74 us -> 0.03 us  [fast_body(): halos_a.append(lax.ppermute(halos[k], 'grid', pairs_a))]
    ppermute x5 -> x6, starting transfers between devices: 2.37 us -> 7.39 us  [swapped(): return lax.ppermute(value, axis, [(i, i ^ bit) for i in range(count)])]
    ppermute x5 -> x6, waiting for transfers between devices: 13.5 us -> 8.52 us  [swapped(): return lax.ppermute(value, axis, [(i, i ^ bit) for i in range(count)])]
    ppermute x1 -> x2, waiting for transfers between devices: 0.01 us -> 3.97 us  [fast_body(): halos_b.append(lax.ppermute(halos[blocks + k], 'grid', pairs_b))]
    ppermute x1 -> x2, starting transfers between devices: 6.1 us -> 4.72 us  [fast_body(): halos_b.append(lax.ppermute(halos[blocks + k], 'grid', pairs_b))]
    ppermute x2, starting transfers between devices: 2.03 us -> 3.06 us  [fast_body(): halos_a.append(lax.ppermute(halos[k], 'grid', pairs_a))]
  transfers between devices with their start and end apart: 8 -> 10, of which waited for: 7 -> 6; matrix products, arithmetic and copies ran while one was open for 0% -> 0% of each run, Pallas kernels for 17% -> 18%
where the time goes in v4:
time: 38.5 us; the launch traced here: 38.4 us
  starting transfers between devices  15.2 us (39%)
  waiting for transfers between devices  12.5 us (32%)
  Pallas kernels  9.14 us (24%)
  between operations  0.81 us (2%)
  other arithmetic  0.66 us (2%)
    pallas_call x11, Pallas kernels, call(): pl.pallas_call(kernel, out_shape=shapes, in_specs=[vmem() for _ in operan...  9.14 us
    ppermute x6, waiting for transfers between devices, swapped(): return lax.ppermute(value, axis, [(i, i ^ bit) for i in range(count)])  8.52 us
    ppermute x6, starting transfers between devices, swapped(): return lax.ppermute(value, axis, [(i, i ^ bit) for i in range(count)])  7.39 us
    ppermute x2, starting transfers between devices, fast_body(): halos_b.append(lax.ppermute(halos[blocks + k], 'grid', pairs_b))  4.72 us
    ppermute x2, waiting for transfers between devices, fast_body(): halos_b.append(lax.ppermute(halos[blocks + k], 'grid', pairs_b))  3.97 us
    ppermute x2, starting transfers between devices, fast_body(): halos_a.append(lax.ppermute(halos[k], 'grid', pairs_a))  3.06 us
  transfers between devices with their start and end apart: 10, of which 6 were waited for; matrix products, arithmetic and copies ran while one was open for 0% of the time, Pallas kernels for 18%

profile of v4, /device:TPU:0, one launch (start us, length us, event | category | flops | bytes accessed | tf_op | source)
XLA Modules:
  0.0 38.4 jit_solution(13782076690223359267)
XLA Ops:
  0.6 1.4 %shard_map.67 = (f32[6,4,8,256]{3,2,1,0:T(8,128)S(1)}, f32[4,4,8,256]{3,2,1,0:T(8,128)S(1)}, f32[5,4,8,256]{3,2,1,0:T(8,128)S(1)}, f32[4,4,8,256]{3,2,1,0:T(8,12...) custom-call(s32[1]{0:T(128)} %bitcast.odd_ref, ...), custom_call_target="tpu_custom_call" | custom-call | tf_op jit(solution)/shard_map/pallas_call | solution.py:387
  2.1 3.1 %collective-permute-start = (f32[6,4,8,256]{3,2,1,0:T(8,128)S(1)}, f32[6,4,8,256]{3,2,1,0:T(8,128)S(1)}, u32[]{:S(2)}, u32[]{:S(2)}) collective-permute-start(f32[6,4,8,256]{3,2,1,0:T(8,128)S(1)} %get-tuple-element.24), channel_id=1, source_target_pairs={{0,1},{1,0},{2,3},{3,2},{4,5},{5,4},{6,7},{7,6},{8,9},{9,8},{10,11... | collective-permute-start | bytes 589832 | tf_op jit(solution)/shard_map/ppermute | solution.py:430
  5.1 3.5 %collective-permute-start.1 = (f32[5,4,8,256]{3,2,1,0:T(8,128)S(1)}, f32[5,4,8,256]{3,2,1,0:T(8,128)S(1)}, u32[]{:S(2)}, u32[]{:S(2)}) collective-permute-start(f32[5,4,8,256]{3,2,1,0:T(8,128)S(1)} %get-tuple-element.27), channel_id=1, source_target_pairs={{0,7},{1,2},{2,1},{3,4},{4,3},{5,6},{6,5},{7,0},{8,15},{9,10},{10,... | collective-permute-start | bytes 491528 | tf_op jit(solution)/shard_map/ppermute | solution.py:433
  8.7 1.2 %collective-permute-start.4 = (f32[4,4,8,256]{3,2,1,0:T(8,128)S(1)}, f32[4,4,8,256]{3,2,1,0:T(8,128)S(1)}, u32[]{:S(2)}, u32[]{:S(2)}) collective-permute-start(f32[4,4,8,256]{3,2,1,0:T(8,128)S(1)} %get-tuple-element.33), channel_id=1, source_target_pairs={{0,7},{1,2},{2,1},{3,4},{4,3},{5,6},{6,5},{7,0},{8,15},{9,10},{10,... | collective-permute-start | bytes 393224 | tf_op jit(solution)/shard_map/ppermute | solution.py:433
  9.8 0.0 collective-permute-start.3
  9.8 4.0 %collective-permute-done.1.refs_0_.halo_ref = f32[5,4,8,256]{3,2,1,0:T(8,128)S(1)} collective-permute-done((f32[5,4,8,256]{3,2,1,0:T(8,128)S(1)}, f32[5,4,8,256]{3,2,1,0:T(8,128)S(1)}, u32[]{:S(2)}, u32[]{:S(2)}) %collective-permute-start.1) | collective-permute-done | bytes 163872 | tf_op jit(solution)/shard_map/ppermute | solution.py:433
  13.8 0.0 collective-permute-start.2
  13.8 1.9 %shard_map.68 = (f32[8,4,2,8,128]{4,3,2,1,0:T(8,128)S(1)}, f32[2,4,4,2,4,2,8,128]{7,6,5,4,3,2,1,0:T(8,128)S(1)}, f32[36,8,128]{2,1,0:T(8,128)S(1)}) custom-call(f32[4,16,256]{2,1,0:T(8,128)S(1)} %get-tuple-element.20.pot_ref, f32[3,4,16,256]{3,2,1,0:T(8,128)S(1)} %get-tuple-element.21.kin_ref, f32[16,4,16,256]{3,2,1,0:T(8,128)S(1)} %get-tuple-element.22.orb_ref), custom_call_target="tpu_custom_call" | custom-call | tf_op jit(solution)/shard_map/pallas_call | solution.py:387
  15.7 1.9 %shard_map.73 = (f32[8,4,2,8,128]{4,3,2,1,0:T(8,128)S(1)}, f32[2,4,4,2,4,2,8,128]{7,6,5,4,3,2,1,0:T(8,128)S(1)}, f32[36,8,128]{2,1,0:T(8,128)S(1)}) custom-call(f32[4,16,256]{2,1,0:T(8,128)S(1)} %get-tuple-element.20.pot_ref, f32[3,4,16,256]{3,2,1,0:T(8,128)S(1)} %get-tuple-element.21.kin_ref, f32[16,4,16,256]{3,2,1,0:T(8,128)S(1)} %get-tuple-element.22.orb_ref), custom_call_target="tpu_custom_call" | custom-call | tf_op jit(solution)/shard_map/pallas_call | solution.py:387
  17.7 0.0 collective-permute-done.refs_0_.halo_ref
  17.7 0.2 shard_map.69.coef_ref
  17.9 0.0 collective-permute-done.2.refs_1_
  17.9 0.2 shard_map.70.coef_ref
  18.1 0.5 %shard_map.71.second_ref = f32[4,4,2,8,128]{4,3,2,1,0:T(8,128)S(1)} custom-call(s32[1]{0:T(128)} %bitcast.odd_ref, f32[5,4,8,256]{3,2,1,0:T(8,128)S(1)} %collective-permute-done.1.refs_0_.halo_ref, f32[4,6,4,2,8,128]{5,4,3,2,1,0:T(8,128)S(1)} %shard_map.70.coef_ref, f32[2,4,4,2,4,2,8,128]{7,6,5,4,3,2,1,0:T(8,128)S(1)} %get-tuple-element.25.seam_ref), custom_call_target="tpu_custom_call" | custom-call | tf_op jit(solution)/shard_map/pallas_call | solution.py:387
  18.6 0.0 collective-permute-done.4.halo_ref
  18.6 0.5 %shard_map.74.second_ref = f32[4,4,2,8,128]{4,3,2,1,0:T(8,128)S(1)} custom-call(s32[1]{0:T(128)} %bitcast.odd_ref, f32[4,4,8,256]{3,2,1,0:T(8,128)S(1)} %collective-permute-done.4.halo_ref, f32[4,6,4,2,8,128]{5,4,3,2,1,0:T(8,128)S(1)} %shard_map.70.coef_ref, f32[2,4,4,2,4,2,8,128]{7,6,5,4,3,2,1,0:T(8,128)S(1)} %get-tuple-element.31.seam_ref), custom_call_target="tpu_custom_call" | custom-call | tf_op jit(solution)/shard_map/pallas_call | solution.py:387
  19.2 0.6 %shard_map.72 = (f32[8,4,2,8,128]{4,3,2,1,0:T(8,128)S(1)}, f32[8,8]{1,0:T(8,128)S(1)}) custom-call(s32[1]{0:T(128)} %bitcast.odd_ref, f32[6,4,8,256]{3,2,1,0:T(8,128)S(1)} %collective-permute-done.refs_0_.halo_ref, f32[4,6,4,2,8,128]{5,4,3,2,1,0:T(8,128)S(1)} %shard_map.69.coef_ref, f32[2,4,4,2,4,2,8,128]{7,6,5,4,3,2,1,0:T(8,128)S(1)} %get-tuple-element.25.seam_ref, ...), custom_call_target="tpu_custom_call" | custom-call | tf_op jit(solution)/shard_map/pallas_call | solution.py:387
  19.8 0.0 copy-start.1
  19.8 0.0 collective-permute-done.3.halo_ref
  19.8 0.6 %shard_map.75 = (f32[8,4,2,8,128]{4,3,2,1,0:T(8,128)S(1)}, f32[8,8]{1,0:T(8,128)S(1)}) custom-call(s32[1]{0:T(128)} %bitcast.odd_ref, f32[4,4,8,256]{3,2,1,0:T(8,128)S(1)} %collective-permute-done.3.halo_ref, f32[4,6,4,2,8,128]{5,4,3,2,1,0:T(8,128)S(1)} %shard_map.69.coef_ref, f32[2,4,4,2,4,2,8,128]{7,6,5,4,3,2,1,0:T(8,128)S(1)} %get-tuple-element.31.seam_ref, ...), custom_call_target="tpu_custom_call" | custom-call | tf_op jit(solution)/shard_map/pallas_call | solution.py:387
  20.5 1.6 %collective-permute-start.5 = (f32[2,8,8]{2,1,0:T(8,128)S(1)}, f32[2,8,8]{2,1,0:T(8,128)S(1)}, u32[]{:S(2)}, u32[]{:S(2)}) collective-permute-start(f32[2,8,8]{2,1,0:T(8,128)S(1)} %maximum_multiply_fusion), channel_id=1, source_target_pairs={{0,1},{1,0},{2,3},{3,2},{4,5},{5,4},{6,7},{7,6},{8,9},{9,8},{10,11... | collective-permute-start | bytes 1544 | tf_op jit(solution)/shard_map/ppermute | solution.py:28
  22.0 2.1 %collective-permute-done.5 = f32[2,8,8]{2,1,0:T(8,128)S(1)} collective-permute-done((f32[2,8,8]{2,1,0:T(8,128)S(1)}, f32[2,8,8]{2,1,0:T(8,128)S(1)}, u32[]{:S(2)}, u32[]{:S(2)}) %collective-permute-start.5) | collective-permute-done | bytes 544 | tf_op jit(solution)/shard_map/ppermute | solution.py:28
  24.2 1.6 %collective-permute-start.6 = (f32[2,8,8]{2,1,0:T(8,128)S(1)}, f32[2,8,8]{2,1,0:T(8,128)S(1)}, u32[]{:S(2)}, u32[]{:S(2)}) collective-permute-start(f32[2,8,8]{2,1,0:T(8,128)S(1)} %fusion), channel_id=1, source_target_pairs={{0,2},{1,3},{2,0},{3,1},{4,6},{5,7},{6,4},{7,5},{8,10},{9,11},{10,... | collective-permute-start | bytes 1544 | tf_op jit(solution)/shard_map/ppermute | solution.py:28
  25.8 2.1 %collective-permute-done.6 = f32[2,8,8]{2,1,0:T(8,128)S(1)} collective-permute-done((f32[2,8,8]{2,1,0:T(8,128)S(1)}, f32[2,8,8]{2,1,0:T(8,128)S(1)}, u32[]{:S(2)}, u32[]{:S(2)}) %collective-permute-start.6) | collective-permute-done | bytes 544 | tf_op jit(solution)/shard_map/ppermute | solution.py:28
  27.9 2.6 %collective-permute-start.7 = (f32[2,8,8]{2,1,0:T(8,128)S(1)}, f32[2,8,8]{2,1,0:T(8,128)S(1)}, u32[]{:S(2)}, u32[]{:S(2)}) collective-permute-start(f32[2,8,8]{2,1,0:T(8,128)S(1)} %fusion.1), channel_id=1, source_target_pairs={{0,4},{1,5},{2,6},{3,7},{4,0},{5,1},{6,2},{7,3},{8,12},{9,13},{10,... | collective-permute-start | bytes 1544 | tf_op jit(solution)/shard_map/ppermute | solution.py:28
  30.4 2.0 %collective-permute-done.7 = f32[2,8,8]{2,1,0:T(8,128)S(1)} collective-permute-done((f32[2,8,8]{2,1,0:T(8,128)S(1)}, f32[2,8,8]{2,1,0:T(8,128)S(1)}, u32[]{:S(2)}, u32[]{:S(2)}) %collective-permute-start.7) | collective-permute-done | bytes 544 | tf_op jit(solution)/shard_map/ppermute | solution.py:28
  32.4 0.0 copy-start
  32.4 0.0 copy-done.1
  32.4 0.2 shard_map.77
  32.6 0.1 collective-permute-start.8
  32.8 1.2 %collective-permute-done.8 = f32[4,2,4,256]{3,2,0,1:T(4,128)S(1)} collective-permute-done((f32[4,2,4,256]{3,2,0,1:T(4,128)S(1)}, f32[4,2,4,256]{3,2,0,1:T(4,128)S(1)}, u32[]{:S(2)}, u32[]{:S(2)}) %collective-permute-start.8) | collective-permute-done | bytes 32800 | tf_op jit(solution)/shard_map/ppermute | solution.py:28
  33.9 1.6 %collective-permute-start.9 = (f32[4,1,4,256]{3,2,0,1:T(4,128)S(1)}, f32[4,1,4,256]{3,2,0,1:T(4,128)S(1)}, u32[]{:S(2)}, u32[]{:S(2)}) collective-permute-start(f32[4,1,4,256]{3,2,0,1:T(4,128)S(1)} %constant_dynamic-slice_fusion), channel_id=1, source_target_pairs={{0,16},{8,24},{16,0},{24,8},{1,17},{9,25},{17,1},{25,9},{2,18},{10... | collective-permute-start | bytes 49160 | tf_op jit(solution)/shard_map/ppermute | solution.py:28
  35.5 1.0 %shard_map.76 = f32[16,4,16,256]{3,2,1,0:T(8,128)} custom-call(f32[8,4,2,8,128]{4,3,2,1,0:T(8,128)S(1)} %get-tuple-element.23.refs_0_, f32[8,4,2,8,128]{4,3,2,1,0:T(8,128)S(1)} %get-tuple-element.28.refs_1_, f32[8,4,2,8,128]{4,3,2,1,0:T(8,128)S(1)} %get-tuple-element.29.refs_2_, f32[8,4,2,8,128]{4,3,2,1,0:T(8,128)S(1)} %get-tuple-element.34.refs_3_), custom_call_target="tpu_custom_call" | custom-call | tf_op jit(solution)/shard_map/pallas_call | solution.py:387
  36.5 1.2 %collective-permute-done.9 = f32[4,1,4,256]{3,2,0,1:T(4,128)S(1)} collective-permute-done((f32[4,1,4,256]{3,2,0,1:T(4,128)S(1)}, f32[4,1,4,256]{3,2,0,1:T(4,128)S(1)}, u32[]{:S(2)}, u32[]{:S(2)}) %collective-permute-start.9) | collective-permute-done | bytes 16416 | tf_op jit(solution)/shard_map/ppermute | solution.py:28
  37.8 0.6 %add_bitcast_fusion = f32[1,4,4,256]{3,2,1,0:T(4,128)} fusion(f32[4,1,4,256]{3,2,0,1:T(4,128)S(1)} %collective-permute-done.9, f32[4,2,4,256]{3,2,0,1:T(4,128)S(1)} %bitcast_add_fusion, s32[]{:T(128)S(6)} %select_n.35), kind=kLoop, calls=%fused_computation.2 | loop fusion | flops 4096 | bytes 49156 | tf_op jit(solution)/shard_map/reshape | solution.py:507
  38.4 0.0 copy-done
  (10 shorter events, 0.1 us)
Async XLA Ops:
  2.1 15.6 %collective-permute-start = (f32[6,4,8,256]{3,2,1,0:T(8,128)S(1)}, f32[6,4,8,256]{3,2,1,0:T(8,128)S(1)}, u32[]{:S(2)}, u32[]{:S(2)}) collective-permute-start(f32[6,4,8,256]{3,2,1,0:T(8,128)S(1)} %get-tuple-element.24), channel_id=1, source_target_pairs={{0,1},{1,0},{2,3},{3,2},{4,5},{5,4},{6,7},{7,6},{8,9},{9,8},{10,11... | collective-permute-start | bytes 589832 | tf_op jit(solution)/shard_map/ppermute | solution.py:430
  5.1 8.7 %collective-permute-start.1 = (f32[5,4,8,256]{3,2,1,0:T(8,128)S(1)}, f32[5,4,8,256]{3,2,1,0:T(8,128)S(1)}, u32[]{:S(2)}, u32[]{:S(2)}) collective-permute-start(f32[5,4,8,256]{3,2,1,0:T(8,128)S(1)} %get-tuple-element.27), channel_id=1, source_target_pairs={{0,7},{1,2},{2,1},{3,4},{4,3},{5,6},{6,5},{7,0},{8,15},{9,10},{10,... | collective-permute-start | bytes 491528 | tf_op jit(solution)/shard_map/ppermute | solution.py:433
  8.7 10.0 %collective-permute-start.4 = (f32[4,4,8,256]{3,2,1,0:T(8,128)S(1)}, f32[4,4,8,256]{3,2,1,0:T(8,128)S(1)}, u32[]{:S(2)}, u32[]{:S(2)}) collective-permute-start(f32[4,4,8,256]{3,2,1,0:T(8,128)S(1)} %get-tuple-element.33), channel_id=1, source_target_pairs={{0,7},{1,2},{2,1},{3,4},{4,3},{5,6},{6,5},{7,0},{8,15},{9,10},{10,... | collective-permute-start | bytes 393224 | tf_op jit(solution)/shard_map/ppermute | solution.py:433
  9.8 10.0 %collective-permute-start.3 = (f32[4,4,8,256]{3,2,1,0:T(8,128)S(1)}, f32[4,4,8,256]{3,2,1,0:T(8,128)S(1)}, u32[]{:S(2)}, u32[]{:S(2)}) collective-permute-start(f32[4,4,8,256]{3,2,1,0:T(8,128)S(1)} %get-tuple-element.30), channel_id=1, source_target_pairs={{0,1},{1,0},{2,3},{3,2},{4,5},{5,4},{6,7},{7,6},{8,9},{9,8},{10,11... | collective-permute-start | bytes 393224 | tf_op jit(solution)/shard_map/ppermute | solution.py:430
  13.8 4.1 %collective-permute-start.2 = (f32[1,4,8,256]{3,2,1,0:T(8,128)S(1)}, f32[1,4,8,256]{3,2,1,0:T(8,128)S(1)}, u32[]{:S(2)}, u32[]{:S(2)}) collective-permute-start(f32[1,4,8,256]{3,2,1,0:T(8,128)S(1)} %slice.4), channel_id=1, source_target_pairs={{0,8},{8,0},{16,24},{24,16},{1,9},{9,1},{17,25},{25,17},{2,10},{10... | collective-permute-start | bytes 98312 | tf_op jit(solution)/shard_map/ppermute | solution.py:28
  19.8 12.6 %copy-start.1 = (f32[2,8]{1,0:T(2,128)S(1)}, f32[2,8]{1,0:T(2,128)}, u32[]{:S(2)}) copy-start(f32[2,8]{1,0:T(2,128)} %occ_ref.1) | copy-start | bytes 196
  20.5 3.7 %collective-permute-start.5 = (f32[2,8,8]{2,1,0:T(8,128)S(1)}, f32[2,8,8]{2,1,0:T(8,128)S(1)}, u32[]{:S(2)}, u32[]{:S(2)}) collective-permute-start(f32[2,8,8]{2,1,0:T(8,128)S(1)} %maximum_multiply_fusion), channel_id=1, source_target_pairs={{0,1},{1,0},{2,3},{3,2},{4,5},{5,4},{6,7},{7,6},{8,9},{9,8},{10,11... | collective-permute-start | bytes 1544 | tf_op jit(solution)/shard_map/ppermute | solution.py:28
  24.2 3.7 %collective-permute-start.6 = (f32[2,8,8]{2,1,0:T(8,128)S(1)}, f32[2,8,8]{2,1,0:T(8,128)S(1)}, u32[]{:S(2)}, u32[]{:S(2)}) collective-permute-start(f32[2,8,8]{2,1,0:T(8,128)S(1)} %fusion), channel_id=1, source_target_pairs={{0,2},{1,3},{2,0},{3,1},{4,6},{5,7},{6,4},{7,5},{8,10},{9,11},{10,... | collective-permute-start | bytes 1544 | tf_op jit(solution)/shard_map/ppermute | solution.py:28
  27.9 4.5 %collective-permute-start.7 = (f32[2,8,8]{2,1,0:T(8,128)S(1)}, f32[2,8,8]{2,1,0:T(8,128)S(1)}, u32[]{:S(2)}, u32[]{:S(2)}) collective-permute-start(f32[2,8,8]{2,1,0:T(8,128)S(1)} %fusion.1), channel_id=1, source_target_pairs={{0,4},{1,5},{2,6},{3,7},{4,0},{5,1},{6,2},{7,3},{8,12},{9,13},{10,... | collective-permute-start | bytes 1544 | tf_op jit(solution)/shard_map/ppermute | solution.py:28
  32.4 6.0 %copy-start = (f32[2,8,8]{2,1,0:T(8,128)}, f32[2,8,8]{2,1,0:T(8,128)S(1)}, u32[]{:S(2)}) copy-start(f32[2,8,8]{2,1,0:T(8,128)S(1)} %add.42.gram_ref) | copy-start | bytes 1540
  32.6 1.3 %collective-permute-start.8 = (f32[4,2,4,256]{3,2,0,1:T(4,128)S(1)}, f32[4,2,4,256]{3,2,0,1:T(4,128)S(1)}, u32[]{:S(2)}, u32[]{:S(2)}) collective-permute-start(f32[4,2,4,256]{3,2,0,1:T(4,128)S(1)} %bitcast.27), channel_id=1, source_target_pairs={{0,8},{8,0},{16,24},{24,16},{1,9},{9,1},{17,25},{25,17},{2,10},{10... | collective-permute-start | bytes 98312 | tf_op jit(solution)/shard_map/ppermute | solution.py:28
  33.9 3.8 %collective-permute-start.9 = (f32[4,1,4,256]{3,2,0,1:T(4,128)S(1)}, f32[4,1,4,256]{3,2,0,1:T(4,128)S(1)}, u32[]{:S(2)}, u32[]{:S(2)}) collective-permute-start(f32[4,1,4,256]{3,2,0,1:T(4,128)S(1)} %constant_dynamic-slice_fusion), channel_id=1, source_target_pairs={{0,16},{8,24},{16,0},{24,8},{1,17},{9,25},{17,1},{25,9},{2,18},{10... | collective-permute-start | bytes 49160 | tf_op jit(solution)/shard_map/ppermute | solution.py:28

commit v5 on v4

--- a/solution.py
+++ b/solution.py
@@ -46,44 +46,56 @@
     return [jnp.where(lane == 0, turned[h - 1], turned[h]) for h in range(len(line))]
 
 
-def pack_kernel(blocks, odd_ref, core_ref, pot_any, kin_any, orb_any, *refs):
-    a_refs, b_refs = refs[:blocks], refs[blocks : 2 * blocks]
-    pot_ref, kin_ref, orb_ref, arrivals = refs[2 * blocks :]
-    count, rows_x, rows_y, depth = orb_ref.shape
-    odd, core = odd_ref[0] == 1, core_ref[0] == 1
+def field_edges(odd, one, two, x, h):
+    rows_y = one.shape[-2]
     row, _ = iotas()
     upper = row < DEGREE
-    size = count // blocks
-    loads = [pltpu.make_async_copy(pot_any, pot_ref, arrivals.at[0]), pltpu.make_async_copy(kin_any, kin_ref, arrivals.at[1])]
-    for k in range(blocks):
-        part = pl.ds(k * size, size)
-        loads.append(pltpu.make_async_copy(orb_any.at[part], orb_ref.at[part], arrivals.at[2 + k]))
+    tail = slice(rows_y - SUB, rows_y)
+    first = jnp.where(upper, one[x, 0:SUB, cut(h)], pltpu.roll(two[x, 0:SUB, cut(h)], DEGREE, 0))
+    last = jnp.where(upper, pltpu.roll(one[x, tail, cut(h)], DEGREE, 0), two[x, tail, cut(h)])
+    return jnp.where(odd, first, last), jnp.where(odd, last, first)
+
+
+def pack_kernel(odd_ref, core_ref, pot_any, kin_any, orb_any, a_ref, b_ref, pot_ref, kin_ref, orb_ref, arrivals):
+    rows_x, _, depth = pot_ref.shape
+    members = orb_ref.shape[0]
+    odd, core = odd_ref[0] == 1, core_ref[0] == 1
+    loads = [
+        pltpu.make_async_copy(pot_any, pot_ref, arrivals.at[0]),
+        pltpu.make_async_copy(kin_any, kin_ref, arrivals.at[1]),
+        pltpu.make_async_copy(orb_any.at[pl.ds(0, members)], orb_ref, arrivals.at[2]),
+    ]
     for load in loads:
         load.start()
-
-    def edges(one, two, x, h):
-        tail = slice(rows_y - SUB, rows_y)
-        first = jnp.where(upper, one[x, 0:SUB, cut(h)], pltpu.roll(two[x, 0:SUB, cut(h)], DEGREE, 0))
-        last = jnp.where(upper, pltpu.roll(one[x, tail, cut(h)], DEGREE, 0), two[x, tail, cut(h)])
-        return jnp.where(odd, first, last), jnp.where(odd, last, first)
-
     places = [(x, h) for x in range(rows_x) for h in range(depth // LANES)]
     loads[0].wait()
     loads[1].wait()
     for x, h in places:
-        low_a, low_b = edges(pot_ref, kin_ref.at[0], x, h)
-        high_a, high_b = edges(kin_ref.at[1], kin_ref.at[2], x, h)
-        a_refs[0][0, x, :, cut(h)] = low_a
-        a_refs[0][1, x, :, cut(h)] = high_a
-        b_refs[0][0, x, :, cut(h)] = jnp.where(core, high_b, low_b)
-    for k in range(blocks):
-        loads[2 + k].wait()
-        for p in range(size // 2):
-            m = k * size + 2 * p
-            for x, h in places:
-                a, b = edges(orb_ref.at[m], orb_ref.at[m + 1], x, h)
-                a_refs[k][(0 if k else 2) + p, x, :, cut(h)] = a
-                b_refs[k][(0 if k else 1) + p, x, :, cut(h)] = b
+        low_a, low_b = field_edges(odd, pot_ref, kin_ref.at[0], x, h)
+        high_a, high_b = field_edges(odd, kin_ref.at[1], kin_ref.at[2], x, h)
+        a_ref[0, x, :, cut(h)] = low_a
+        a_ref[1, x, :, cut(h)] = high_a
+        b_ref[0, x, :, cut(h)] = jnp.where(core, high_b, low_b)
+    loads[2].wait()
+    for p in range(members // 2):
+        for x, h in places:
+            a, b = field_edges(odd, orb_ref.at[2 * p], orb_ref.at[2 * p + 1], x, h)
+            a_ref[2 + p, x, :, cut(h)] = a
+            b_ref[1 + p, x, :, cut(h)] = b
+
+
+def rest_kernel(k, odd_ref, orb_any, a_ref, b_ref, orb_ref, arrivals):
+    members, rows_x, _, depth = orb_ref.shape
+    odd = odd_ref[0] == 1
+    load = pltpu.make_async_copy(orb_any.at[pl.ds(k * members, members)], orb_ref, arrivals.at[0])
+    load.start()
+    load.wait()
+    for p in range(members // 2):
+        for x in range(rows_x):
+            for h in range(depth // LANES):
+                a, b = field_edges(odd, orb_ref.at[2 * p], orb_ref.at[2 * p + 1], x, h)
+                a_ref[p, x, :, cut(h)] = a
+                b_ref[p, x, :, cut(h)] = b
 
 
 def ring_tiles(ref, index, parts):
@@ -148,7 +160,7 @@
     return [(a, b) for a in range(members) for b in range(a, members)]
 
 
-def interior_kernel(k, pot_ref, kin_ref, orb_ref, body_ref, seam_ref, sums_ref, coef_ref, coef_ring, ring):
+def interior_kernel(pot_ref, kin_ref, orb_ref, body_ref, seam_ref, sums_ref, coef_ref, coef_ring, ring):
     members, rows_x, blocks_z = body_ref.shape[:3]
     rows_y = orb_ref.shape[2]
     parts = rows_y // SUB
@@ -159,7 +171,7 @@
         pair, half = m // 2, m % 2
         for x in range(rows_x):
             for h in range(blocks_z):
-                ring[half, x, h] = orb_ref[k * members + m, x, :, cut(h)]
+                ring[half, x, h] = orb_ref[m, x, :, cut(h)]
         v = [ring_tiles(ring.at[half], (x,), parts) for x in range(rows_x)]
         previous = None
         for step in range(DEGREE):
@@ -410,21 +422,42 @@
     pairs_a = [(i, i ^ 1) for i in range(domains)]
     pairs_b = [(i, (i + 1) % domains if i % 2 else (i - 1) % domains) for i in range(domains)]
     half = members // 2
-    *halos, pot, kin, fields = call(
-        functools.partial(pack_kernel, blocks),
+    whole = pltpu.with_memory_space_constraint(orbitals.reshape(count, rows_x, rows_y, depth), pltpu.HBM)
+    block_shape = (members, rows_x, rows_y, depth)
+    packed_a, packed_b, pot, kin, field = call(
+        pack_kernel,
         (
             odd,
             core,
             pltpu.with_memory_space_constraint(potential[0], pltpu.HBM),
             pltpu.with_memory_space_constraint(kinetic[:, 0], pltpu.HBM),
-            pltpu.with_memory_space_constraint(orbitals.reshape(count, rows_x, rows_y, depth), pltpu.HBM),
+            whole,
         ),
-        [(size, rows_x, SUB, depth) for size in [2 + half] + [half] * (blocks - 1) + [1 + half] + [half] * (blocks - 1)]
-        + [(rows_x, rows_y, depth), (3, rows_x, rows_y, depth), (count, rows_x, rows_y, depth)],
-        [pltpu.SemaphoreType.DMA((2 + blocks,))],
+        [
+            (2 + half, rows_x, SUB, depth),
+            (1 + half, rows_x, SUB, depth),
+            (rows_x, rows_y, depth),
+            (3, rows_x, rows_y, depth),
+            block_shape,
+        ],
+        [pltpu.SemaphoreType.DMA((3,))],
         specs=[smem()] * 2 + [anywhere()] * 3,
         place=pltpu.VMEM,
     )
+    packs_a, packs_b, fields = [packed_a], [packed_b], [field]
+    for k in range(1, blocks):
+        packed_a, packed_b, field = call(
+            functools.partial(rest_kernel, k),
+            (odd, whole),
+            [(half, rows_x, SUB, depth)] * 2 + [block_shape],
+            [pltpu.SemaphoreType.DMA((1,))],
+            specs=[smem(), anywhere()],
+            place=pltpu.VMEM,
+        )
+        packs_a.append(packed_a)
+        packs_b.append(packed_b)
+        fields.append(field)
+    halos = packs_a + packs_b
     halos_a = []
     for k in range(blocks):
         halos_a.append(lax.ppermute(halos[k], "grid", pairs_a))
@@ -435,8 +468,8 @@
 
     inner = [
         call(
-            functools.partial(interior_kernel, k),
-            (pot, kin, fields),
+            interior_kernel,
+            (pot, kin, fields[k]),
             [
                 (members, rows_x, blocks_z) + tile,
                 (2, half, DEGREE, 2, rows_x, blocks_z) + tile,
@@ -489,7 +522,7 @@
         gram = gram + swapped(gram, "grid", bit)
         bit *= 2
 
-    (filtered,) = call(assemble_kernel, rows, [fields.shape])
+    (filtered,) = call(assemble_kernel, rows, [(count, rows_x, rows_y, depth)])
     (partial_value,) = call(density_kernel, (gram, occupations, *rows), [pot.shape])
 
     share = rows_y // bands

time: 38.5 us -> 38.2 us (level)
  waiting for transfers between devices: 12.5 us -> 10.4 us
  Pallas kernels: 9.14 us -> 10.1 us
  starting transfers between devices: 15.2 us -> 16 us
    ppermute x2, waiting for transfers between devices: 3.97 us -> 2.58 us  [fast_body(): halos_b.append(lax.ppermute(halos[blocks + k], 'grid', pairs_b))]
    pallas_call x11 -> x12, Pallas kernels: 9.14 us -> 10.1 us  [call(): pl.pallas_call(kernel, out_shape=shapes, in_specs=[vmem() for _ in operan...]
    ppermute x6, waiting for transfers between devices: 8.52 us -> 7.81 us  [swapped(): return lax.ppermute(value, axis, [(i, i ^ bit) for i in range(count)])]
    ppermute x6, starting transfers between devices: 7.39 us -> 8.1 us  [swapped(): return lax.ppermute(value, axis, [(i, i ^ bit) for i in range(count)])]
  transfers between devices with their start and end apart: 10 -> 10, of which waited for: 6 -> 6; matrix products, arithmetic and copies ran while one was open for 0% -> 0% of each run, Pallas kernels for 18% -> 21%
where the time goes in v5:
time: 38.2 us; the launch traced here: 38.1 us
  starting transfers between devices  16 us (42%)
  waiting for transfers between devices  10.4 us (27%)
  Pallas kernels  10.1 us (26%)
  between operations  0.82 us (2%)
  other arithmetic  0.66 us (2%)
    pallas_call x12, Pallas kernels, call(): pl.pallas_call(kernel, out_shape=shapes, in_specs=[vmem() for _ in operan...  10.1 us
    ppermute x6, starting transfers between devices, swapped(): return lax.ppermute(value, axis, [(i, i ^ bit) for i in range(count)])  8.1 us
    ppermute x6, waiting for transfers between devices, swapped(): return lax.ppermute(value, axis, [(i, i ^ bit) for i in range(count)])  7.81 us
    ppermute x2, starting transfers between devices, fast_body(): halos_b.append(lax.ppermute(halos[blocks + k], 'grid', pairs_b))  4.79 us
    ppermute x2, starting transfers between devices, fast_body(): halos_a.append(lax.ppermute(halos[k], 'grid', pairs_a))  3.06 us
    ppermute x2, waiting for transfers between devices, fast_body(): halos_b.append(lax.ppermute(halos[blocks + k], 'grid', pairs_b))  2.58 us
  transfers between devices with their start and end apart: 10, of which 6 were waited for; matrix products, arithmetic and copies ran while one was open for 0% of the time, Pallas kernels for 21%

profile of v5, /device:TPU:0, one launch (start us, length us, event | category | flops | bytes accessed | tf_op | source)
XLA Modules:
  0.0 38.1 jit_solution(17395365682341335897)
XLA Ops:
  0.6 1.2 %shard_map.67 = (f32[6,4,8,256]{3,2,1,0:T(8,128)S(1)}, f32[5,4,8,256]{3,2,1,0:T(8,128)S(1)}, f32[4,16,256]{2,1,0:T(8,128)S(1)}, f32[3,4,16,256]{3,2,1,0:T(8,128)S(1)}, f32[8,4,16,256]{3,2,1,0:T(8,128)S(1)}) custom-call(s32[1]{0:T(128)} %bitcast.odd_ref, s32[1]{0:T(128)} %bitcast.1.core_ref, f32[4,16,256]{2,1,0:T(8,128)} %bitcast.27, ...), custom_call_target="tpu_custom_call" | custom-call | tf_op jit(solution)/shard_map/pallas_call | solution.py:399
  1.9 3.1 %collective-permute-start = (f32[6,4,8,256]{3,2,1,0:T(8,128)S(1)}, f32[6,4,8,256]{3,2,1,0:T(8,128)S(1)}, u32[]{:S(2)}, u32[]{:S(2)}) collective-permute-start(f32[6,4,8,256]{3,2,1,0:T(8,128)S(1)} %get-tuple-element.25), channel_id=1, source_target_pairs={{0,1},{1,0},{2,3},{3,2},{4,5},{5,4},{6,7},{7,6},{8,9},{9,8},{10,11... | collective-permute-start | bytes 589832 | tf_op jit(solution)/shard_map/ppermute | solution.py:463
  4.9 3.5 %collective-permute-start.1 = (f32[5,4,8,256]{3,2,1,0:T(8,128)S(1)}, f32[5,4,8,256]{3,2,1,0:T(8,128)S(1)}, u32[]{:S(2)}, u32[]{:S(2)}) collective-permute-start(f32[5,4,8,256]{3,2,1,0:T(8,128)S(1)} %get-tuple-element.28), channel_id=1, source_target_pairs={{0,7},{1,2},{2,1},{3,4},{4,3},{5,6},{6,5},{7,0},{8,15},{9,10},{10,... | collective-permute-start | bytes 491528 | tf_op jit(solution)/shard_map/ppermute | solution.py:466
  8.5 1.1 %shard_map.73 = (f32[4,4,8,256]{3,2,1,0:T(8,128)S(1)}, f32[4,4,8,256]{3,2,1,0:T(8,128)S(1)}, f32[8,4,16,256]{3,2,1,0:T(8,128)S(1)}) custom-call(s32[1]{0:T(128)} %bitcast.odd_ref, f32[16,4,16,256]{3,2,1,0:T(8,128)} %bitcast.24), custom_call_target="tpu_custom_call" | custom-call | tf_op jit(solution)/shard_map/pallas_call | solution.py:399
  9.6 1.2 %collective-permute-start.4 = (f32[4,4,8,256]{3,2,1,0:T(8,128)S(1)}, f32[4,4,8,256]{3,2,1,0:T(8,128)S(1)}, u32[]{:S(2)}, u32[]{:S(2)}) collective-permute-start(f32[4,4,8,256]{3,2,1,0:T(8,128)S(1)} %get-tuple-element.35), channel_id=1, source_target_pairs={{0,7},{1,2},{2,1},{3,4},{4,3},{5,6},{6,5},{7,0},{8,15},{9,10},{10,... | collective-permute-start | bytes 393224 | tf_op jit(solution)/shard_map/ppermute | solution.py:466
  10.8 0.0 collective-permute-start.3
  10.8 2.6 %collective-permute-done.1.refs_0_.halo_ref = f32[5,4,8,256]{3,2,1,0:T(8,128)S(1)} collective-permute-done((f32[5,4,8,256]{3,2,1,0:T(8,128)S(1)}, f32[5,4,8,256]{3,2,1,0:T(8,128)S(1)}, u32[]{:S(2)}, u32[]{:S(2)}) %collective-permute-start.1) | collective-permute-done | bytes 163872 | tf_op jit(solution)/shard_map/ppermute | solution.py:466
  13.4 0.0 collective-permute-start.2
  13.4 1.9 %shard_map.68 = (f32[8,4,2,8,128]{4,3,2,1,0:T(8,128)S(1)}, f32[2,4,4,2,4,2,8,128]{7,6,5,4,3,2,1,0:T(8,128)S(1)}, f32[36,8,128]{2,1,0:T(8,128)S(1)}) custom-call(f32[4,16,256]{2,1,0:T(8,128)S(1)} %get-tuple-element.21.pot_ref, f32[3,4,16,256]{3,2,1,0:T(8,128)S(1)} %get-tuple-element.22.kin_ref, f32[8,4,16,256]{3,2,1,0:T(8,128)S(1)} %get-tuple-element.23.orb_ref), custom_call_target="tpu_custom_call" | custom-call | tf_op jit(solution)/shard_map/pallas_call | solution.py:399
  15.3 1.9 %shard_map.74 = (f32[8,4,2,8,128]{4,3,2,1,0:T(8,128)S(1)}, f32[2,4,4,2,4,2,8,128]{7,6,5,4,3,2,1,0:T(8,128)S(1)}, f32[36,8,128]{2,1,0:T(8,128)S(1)}) custom-call(f32[4,16,256]{2,1,0:T(8,128)S(1)} %get-tuple-element.21.pot_ref, f32[3,4,16,256]{3,2,1,0:T(8,128)S(1)} %get-tuple-element.22.kin_ref, f32[8,4,16,256]{3,2,1,0:T(8,128)S(1)} %get-tuple-element.30.orb_ref), custom_call_target="tpu_custom_call" | custom-call | tf_op jit(solution)/shard_map/pallas_call | solution.py:399
  17.3 0.0 collective-permute-done.refs_0_.halo_ref
  17.3 0.2 shard_map.69.coef_ref
  17.5 0.0 collective-permute-done.2.refs_1_
  17.5 0.2 shard_map.70.coef_ref
  17.7 0.6 %shard_map.71.second_ref = f32[4,4,2,8,128]{4,3,2,1,0:T(8,128)S(1)} custom-call(s32[1]{0:T(128)} %bitcast.odd_ref, f32[5,4,8,256]{3,2,1,0:T(8,128)S(1)} %collective-permute-done.1.refs_0_.halo_ref, f32[4,6,4,2,8,128]{5,4,3,2,1,0:T(8,128)S(1)} %shard_map.70.coef_ref, f32[2,4,4,2,4,2,8,128]{7,6,5,4,3,2,1,0:T(8,128)S(1)} %get-tuple-element.26.seam_ref), custom_call_target="tpu_custom_call" | custom-call | tf_op jit(solution)/shard_map/pallas_call | solution.py:399
  18.2 0.0 collective-permute-done.4.halo_ref
  18.3 0.6 %shard_map.75.second_ref = f32[4,4,2,8,128]{4,3,2,1,0:T(8,128)S(1)} custom-call(s32[1]{0:T(128)} %bitcast.odd_ref, f32[4,4,8,256]{3,2,1,0:T(8,128)S(1)} %collective-permute-done.4.halo_ref, f32[4,6,4,2,8,128]{5,4,3,2,1,0:T(8,128)S(1)} %shard_map.70.coef_ref, f32[2,4,4,2,4,2,8,128]{7,6,5,4,3,2,1,0:T(8,128)S(1)} %get-tuple-element.33.seam_ref), custom_call_target="tpu_custom_call" | custom-call | tf_op jit(solution)/shard_map/pallas_call | solution.py:399
  18.8 0.6 %shard_map.72 = (f32[8,4,2,8,128]{4,3,2,1,0:T(8,128)S(1)}, f32[8,8]{1,0:T(8,128)S(1)}) custom-call(s32[1]{0:T(128)} %bitcast.odd_ref, f32[6,4,8,256]{3,2,1,0:T(8,128)S(1)} %collective-permute-done.refs_0_.halo_ref, f32[4,6,4,2,8,128]{5,4,3,2,1,0:T(8,128)S(1)} %shard_map.69.coef_ref, f32[2,4,4,2,4,2,8,128]{7,6,5,4,3,2,1,0:T(8,128)S(1)} %get-tuple-element.26.seam_ref, ...), custom_call_target="tpu_custom_call" | custom-call | tf_op jit(solution)/shard_map/pallas_call | solution.py:399
  19.5 0.0 copy-start.1
  19.5 0.0 collective-permute-done.3.halo_ref
  19.5 0.6 %shard_map.76 = (f32[8,4,2,8,128]{4,3,2,1,0:T(8,128)S(1)}, f32[8,8]{1,0:T(8,128)S(1)}) custom-call(s32[1]{0:T(128)} %bitcast.odd_ref, f32[4,4,8,256]{3,2,1,0:T(8,128)S(1)} %collective-permute-done.3.halo_ref, f32[4,6,4,2,8,128]{5,4,3,2,1,0:T(8,128)S(1)} %shard_map.69.coef_ref, f32[2,4,4,2,4,2,8,128]{7,6,5,4,3,2,1,0:T(8,128)S(1)} %get-tuple-element.33.seam_ref, ...), custom_call_target="tpu_custom_call" | custom-call | tf_op jit(solution)/shard_map/pallas_call | solution.py:399
  20.2 1.8 %collective-permute-start.5 = (f32[2,8,8]{2,1,0:T(8,128)S(1)}, f32[2,8,8]{2,1,0:T(8,128)S(1)}, u32[]{:S(2)}, u32[]{:S(2)}) collective-permute-start(f32[2,8,8]{2,1,0:T(8,128)S(1)} %maximum_multiply_fusion), channel_id=1, source_target_pairs={{0,1},{1,0},{2,3},{3,2},{4,5},{5,4},{6,7},{7,6},{8,9},{9,8},{10,11... | collective-permute-start | bytes 1544 | tf_op jit(solution)/shard_map/ppermute | solution.py:28
  22.0 1.9 %collective-permute-done.5 = f32[2,8,8]{2,1,0:T(8,128)S(1)} collective-permute-done((f32[2,8,8]{2,1,0:T(8,128)S(1)}, f32[2,8,8]{2,1,0:T(8,128)S(1)}, u32[]{:S(2)}, u32[]{:S(2)}) %collective-permute-start.5) | collective-permute-done | bytes 544 | tf_op jit(solution)/shard_map/ppermute | solution.py:28
  23.9 1.8 %collective-permute-start.6 = (f32[2,8,8]{2,1,0:T(8,128)S(1)}, f32[2,8,8]{2,1,0:T(8,128)S(1)}, u32[]{:S(2)}, u32[]{:S(2)}) collective-permute-start(f32[2,8,8]{2,1,0:T(8,128)S(1)} %fusion), channel_id=1, source_target_pairs={{0,2},{1,3},{2,0},{3,1},{4,6},{5,7},{6,4},{7,5},{8,10},{9,11},{10,... | collective-permute-start | bytes 1544 | tf_op jit(solution)/shard_map/ppermute | solution.py:28
  25.7 1.8 %collective-permute-done.6 = f32[2,8,8]{2,1,0:T(8,128)S(1)} collective-permute-done((f32[2,8,8]{2,1,0:T(8,128)S(1)}, f32[2,8,8]{2,1,0:T(8,128)S(1)}, u32[]{:S(2)}, u32[]{:S(2)}) %collective-permute-start.6) | collective-permute-done | bytes 544 | tf_op jit(solution)/shard_map/ppermute | solution.py:28
  27.5 2.8 %collective-permute-start.7 = (f32[2,8,8]{2,1,0:T(8,128)S(1)}, f32[2,8,8]{2,1,0:T(8,128)S(1)}, u32[]{:S(2)}, u32[]{:S(2)}) collective-permute-start(f32[2,8,8]{2,1,0:T(8,128)S(1)} %fusion.1), channel_id=1, source_target_pairs={{0,4},{1,5},{2,6},{3,7},{4,0},{5,1},{6,2},{7,3},{8,12},{9,13},{10,... | collective-permute-start | bytes 1544 | tf_op jit(solution)/shard_map/ppermute | solution.py:28
  30.4 1.7 %collective-permute-done.7 = f32[2,8,8]{2,1,0:T(8,128)S(1)} collective-permute-done((f32[2,8,8]{2,1,0:T(8,128)S(1)}, f32[2,8,8]{2,1,0:T(8,128)S(1)}, u32[]{:S(2)}, u32[]{:S(2)}) %collective-permute-start.7) | collective-permute-done | bytes 544 | tf_op jit(solution)/shard_map/ppermute | solution.py:28
  32.1 0.0 copy-start
  32.1 0.0 copy-done.1
  32.1 0.2 shard_map.78
  32.3 0.1 collective-permute-start.8
  32.5 1.2 %collective-permute-done.8 = f32[4,2,4,256]{3,2,0,1:T(4,128)S(1)} collective-permute-done((f32[4,2,4,256]{3,2,0,1:T(4,128)S(1)}, f32[4,2,4,256]{3,2,0,1:T(4,128)S(1)}, u32[]{:S(2)}, u32[]{:S(2)}) %collective-permute-start.8) | collective-permute-done | bytes 32800 | tf_op jit(solution)/shard_map/ppermute | solution.py:28
  33.6 1.6 %collective-permute-start.9 = (f32[4,1,4,256]{3,2,0,1:T(4,128)S(1)}, f32[4,1,4,256]{3,2,0,1:T(4,128)S(1)}, u32[]{:S(2)}, u32[]{:S(2)}) collective-permute-start(f32[4,1,4,256]{3,2,0,1:T(4,128)S(1)} %constant_dynamic-slice_fusion), channel_id=1, source_target_pairs={{0,16},{8,24},{16,0},{24,8},{1,17},{9,25},{17,1},{25,9},{2,18},{10... | collective-permute-start | bytes 49160 | tf_op jit(solution)/shard_map/ppermute | solution.py:28
  35.2 1.0 %shard_map.77 = f32[16,4,16,256]{3,2,1,0:T(8,128)} custom-call(f32[8,4,2,8,128]{4,3,2,1,0:T(8,128)S(1)} %get-tuple-element.24.refs_0_, f32[8,4,2,8,128]{4,3,2,1,0:T(8,128)S(1)} %get-tuple-element.29.refs_1_, f32[8,4,2,8,128]{4,3,2,1,0:T(8,128)S(1)} %get-tuple-element.31.refs_2_, f32[8,4,2,8,128]{4,3,2,1,0:T(8,128)S(1)} %get-tuple-element.36.refs_3_), custom_call_target="tpu_custom_call" | custom-call | tf_op jit(solution)/shard_map/pallas_call | solution.py:399
  36.2 1.2 %collective-permute-done.9 = f32[4,1,4,256]{3,2,0,1:T(4,128)S(1)} collective-permute-done((f32[4,1,4,256]{3,2,0,1:T(4,128)S(1)}, f32[4,1,4,256]{3,2,0,1:T(4,128)S(1)}, u32[]{:S(2)}, u32[]{:S(2)}) %collective-permute-start.9) | collective-permute-done | bytes 16416 | tf_op jit(solution)/shard_map/ppermute | solution.py:28
  37.4 0.6 %add_bitcast_fusion = f32[1,4,4,256]{3,2,1,0:T(4,128)} fusion(f32[4,1,4,256]{3,2,0,1:T(4,128)S(1)} %collective-permute-done.9, f32[4,2,4,256]{3,2,0,1:T(4,128)S(1)} %bitcast_add_fusion, s32[]{:T(128)S(6)} %select_n.35), kind=kLoop, calls=%fused_computation.2 | loop fusion | flops 4096 | bytes 49156 | tf_op jit(solution)/shard_map/reshape | solution.py:540
  38.1 0.0 copy-done
  (10 shorter events, 0.1 us)
Async XLA Ops:
  1.9 15.4 %collective-permute-start = (f32[6,4,8,256]{3,2,1,0:T(8,128)S(1)}, f32[6,4,8,256]{3,2,1,0:T(8,128)S(1)}, u32[]{:S(2)}, u32[]{:S(2)}) collective-permute-start(f32[6,4,8,256]{3,2,1,0:T(8,128)S(1)} %get-tuple-element.25), channel_id=1, source_target_pairs={{0,1},{1,0},{2,3},{3,2},{4,5},{5,4},{6,7},{7,6},{8,9},{9,8},{10,11... | collective-permute-start | bytes 589832 | tf_op jit(solution)/shard_map/ppermute | solution.py:463
  4.9 8.5 %collective-permute-start.1 = (f32[5,4,8,256]{3,2,1,0:T(8,128)S(1)}, f32[5,4,8,256]{3,2,1,0:T(8,128)S(1)}, u32[]{:S(2)}, u32[]{:S(2)}) collective-permute-start(f32[5,4,8,256]{3,2,1,0:T(8,128)S(1)} %get-tuple-element.28), channel_id=1, source_target_pairs={{0,7},{1,2},{2,1},{3,4},{4,3},{5,6},{6,5},{7,0},{8,15},{9,10},{10,... | collective-permute-start | bytes 491528 | tf_op jit(solution)/shard_map/ppermute | solution.py:466
  9.6 8.7 %collective-permute-start.4 = (f32[4,4,8,256]{3,2,1,0:T(8,128)S(1)}, f32[4,4,8,256]{3,2,1,0:T(8,128)S(1)}, u32[]{:S(2)}, u32[]{:S(2)}) collective-permute-start(f32[4,4,8,256]{3,2,1,0:T(8,128)S(1)} %get-tuple-element.35), channel_id=1, source_target_pairs={{0,7},{1,2},{2,1},{3,4},{4,3},{5,6},{6,5},{7,0},{8,15},{9,10},{10,... | collective-permute-start | bytes 393224 | tf_op jit(solution)/shard_map/ppermute | solution.py:466
  10.8 8.7 %collective-permute-start.3 = (f32[4,4,8,256]{3,2,1,0:T(8,128)S(1)}, f32[4,4,8,256]{3,2,1,0:T(8,128)S(1)}, u32[]{:S(2)}, u32[]{:S(2)}) collective-permute-start(f32[4,4,8,256]{3,2,1,0:T(8,128)S(1)} %get-tuple-element.32), channel_id=1, source_target_pairs={{0,1},{1,0},{2,3},{3,2},{4,5},{5,4},{6,7},{7,6},{8,9},{9,8},{10,11... | collective-permute-start | bytes 393224 | tf_op jit(solution)/shard_map/ppermute | solution.py:463
  13.4 4.1 %collective-permute-start.2 = (f32[1,4,8,256]{3,2,1,0:T(8,128)S(1)}, f32[1,4,8,256]{3,2,1,0:T(8,128)S(1)}, u32[]{:S(2)}, u32[]{:S(2)}) collective-permute-start(f32[1,4,8,256]{3,2,1,0:T(8,128)S(1)} %slice.4), channel_id=1, source_target_pairs={{0,8},{8,0},{16,24},{24,16},{1,9},{9,1},{17,25},{25,17},{2,10},{10... | collective-permute-start | bytes 98312 | tf_op jit(solution)/shard_map/ppermute | solution.py:28
  19.5 12.6 %copy-start.1 = (f32[2,8]{1,0:T(2,128)S(1)}, f32[2,8]{1,0:T(2,128)}, u32[]{:S(2)}) copy-start(f32[2,8]{1,0:T(2,128)} %occ_ref.1) | copy-start | bytes 196
  20.2 3.7 %collective-permute-start.5 = (f32[2,8,8]{2,1,0:T(8,128)S(1)}, f32[2,8,8]{2,1,0:T(8,128)S(1)}, u32[]{:S(2)}, u32[]{:S(2)}) collective-permute-start(f32[2,8,8]{2,1,0:T(8,128)S(1)} %maximum_multiply_fusion), channel_id=1, source_target_pairs={{0,1},{1,0},{2,3},{3,2},{4,5},{5,4},{6,7},{7,6},{8,9},{9,8},{10,11... | collective-permute-start | bytes 1544 | tf_op jit(solution)/shard_map/ppermute | solution.py:28
  23.9 3.7 %collective-permute-start.6 = (f32[2,8,8]{2,1,0:T(8,128)S(1)}, f32[2,8,8]{2,1,0:T(8,128)S(1)}, u32[]{:S(2)}, u32[]{:S(2)}) collective-permute-start(f32[2,8,8]{2,1,0:T(8,128)S(1)} %fusion), channel_id=1, source_target_pairs={{0,2},{1,3},{2,0},{3,1},{4,6},{5,7},{6,4},{7,5},{8,10},{9,11},{10,... | collective-permute-start | bytes 1544 | tf_op jit(solution)/shard_map/ppermute | solution.py:28
  27.5 4.5 %collective-permute-start.7 = (f32[2,8,8]{2,1,0:T(8,128)S(1)}, f32[2,8,8]{2,1,0:T(8,128)S(1)}, u32[]{:S(2)}, u32[]{:S(2)}) collective-permute-start(f32[2,8,8]{2,1,0:T(8,128)S(1)} %fusion.1), channel_id=1, source_target_pairs={{0,4},{1,5},{2,6},{3,7},{4,0},{5,1},{6,2},{7,3},{8,12},{9,13},{10,... | collective-permute-start | bytes 1544 | tf_op jit(solution)/shard_map/ppermute | solution.py:28
  32.1 6.0 %copy-start = (f32[2,8,8]{2,1,0:T(8,128)}, f32[2,8,8]{2,1,0:T(8,128)S(1)}, u32[]{:S(2)}) copy-start(f32[2,8,8]{2,1,0:T(8,128)S(1)} %add.42.gram_ref) | copy-start | bytes 1540
  32.3 1.3 %collective-permute-start.8 = (f32[4,2,4,256]{3,2,0,1:T(4,128)S(1)}, f32[4,2,4,256]{3,2,0,1:T(4,128)S(1)}, u32[]{:S(2)}, u32[]{:S(2)}) collective-permute-start(f32[4,2,4,256]{3,2,0,1:T(4,128)S(1)} %bitcast.28), channel_id=1, source_target_pairs={{0,8},{8,0},{16,24},{24,16},{1,9},{9,1},{17,25},{25,17},{2,10},{10... | collective-permute-start | bytes 98312 | tf_op jit(solution)/shard_map/ppermute | solution.py:28
  33.6 3.8 %collective-permute-start.9 = (f32[4,1,4,256]{3,2,0,1:T(4,128)S(1)}, f32[4,1,4,256]{3,2,0,1:T(4,128)S(1)}, u32[]{:S(2)}, u32[]{:S(2)}) collective-permute-start(f32[4,1,4,256]{3,2,0,1:T(4,128)S(1)} %constant_dynamic-slice_fusion), channel_id=1, source_target_pairs={{0,16},{8,24},{16,0},{24,8},{1,17},{9,25},{17,1},{25,9},{2,18},{10... | collective-permute-start | bytes 49160 | tf_op jit(solution)/shard_map/ppermute | solution.py:28
